TPU v7x, 128 devices: a whole 4x4x4 slice. The times are simulated.
128 devices in a mesh: lon: 32 (over z, x, core), lat: 4 (over y).
Axes of the slice: x: 4, y: 4, z: 4, core: 2. Of those that a mesh axis runs over, the one named last changes fastest.
Arguments:
- fields: bfloat16 [222, 512, 512], P(None, 'lon', 'lat'), may hold values from -6 to 6
- conv_weight: bfloat16 [9, 128, 222], replicated, may hold values from -0.125 to 0.125
- regrid_blocks: bfloat16 [16384, 128, 128], P(('lon', 'lat')), may hold values from -0.125 to 0.125
- source_block: int32 [16384], P(('lon', 'lat')), may hold values from 0 to 15
- target_device: int32 [16384, 1], replicated, may hold values from 0 to 127; in each aligned block of 128 rows (0 to 127, 128 to 255, ...) at most 2 rows name the same one
- target_half: int32 [16384], replicated, may hold values from 0 to 7
- neighbours: int32 [512, 4, 3], P(('lon', 'lat')), may hold values from 0 to 511, as said below
- hp_weight: bfloat16 [2, 128, 128], replicated, may hold values from -0.3125 to 0.3125
- rate_scale: float32 [128], replicated, may hold values from 0.3 to 3
Outputs:
- latent_codes: bfloat16 [131072, 128], P(('lon', 'lat'))
- grad_fields: float32 [222, 512, 512], P(None, 'lon', 'lat')
Inputs may be any that keep to these rules, and one draw needn't show every extreme that they name: `target_device`: within the 128 blocks of one device no device is named more than 2 times, and some device is named exactly 2 times. `neighbours`: entries are (tile, side, reversed). Side 0 meets side 2 and side 1 meets side 3; the relation is symmetric with the same reversal bit on both sides of a pair. Across side 0 or 2 the neighbour lies on a device whose lon index is one above or one below around the cycle (side 0 above); across side 1 or 3 on a device with the same lon index.
All inputs are finite; a program needn't handle non-finite values.
Results may differ from a plain program's by a relative error of at most 0.008.
Values may be sent and summed in bfloat16 or wider, within the bound.
A program may use at most 128 MiB of HBM per device.

v0:
```python
import jax
import jax.numpy as jnp
from jax import lax
from jax.sharding import PartitionSpec as P

TS = 16
CAP = 2


LOG_TWO = 0.6931471805599453


def extended(cells, sides, width):
    for axis, dim in sides:
        count = lax.axis_size(axis)
        head = lax.slice_in_dim(cells, 0, width, axis=dim)
        tail = lax.slice_in_dim(cells, cells.shape[dim] - width, cells.shape[dim], axis=dim)
        cells = jnp.concatenate(
            [
                lax.ppermute(tail, axis, [(i, (i + 1) % count) for i in range(count)]),
                cells,
                lax.ppermute(head, axis, [((i + 1) % count, i) for i in range(count)]),
            ],
            axis=dim,
        )
    return cells


def joined_along(parts, dim):
    parts = jnp.moveaxis(parts, 0, dim)
    shape = parts.shape
    return parts.reshape(*shape[:dim], shape[dim] * shape[dim + 1], *shape[dim + 2 :])


def from_everyone(x, axis):
    peers = lax.axis_size(axis)
    return lax.all_to_all(jnp.broadcast_to(x[None], (peers, *x.shape)), axis, 0, 0, tiled=True)


def collect(x, axis, dim):
    return joined_along(from_everyone(x, axis), dim)


def passed_along(value, axis, steps):
    count = lax.axis_size(axis)
    pairs = [(source, (source + steps) % count) for source in range(count)]
    return lax.ppermute(value, axis, pairs)


def silu_slope(values):
    sigma = jax.nn.sigmoid(values)
    return sigma * (1.0 + values * (1.0 - sigma))


def laplace_slope(latent, spread):
    magnitude = jnp.abs(latent)
    edge_mass = jnp.exp(-0.5 / spread)
    near_mass = 1.0 - edge_mass * jnp.cosh(jnp.minimum(magnitude, 0.5) / spread)
    slope_near = (
        edge_mass * jnp.sinh(jnp.clip(latent, -0.5, 0.5) / spread) / (spread * near_mass * LOG_TWO)
    )
    slope_far = jnp.sign(latent) / (spread * LOG_TWO)
    return jnp.where(magnitude < 0.5, slope_near, slope_far)


def conv_taps(kernel, padded, reverse):
    lon_cells = padded.shape[1] - 2
    lat_cells = padded.shape[2] - 2
    out_rows = kernel.shape[2] if reverse else kernel.shape[1]
    result = jnp.zeros((out_rows, lon_cells * lat_cells), jnp.float32)
    for tap_index in range(9):
        lon_shift = tap_index // 3
        lat_shift = tap_index % 3
        if reverse:
            lon_shift = 2 - lon_shift
            lat_shift = 2 - lat_shift
        window = padded[
            :, lon_shift : lon_shift + lon_cells, lat_shift : lat_shift + lat_cells
        ].reshape(padded.shape[0], lon_cells * lat_cells)
        if reverse:
            result = result + lax.dot_general(
                kernel[tap_index],
                window,
                (((0,), (0,)), ((), ())),
                preferred_element_type=jnp.float32,
            )
        else:
            result = result + jnp.dot(kernel[tap_index], window, preferred_element_type=jnp.float32)
    return result


def tile_edges(tile_values):
    return jnp.stack(
        [tile_values[:, 0], tile_values[:, :, -1], tile_values[:, -1], tile_values[:, :, 0]], axis=1
    )


def neighbour_sum(tile_values, rim_values):
    tiles_float = tile_values.astype(jnp.float32)
    from_above = jnp.concatenate([rim_values[:, 0][:, None], tiles_float[:, :-1]], axis=1)
    from_below = jnp.concatenate([tiles_float[:, 1:], rim_values[:, 2][:, None]], axis=1)
    from_left = jnp.concatenate([rim_values[:, 3][:, :, None], tiles_float[:, :, :-1]], axis=2)
    from_right = jnp.concatenate([tiles_float[:, :, 1:], rim_values[:, 1][:, :, None]], axis=2)
    return from_above + from_below + from_left + from_right


def grid_rims(values):
    padded = extended(values, (("lon", 1), ("lat", 2)), 1)
    lat_pos = lax.axis_index("lat")
    lat_last = lax.axis_size("lat") - 1
    column = lax.broadcasted_iota(jnp.int32, (1, 1, padded.shape[2]), 2)
    outside = (column == 0) & (lat_pos == 0) | (column == padded.shape[2] - 1) & (
        lat_pos == lat_last
    )
    return jnp.where(outside, jnp.zeros_like(padded), padded)


def route(buffer):
    return lax.all_to_all(buffer, ("lon", "lat"), split_axis=0, concat_axis=0, tiled=True)


def pick_rims(edge_rows, tile_pos, side_pos, flip_bit):
    tile_count = edge_rows.shape[0]
    flat_edges = edge_rows.reshape(tile_count * 4, -1)
    flipped = edge_rows[:, :, ::-1, :].reshape(tile_count * 4, -1)
    target_column = (tile_pos * 4 + side_pos)[..., None]
    column_ids = jnp.arange(tile_count * 4, dtype=jnp.int32)
    straight = (
        ((target_column == column_ids) & (flip_bit[..., None] == 0))
        .astype(jnp.bfloat16)
        .reshape(-1, tile_count * 4)
    )
    reversed_pick = (
        ((target_column == column_ids) & (flip_bit[..., None] == 1))
        .astype(jnp.bfloat16)
        .reshape(-1, tile_count * 4)
    )
    picked = jnp.dot(straight, flat_edges, preferred_element_type=jnp.float32) + jnp.dot(
        reversed_pick, flipped, preferred_element_type=jnp.float32
    )
    return picked.reshape(tile_pos.shape + edge_rows.shape[2:])


def fetch_rims(edge_rows, neighbours):
    band_edges = collect(edge_rows, "lat", 0)
    column_tiles = band_edges.shape[0]
    beside_all = []
    for step_by in (1, -1):
        beside_all.append(passed_along(band_edges, "lon", step_by))
    joined = jnp.concatenate([beside_all[0], band_edges, beside_all[1]], axis=0)
    owner_col = neighbours[:, :, 0] // column_tiles
    relative = (owner_col - lax.axis_index("lon") + 1) % lax.axis_size("lon")
    position = relative * column_tiles + neighbours[:, :, 0] % column_tiles
    return pick_rims(joined, position, neighbours[:, :, 1], neighbours[:, :, 2])


def on_device(
    fields,
    conv_weight,
    regrid_blocks,
    source_block,
    target_device,
    target_half,
    neighbours,
    hp_weight,
    rate_scale,
):
    channels, lon_cells, lat_cells = fields.shape
    latent_width = conv_weight.shape[1]
    block_rows = regrid_blocks.shape[1]
    block_count = regrid_blocks.shape[0]
    device_count = lax.axis_size("lon") * lax.axis_size("lat")
    device_pos = lax.axis_index(("lon", "lat"))
    source_count = lon_cells * lat_cells // block_rows
    tile_count = neighbours.shape[0]
    half_count = tile_count * TS * TS // block_rows
    pre_conv = conv_taps(conv_weight, grid_rims(fields), False)
    hidden = jax.nn.silu(pre_conv).astype(jnp.bfloat16)
    sources = jnp.take(hidden.reshape(latent_width, source_count, block_rows), source_block, axis=1)
    contrib = jnp.einsum(
        "bij,cbj->bic", regrid_blocks, sources, preferred_element_type=jnp.float32
    ).astype(jnp.bfloat16)
    all_targets = target_device[:, 0].reshape(device_count, block_count)
    all_halves = target_half.reshape(device_count, block_count)
    device_ids = jnp.arange(device_count, dtype=jnp.int32)
    target_hits = all_targets[:, :, None] == device_ids
    arrival_rank = jnp.sum(
        jnp.where(target_hits, jnp.cumsum(target_hits.astype(jnp.int32), axis=1) - 1, 0), axis=2
    )
    own_targets = lax.dynamic_index_in_dim(all_targets, device_pos, 0, False)
    own_ranks = lax.dynamic_index_in_dim(arrival_rank, device_pos, 0, False)
    slot_of_block = own_targets * CAP + own_ranks
    slot_count = device_count * CAP
    slot_ids = jnp.arange(slot_count, dtype=jnp.int32)
    slot_match = slot_of_block[None, :] == slot_ids[:, None]
    block_of_slot = jnp.sum(
        jnp.where(slot_match, jnp.arange(block_count, dtype=jnp.int32)[None, :], 0), axis=1
    )
    slot_used = jnp.any(slot_match, axis=1)
    outgoing = jnp.where(
        slot_used[:, None, None],
        jnp.take(contrib, block_of_slot, axis=0),
        jnp.zeros((), jnp.bfloat16),
    )
    incoming = route(outgoing)
    to_me = all_targets == device_pos
    arrival = to_me[:, :, None] & (arrival_rank[:, :, None] == jnp.arange(CAP, dtype=jnp.int32))
    half_of_slot = jnp.sum(jnp.where(arrival, all_halves[:, :, None], 0), axis=1).reshape(
        slot_count
    )
    slot_live = jnp.any(arrival, axis=1).reshape(slot_count)
    placing = (
        (half_of_slot[None, :] == jnp.arange(half_count, dtype=jnp.int32)[:, None])
        & slot_live[None, :]
    ).astype(jnp.bfloat16)
    latent_in = jnp.einsum(
        "hs,sic->hic", placing, incoming, preferred_element_type=jnp.float32
    ).astype(jnp.bfloat16)
    tiles_in = latent_in.reshape(tile_count, TS, TS, latent_width)
    flat_latent = latent_in.reshape(-1, latent_width)
    rim_values = fetch_rims(tile_edges(tiles_in), neighbours)
    near_sum = neighbour_sum(tiles_in, rim_values).astype(jnp.bfloat16).reshape(-1, latent_width)
    pre_mix = jnp.dot(flat_latent, hp_weight[0], preferred_element_type=jnp.float32) + jnp.dot(
        near_sum, hp_weight[1], preferred_element_type=jnp.float32
    )
    mixed_latent = jax.nn.silu(pre_mix)
    bit_slope = laplace_slope(mixed_latent, rate_scale)
    mix_grad = (bit_slope * silu_slope(pre_mix)).astype(jnp.bfloat16)
    self_grad = lax.dot_general(
        mix_grad, hp_weight[0], (((1,), (1,)), ((), ())), preferred_element_type=jnp.float32
    )
    near_grad = lax.dot_general(
        mix_grad, hp_weight[1], (((1,), (1,)), ((), ())), preferred_element_type=jnp.float32
    )
    near_grad = near_grad.astype(jnp.bfloat16).reshape(tiles_in.shape)
    back_rims = fetch_rims(tile_edges(near_grad), neighbours)
    latent_grad = (
        self_grad + neighbour_sum(near_grad, back_rims).reshape(-1, latent_width)
    ).astype(jnp.bfloat16)
    halves_grad = latent_grad.reshape(half_count, block_rows, latent_width)
    replies = jnp.where(
        slot_live[:, None, None],
        jnp.take(halves_grad, half_of_slot, axis=0),
        jnp.zeros((), jnp.bfloat16),
    )
    answers = route(replies)
    contrib_grad = jnp.take(answers, slot_of_block, axis=0)
    source_grad = jnp.einsum(
        "bij,bic->bcj", regrid_blocks, contrib_grad, preferred_element_type=jnp.float32
    )
    source_onehot = (
        source_block[:, None] == jnp.arange(source_count, dtype=jnp.int32)[None, :]
    ).astype(jnp.float32)
    hidden_grad = jnp.einsum(
        "bs,bcj->csj", source_onehot, source_grad, precision=lax.Precision.HIGHEST
    ).reshape(latent_width, -1)
    pre_grad = (
        (hidden_grad * silu_slope(pre_conv))
        .astype(jnp.bfloat16)
        .reshape(latent_width, lon_cells, lat_cells)
    )
    grad_fields = conv_taps(conv_weight, grid_rims(pre_grad), True).reshape(
        channels, lon_cells, lat_cells
    )
    return (mixed_latent.astype(jnp.bfloat16), grad_fields)


def solution(mesh):
    placed = (
        P(None, "lon", "lat"),
        P(),
        P(("lon", "lat"), None, None),
        P(("lon", "lat")),
        P(),
        P(),
        P(("lon", "lat"), None, None),
        P(),
        P(),
    )
    return jax.shard_map(
        on_device,
        mesh=mesh,
        in_specs=placed,
        out_specs=(P(("lon", "lat"), None), P(None, "lon", "lat")),
        check_vma=False,
    )
```

profile of v0, /device:TPU:0, one launch (start us, length us, event | category | flops | bytes accessed | tf_op | source)
XLA Modules:
  0.0 412.0 jit_solution(12134573393255526552)
XLA Ops:
  0.6 2.1 copy.104
  2.9 5.9 %collective-permute-start.1 = (bf16[222,1,128]{0,1,2:T(2,128)(2,1)S(1)}, bf16[222,1,128]{0,1,2:T(2,128)(2,1)S(1)}, u32[]{:S(2)}, u32[]{:S(2)}) collective-permute-start(bf16[222,1,128]{0,1,2:T(2,128)(2,1)S(1)} %get-tuple-element.14), channel_id=1, source_target_pairs={{4,0},{8,4},{12,8},{16,12},{20,16},{24,20},{28,24},{32,28},{36,32}... | collective-permute-start | bytes 170504 | tf_op jit(solution)/shard_map/ppermute | solution.py:22
  10.1 0.9 copy.99
  11.0 6.6 %select_reduce_fusion = s32[128,128]{0,1:T(8,128)S(1)} fusion(s32[128,128]{0,1:T(8,128)S(1)} %copy.99), kind=kOutput, calls=%fused_computation.10 | output fusion | flops 278904832 | bytes 131072 | tf_op jit(solution)/shard_map/jit(cumsum)/reduce_window_sum | solution.py:188
  18.1 1.0 pad_maximum_fusion
  19.1 3.1 collective-permute-start.3
  22.8 0.9 collective-permute-done.3
  23.6 3.7 collective-permute-done.2
  28.1 2.4 fusion.135
  33.9 1.4 multiply_convert_fusion
  35.6 3.1 gather_fusion
  38.7 8.5 %convert_bitcast_fusion = bf16[128,128,128]{1,2,0:T(8,128)(2,1)} fusion(bf16[128,128,128]{2,1,0:T(8,128)(2,1)} %param.11, bf16[128,128,128]{2,1,0:T(8,128)(2,1)} %gather_fusion, pred[128]{0:T(512)(128)(4,1)S(1)} %compare_and_fusion.2), kind=kOutput, calls=%fused_computation.19 | convolution fusion | flops 541065216 | bytes 12583040 | tf_op jit(solution)/shard_map/bij,cbj->bic/dot_general | solution.py:180
  47.2 6.4 %copy.111 = bf16[128,128,128]{2,1,0:T(8,128)(2,1)} copy(bf16[128,128,128]{1,2,0:T(8,128)(2,1)} %convert_bitcast_fusion) | data formatting | bytes 8388608 | tf_op jit(solution)/shard_map/convert_element_type | solution.py:182
  53.7 10.6 %gather_fusion.1 = bf16[256,128,128]{2,1,0:T(8,128)(2,1)} fusion(bf16[128,128,128]{2,1,0:T(8,128)(2,1)} %copy.111, s32[1024]{0:T(1024)S(1)} %pad_clamp_fusion.2), kind=kCustom, calls=%fused_computation.1 | custom fusion | bytes 16778240 | tf_op jit(solution)/shard_map/jit(_take)/gather | solution.py:202
  64.3 7.7 %select_select_fusion.1 = bf16[256,128,128]{2,1,0:T(8,128)(2,1)} fusion(bf16[256,128,128]{2,1,0:T(8,128)(2,1)} %gather_fusion.1, pred[256]{0:T(512)(128)(4,1)S(1)} %compare_and_fusion.3, pred[256]{0:T(512)(128)(4,1)S(1)} %fusion.51), kind=kLoop, calls=%fused_computation.9 | loop fusion | flops 8388608 | bytes 16777728 | tf_op jit(solution)/shard_map/jit(_where)/select_n | solution.py:200
  72.0 16.4 %all-to-all-start = ((bf16[256,128,128]{2,1,0:T(8,128)(2,1)}), bf16[256,128,128]{2,1,0:T(8,128)(2,1)}, u32[]{:S(2)}, u32[]{:S(2)}) async-start(bf16[256,128,128]{2,1,0:T(8,128)(2,1)} %select_select_fusion.1), calls=%async_computation | async-start | bytes 16777216 | tf_op jit(solution)/shard_map/all_to_all | solution.py:119
  89.8 99.0 %all-to-all-done = bf16[256,128,128]{2,1,0:T(8,128)(2,1)} async-done(((bf16[256,128,128]{2,1,0:T(8,128)(2,1)}), bf16[256,128,128]{2,1,0:T(8,128)(2,1)}, u32[]{:S(2)}, u32[]{:S(2)}) %all-to-all-start) | async-done | bytes 8388640 | tf_op jit(solution)/shard_map/all_to_all | solution.py:119
  188.8 7.8 %fusion.23 = bf16[8,128,128]{2,0,1:T(8,128)(2,1)S(1)} fusion(bf16[256,128,128]{2,1,0:T(8,128)(2,1)} %all-to-all-done, s32[256]{0:T(256)S(1)} %eq.164, pred[256]{0:T(512)(128)(4,1)S(1)} %and.125), kind=kOutput, calls=%fused_computation.50 | convolution fusion | flops 67244032 | bytes 8652032 | tf_op jit(solution)/shard_map/hs,sic->hic/dot_general | solution.py:216
  197.6 3.4 all-to-all-start.1
  201.0 0.9 fusion.143
  201.8 5.8 %all-to-all-done.1 = bf16[4,4,4,16,128]{4,3,2,1,0:T(8,128)(2,1)S(1)} async-done(((bf16[4,4,4,16,128]{4,3,2,1,0:T(8,128)(2,1)}), bf16[4,4,4,16,128]{4,3,2,1,0:T(8,128)(2,1)S(1)}, u32[]{:S(2)}, u32[]{:S(2)}) %all-to-all-start.1) | async-done | bytes 262176 | tf_op jit(solution)/shard_map/all_to_all | solution.py:37
  207.6 3.3 collective-permute-start.5
  210.9 1.0 fusion.95
  212.0 2.7 collective-permute-done.5
  214.8 5.2 %collective-permute-done.4 = bf16[16,4,16,128]{3,2,1,0:T(8,128)(2,1)S(1)} collective-permute-done((bf16[16,4,16,128]{3,2,1,0:T(8,128)(2,1)S(1)}, bf16[16,4,16,128]{3,2,1,0:T(8,128)(2,1)S(1)}, u32[]{:S(2)}, u32[]{:S(2)}) %collective-permute-start.4) | collective-permute-done | bytes 262176 | tf_op jit(solution)/shard_map/ppermute | solution.py:47
  221.1 1.2 fusion.46
  222.4 1.9 multiply_convert_fusion.1
  225.4 3.4 all-to-all-start.2
  228.8 6.6 %all-to-all-done.2 = bf16[4,4,4,16,128]{4,3,2,1,0:T(8,128)(2,1)S(1)} async-done(((bf16[4,4,4,16,128]{4,3,2,1,0:T(8,128)(2,1)}), bf16[4,4,4,16,128]{4,3,2,1,0:T(8,128)(2,1)S(1)}, u32[]{:S(2)}, u32[]{:S(2)}) %all-to-all-start.2) | async-done | bytes 262176 | tf_op jit(solution)/shard_map/all_to_all | solution.py:37
  236.0 0.9 fusion.140
  236.9 2.4 collective-permute-done.7
  239.3 5.2 %collective-permute-done.6 = bf16[16,4,16,128]{3,2,1,0:T(8,128)(2,1)S(1)} collective-permute-done((bf16[16,4,16,128]{3,2,1,0:T(8,128)(2,1)S(1)}, bf16[16,4,16,128]{3,2,1,0:T(8,128)(2,1)S(1)}, u32[]{:S(2)}, u32[]{:S(2)}) %collective-permute-start.6) | collective-permute-done | bytes 262176 | tf_op jit(solution)/shard_map/ppermute | solution.py:47
  245.7 1.2 fusion.48
  247.1 8.4 %gather_fusion.2 = bf16[256,128,128]{2,1,0:T(8,128)(2,1)} fusion(bf16[8,128,128]{2,1,0:T(8,128)(2,1)S(1)} %bitcast.207, s32[1024]{0:T(1024)S(1)} %pad_clamp_fusion.1), kind=kCustom, calls=%fused_computation.2 | custom fusion | bytes 16778240 | tf_op jit(solution)/shard_map/jit(_take)/gather | solution.py:243
  255.5 7.7 %select_select_fusion = bf16[256,128,128]{2,1,0:T(8,128)(2,1)} fusion(bf16[256,128,128]{2,1,0:T(8,128)(2,1)} %gather_fusion.2, pred[256]{0:T(512)(128)(4,1)S(1)} %compare_and_fusion, pred[256]{0:T(512)(128)(4,1)S(1)} %and.125), kind=kLoop, calls=%fused_computation.8 | loop fusion | flops 8388608 | bytes 16777728 | tf_op jit(solution)/shard_map/jit(_where)/select_n | solution.py:241
  263.2 6.1 %all-to-all-start.3 = ((bf16[256,128,128]{2,1,0:T(8,128)(2,1)}), bf16[256,128,128]{2,1,0:T(8,128)(2,1)}, u32[]{:S(2)}, u32[]{:S(2)}) async-start(bf16[256,128,128]{2,1,0:T(8,128)(2,1)} %select_select_fusion), calls=%async_computation.3 | async-start | bytes 16777216 | tf_op jit(solution)/shard_map/all_to_all | solution.py:119
  269.4 100.6 %all-to-all-done.3 = bf16[256,128,128]{2,1,0:T(8,128)(2,1)} async-done(((bf16[256,128,128]{2,1,0:T(8,128)(2,1)}), bf16[256,128,128]{2,1,0:T(8,128)(2,1)}, u32[]{:S(2)}, u32[]{:S(2)}) %all-to-all-start.3) | async-done | bytes 8388640 | tf_op jit(solution)/shard_map/all_to_all | solution.py:119
  370.0 6.5 %gather_fusion.3 = bf16[128,128,128]{2,1,0:T(8,128)(2,1)} fusion(bf16[256,128,128]{2,1,0:T(8,128)(2,1)} %all-to-all-done.3, s32[1024]{0:T(1024)S(1)} %pad_clamp_fusion), kind=kCustom, calls=%fused_computation.3 | custom fusion | bytes 8389120 | tf_op jit(solution)/shard_map/jit(_take)/gather | solution.py:247
  376.5 5.2 %fusion.9 = f32[128,128,128]{2,1,0:T(8,128)S(1)} fusion(bf16[128,128,128]{2,1,0:T(8,128)(2,1)} %param.11, bf16[128,128,128]{2,1,0:T(8,128)(2,1)} %gather_fusion.3, pred[128]{0:T(512)(128)(4,1)S(1)} %compare_and_fusion.1), kind=kOutput, calls=%fused_computation.17 | convolution fusion | flops 538968064 | bytes 16777344 | tf_op jit(solution)/shard_map/bij,bic->bcj/dot_general | solution.py:248
  381.6 7.5 %fusion.19 = f32[128,16,128]{2,1,0:T(8,128)S(1)} fusion(f32[128,128,128]{2,1,0:T(8,128)S(1)} %fusion.9, s32[128]{0:T(128)S(1)} %copy-done.8), kind=kOutput, calls=%fused_computation.45 | convolution fusion | flops 402655232 | bytes 9437696 | tf_op jit(solution)/shard_map/bs,bcj->csj/dot_general | solution.py:254
  390.0 2.9 collective-permute-start.9
  393.0 1.6 collective-permute-done.9
  394.6 5.1 %collective-permute-done.8 = bf16[128,1,128]{0,2,1:T(8,128)(2,1)S(1)} collective-permute-done((bf16[128,1,128]{0,2,1:T(8,128)(2,1)S(1)}, bf16[128,1,128]{0,2,1:T(8,128)(2,1)S(1)}, u32[]{:S(2)}, u32[]{:S(2)}) %collective-permute-start.8) | collective-permute-done | bytes 32800 | tf_op jit(solution)/shard_map/ppermute | solution.py:20
  400.0 2.0 collective-permute-start.10
  402.0 1.6 collective-permute-done.11
  403.6 1.3 collective-permute-done.10
  405.2 0.9 fusion.137
  410.3 1.3 slice.328
  (119 shorter events, 18.8 us)
Async XLA Ops:
  2.9 15.2 %collective-permute-start.1 = (bf16[222,1,128]{0,1,2:T(2,128)(2,1)S(1)}, bf16[222,1,128]{0,1,2:T(2,128)(2,1)S(1)}, u32[]{:S(2)}, u32[]{:S(2)}) collective-permute-start(bf16[222,1,128]{0,1,2:T(2,128)(2,1)S(1)} %get-tuple-element.14), channel_id=1, source_target_pairs={{4,0},{8,4},{12,8},{16,12},{20,16},{24,20},{28,24},{32,28},{36,32}... | collective-permute-start | bytes 170504 | tf_op jit(solution)/shard_map/ppermute | solution.py:22
  8.8 9.3 %collective-permute-start = (bf16[222,1,128]{0,1,2:T(2,128)(2,1)S(1)}, bf16[222,1,128]{0,1,2:T(2,128)(2,1)S(1)}, u32[]{:S(2)}, u32[]{:S(2)}) collective-permute-start(bf16[222,1,128]{0,1,2:T(2,128)(2,1)S(1)} %get-tuple-element.13), channel_id=1, source_target_pairs={{0,4},{4,8},{8,12},{12,16},{16,20},{20,24},{24,28},{28,32},{32,36}... | collective-permute-start | bytes 170504 | tf_op jit(solution)/shard_map/ppermute | solution.py:20
  19.1 4.5 %collective-permute-start.3 = (bf16[222,18,1]{0,1,2:T(8,128)(2,1)S(1)}, bf16[222,18,1]{0,1,2:T(8,128)(2,1)S(1)}, u32[]{:S(2)}, u32[]{:S(2)}) collective-permute-start(bf16[222,18,1]{0,1,2:T(8,128)(2,1)S(1)} %get-tuple-element.3), channel_id=1, source_target_pairs={{1,0},{2,1},{3,2},{0,3},{5,4},{6,5},{7,6},{4,7},{9,8},{10,9},{11,1... | collective-permute-start | bytes 23984 | tf_op jit(solution)/shard_map/ppermute | solution.py:22
  22.2 5.1 %collective-permute-start.2 = (bf16[222,18,1]{0,1,2:T(8,128)(2,1)S(1)}, bf16[222,18,1]{0,1,2:T(8,128)(2,1)S(1)}, u32[]{:S(2)}, u32[]{:S(2)}) collective-permute-start(bf16[222,18,1]{0,1,2:T(8,128)(2,1)S(1)} %get-tuple-element.2), channel_id=1, source_target_pairs={{0,1},{1,2},{2,3},{3,0},{4,5},{5,6},{6,7},{7,4},{8,9},{9,10},{10,1... | collective-permute-start | bytes 23984 | tf_op jit(solution)/shard_map/ppermute | solution.py:20
  28.0 2.4 copy-start
  72.0 16.5 %copy-start.4 = (s32[16384,1]{0,1:T(1,128)S(1)}, s32[16384,1]{0,1:T(1,128)}, u32[]{:S(2)}) copy-start(s32[16384,1]{0,1:T(1,128)} %param.13) | copy-start | bytes 196612
  72.0 16.5 %copy-start.6 = (s32[16384]{0:T(1024)S(1)}, s32[16384]{0:T(1024)}, u32[]{:S(2)}) copy-start(s32[16384]{0:T(1024)} %param.14) | copy-start | bytes 196612
  72.0 17.5 %copy-start.7 = (s32[4,4,3]{1,0,2:T(4,128)S(1)}, s32[4,4,3]{1,0,2:T(4,128)}, u32[]{:S(2)}) copy-start(s32[4,4,3]{1,0,2:T(4,128)} %param.15) | copy-start | bytes 580
  72.0 17.8 %copy-start.9 = (f32[128]{0:T(128)S(1)}, f32[128]{0:T(128)}, u32[]{:S(2)}) copy-start(f32[128]{0:T(128)} %param.17) | copy-start | bytes 1540
  72.0 116.8 %all-to-all-start = ((bf16[256,128,128]{2,1,0:T(8,128)(2,1)}), bf16[256,128,128]{2,1,0:T(8,128)(2,1)}, u32[]{:S(2)}, u32[]{:S(2)}) async-start(bf16[256,128,128]{2,1,0:T(8,128)(2,1)} %select_select_fusion.1), calls=%async_computation | async-start | bytes 16777216 | tf_op jit(solution)/shard_map/all_to_all | solution.py:119
  89.8 121.1 %copy-start.5 = (bf16[2,128,128]{2,1,0:T(8,128)(2,1)S(1)}, bf16[2,128,128]{2,1,0:T(8,128)(2,1)}, u32[]{:S(2)}) copy-start(bf16[2,128,128]{2,1,0:T(8,128)(2,1)} %param.16) | copy-start | bytes 196612
  197.6 10.1 %all-to-all-start.1 = ((bf16[4,4,4,16,128]{4,3,2,1,0:T(8,128)(2,1)}), bf16[4,4,4,16,128]{4,3,2,1,0:T(8,128)(2,1)S(1)}, u32[]{:S(2)}, u32[]{:S(2)}) async-start(bf16[4,4,4,16,128]{4,3,2,1,0:T(8,128)(2,1)} %broadcast_in_dim.158), calls=%async_computation.1 | async-start | bytes 524288 | tf_op jit(solution)/shard_map/all_to_all | solution.py:37
  207.6 7.2 %collective-permute-start.5 = (bf16[16,4,16,128]{3,2,1,0:T(8,128)(2,1)S(1)}, bf16[16,4,16,128]{3,2,1,0:T(8,128)(2,1)S(1)}, u32[]{:S(2)}, u32[]{:S(2)}) collective-permute-start(bf16[16,4,16,128]{3,2,1,0:T(8,128)(2,1)S(1)} %bitcast.248), channel_id=1, source_target_pairs={{0,124},{4,0},{8,4},{12,8},{16,12},{20,16},{24,20},{28,24},{32,28}... | collective-permute-start | bytes 786440 | tf_op jit(solution)/shard_map/ppermute | solution.py:47
  210.9 9.1 %collective-permute-start.4 = (bf16[16,4,16,128]{3,2,1,0:T(8,128)(2,1)S(1)}, bf16[16,4,16,128]{3,2,1,0:T(8,128)(2,1)S(1)}, u32[]{:S(2)}, u32[]{:S(2)}) collective-permute-start(bf16[16,4,16,128]{3,2,1,0:T(8,128)(2,1)S(1)} %bitcast.249), channel_id=1, source_target_pairs={{0,4},{4,8},{8,12},{12,16},{16,20},{20,24},{24,28},{28,32},{32,36}... | collective-permute-start | bytes 786440 | tf_op jit(solution)/shard_map/ppermute | solution.py:47
  220.5 1.8 copy-start.3
  225.4 10.1 %all-to-all-start.2 = ((bf16[4,4,4,16,128]{4,3,2,1,0:T(8,128)(2,1)}), bf16[4,4,4,16,128]{4,3,2,1,0:T(8,128)(2,1)S(1)}, u32[]{:S(2)}, u32[]{:S(2)}) async-start(bf16[4,4,4,16,128]{4,3,2,1,0:T(8,128)(2,1)} %broadcast_in_dim.164), calls=%async_computation.2 | async-start | bytes 524288 | tf_op jit(solution)/shard_map/all_to_all | solution.py:37
  235.5 3.9 collective-permute-start.7
  235.5 9.1 %collective-permute-start.6 = (bf16[16,4,16,128]{3,2,1,0:T(8,128)(2,1)S(1)}, bf16[16,4,16,128]{3,2,1,0:T(8,128)(2,1)S(1)}, u32[]{:S(2)}, u32[]{:S(2)}) collective-permute-start(bf16[16,4,16,128]{3,2,1,0:T(8,128)(2,1)S(1)} %bitcast.246), channel_id=1, source_target_pairs={{0,4},{4,8},{8,12},{12,16},{16,20},{20,24},{24,28},{28,32},{32,36}... | collective-permute-start | bytes 786440 | tf_op jit(solution)/shard_map/ppermute | solution.py:47
  263.2 106.8 %all-to-all-start.3 = ((bf16[256,128,128]{2,1,0:T(8,128)(2,1)}), bf16[256,128,128]{2,1,0:T(8,128)(2,1)}, u32[]{:S(2)}, u32[]{:S(2)}) async-start(bf16[256,128,128]{2,1,0:T(8,128)(2,1)} %select_select_fusion), calls=%async_computation.3 | async-start | bytes 16777216 | tf_op jit(solution)/shard_map/all_to_all | solution.py:119
  376.5 5.2 %copy-start.8 = (s32[128]{0:T(128)S(1)}, s32[128]{0:T(128)}, u32[]{:S(2)}) copy-start(s32[128]{0:T(128)} %param.12) | copy-start | bytes 1540
  381.6 8.0 %copy-start.2 = (f32[128,2048]{0,1:T(8,128)S(1)}, f32[128,2048]{0,1:T(8,128)}, u32[]{:S(2)}) copy-start(f32[128,2048]{0,1:T(8,128)} %get-tuple-element.59) | copy-start | bytes 3145732
  390.0 4.5 %collective-permute-start.9 = (bf16[128,1,128]{0,2,1:T(8,128)(2,1)S(1)}, bf16[128,1,128]{0,2,1:T(8,128)(2,1)S(1)}, u32[]{:S(2)}, u32[]{:S(2)}) collective-permute-start(bf16[128,1,128]{0,2,1:T(8,128)(2,1)S(1)} %get-tuple-element.27), channel_id=1, source_target_pairs={{4,0},{8,4},{12,8},{16,12},{20,16},{24,20},{28,24},{32,28},{36,32}... | collective-permute-start | bytes 98312 | tf_op jit(solution)/shard_map/ppermute | solution.py:22
  393.0 6.7 %collective-permute-start.8 = (bf16[128,1,128]{0,2,1:T(8,128)(2,1)S(1)}, bf16[128,1,128]{0,2,1:T(8,128)(2,1)S(1)}, u32[]{:S(2)}, u32[]{:S(2)}) collective-permute-start(bf16[128,1,128]{0,2,1:T(8,128)(2,1)S(1)} %get-tuple-element.26), channel_id=1, source_target_pairs={{0,4},{4,8},{8,12},{12,16},{16,20},{20,24},{24,28},{28,32},{32,36}... | collective-permute-start | bytes 98312 | tf_op jit(solution)/shard_map/ppermute | solution.py:20
  399.6 4.0 collective-permute-start.11
  400.0 4.9 %collective-permute-start.10 = (bf16[128,18,1]{0,2,1:T(2,128)(2,1)S(1)}, bf16[128,18,1]{0,2,1:T(2,128)(2,1)S(1)}, u32[]{:S(2)}, u32[]{:S(2)}) collective-permute-start(bf16[128,18,1]{0,2,1:T(2,128)(2,1)S(1)} %get-tuple-element.24), channel_id=1, source_target_pairs={{0,1},{1,2},{2,3},{3,0},{4,5},{5,6},{6,7},{7,4},{8,9},{9,10},{10,1... | collective-permute-start | bytes 13832 | tf_op jit(solution)/shard_map/ppermute | solution.py:20
  405.2 1.0 copy-start.1
where the time goes:
time: 420 us; the launch traced here: 412 us
  waiting for transfers between devices  242 us (58%)
  local copies, waits for them, and re-layouts  50 us (12%)
  starting transfers between devices  47.6 us (11%)
  matrix products  41.9 us (10%)
  other arithmetic  29 us (7%)
    all_to_all x2, waiting for transfers between devices, route(): lax.all_to_all(buffer, ('lon', 'lat'), split_axis=0, concat_axis=0, tiled...  200 us
    all_to_all x2, starting transfers between devices, route(): lax.all_to_all(buffer, ('lon', 'lat'), split_axis=0, concat_axis=0, tiled...  22.5 us
    ppermute x4, waiting for transfers between devices, passed_along(): return lax.ppermute(value, axis, pairs)  15.6 us
    all_to_all x2, waiting for transfers between devices, from_everyone(): lax.all_to_all(jnp.broadcast_to(x[None], (peers, *x.shape)), axis, 0, 0,...  12.4 us
    ppermute x4, starting transfers between devices, extended(): lax.ppermute(head, axis, [((i + 1) % count, i) for i in range(count)])  12.2 us
    gather x1, local copies, waits for them, and re-layouts, on_device(): jnp.take(contrib, block_of_slot, axis=0)  10.6 us
    ppermute x4, waiting for transfers between devices, extended(): lax.ppermute(tail, axis, [(i, (i + 1) % count) for i in range(count)])  10.1 us
    dot_general x1, matrix products, on_device(): jnp.einsum('bij,cbj->bic', regrid_blocks, sources, preferred_element_type...  8.5 us
  transfers between devices with their start and end apart: 16, of which 14 were waited for; matrix products, arithmetic and copies ran while one was open for 3% of the time, Pallas kernels for 0%

commit v1 on v0

--- a/solution.py
+++ b/solution.py
@@ -1,13 +1,22 @@
+import functools
+
 import jax
 import jax.numpy as jnp
 from jax import lax
+from jax.experimental import pallas as pl
+from jax.experimental.pallas import tpu as pltpu
 from jax.sharding import PartitionSpec as P
 
 TS = 16
-CAP = 2
-
-
+RING = 4
+BLOCK = 128
+HALVES = 8
+MESH = pl.DeviceIdType.MESH
 LOG_TWO = 0.6931471805599453
+
+PARTS = ((0, 48), (48, 48), (96, 32))
+LINE = ("y", "z", "x")
+PLANE = (("z", "x"), ("x", "y"), ("y", "z"))
 
 
 def extended(cells, sides, width):
@@ -115,10 +124,6 @@
     return jnp.where(outside, jnp.zeros_like(padded), padded)
 
 
-def route(buffer):
-    return lax.all_to_all(buffer, ("lon", "lat"), split_axis=0, concat_axis=0, tiled=True)
-
-
 def pick_rims(edge_rows, tile_pos, side_pos, flip_bit):
     tile_count = edge_rows.shape[0]
     flat_edges = edge_rows.reshape(tile_count * 4, -1)
@@ -152,6 +157,470 @@
     relative = (owner_col - lax.axis_index("lon") + 1) % lax.axis_size("lon")
     position = relative * column_tiles + neighbours[:, :, 0] % column_tiles
     return pick_rims(joined, position, neighbours[:, :, 1], neighbours[:, :, 2])
+
+
+def torus_position():
+    lon = lax.axis_index("lon")
+    return {"z": lon // 8, "x": (lon // 2) % 4, "c": lon % 2, "y": lax.axis_index("lat")}
+
+
+def moved(here, **steps):
+    place = dict(here)
+    for axis, step in steps.items():
+        if axis == "c":
+            place["c"] = (here["c"] + step) % 2
+        else:
+            place[axis] = (here[axis] + step + RING) % RING
+    return place
+
+
+def device_at(place):
+    return (place["z"] * 8 + place["x"] * 2 + place["c"], place["y"])
+
+
+def meet(peers):
+    barrier = pltpu.get_barrier_semaphore()
+    for peer in peers:
+        pl.semaphore_signal(barrier, inc=1, device_id=device_at(peer), device_id_type=MESH)
+    pl.semaphore_wait(barrier, len(peers))
+
+
+def line_body(sign, s0, s1, s2, r0, r1, r2, send, recv, local):
+    here = torus_position()
+    peers = [moved(here, c=1)]
+    for axis in LINE:
+        for step in range(1, RING):
+            for flip in range(2):
+                peers.append(moved(here, **{axis: step, "c": flip}))
+    meet(peers)
+    sources, targets = (s0, s1, s2), (r0, r1, r2)
+    copies = []
+    for chunk in (4, 5, 2, 3, 6, 7, 1):
+        step, flip = chunk // 2, chunk % 2
+        for k in range(3):
+            copy = pltpu.make_async_remote_copy(
+                src_ref=sources[k].at[chunk],
+                dst_ref=targets[k].at[chunk],
+                send_sem=send.at[k, chunk],
+                recv_sem=recv.at[k, chunk],
+                device_id=device_at(moved(here, **{LINE[k]: sign * step, "c": flip})),
+                device_id_type=MESH,
+            )
+            copy.start()
+            copies.append(copy)
+    own = []
+    for k in range(3):
+        copy = pltpu.make_async_copy(sources[k].at[0], targets[k].at[0], local.at[k])
+        copy.start()
+        own.append(copy)
+    for copy in own + copies:
+        copy.wait()
+
+
+def line_exchange(parts, sign, collective_id):
+    anywhere = pl.BlockSpec(memory_space=pl.ANY)
+    return pl.pallas_call(
+        functools.partial(line_body, sign),
+        out_shape=[jax.ShapeDtypeStruct(part.shape, part.dtype) for part in parts],
+        in_specs=[anywhere] * 3,
+        out_specs=[anywhere] * 3,
+        scratch_shapes=[
+            pltpu.SemaphoreType.DMA((3, 8)),
+            pltpu.SemaphoreType.DMA((3, 8)),
+            pltpu.SemaphoreType.DMA((3,)),
+        ],
+        compiler_params=pltpu.CompilerParams(collective_id=collective_id, has_side_effects=True),
+        name="line_exchange_%d" % collective_id,
+    )(*parts)
+
+
+def plane_body(p0, p1, p2, q0, q1, q2, send, recv, local):
+    here = torus_position()
+    peers = []
+    for axis in LINE:
+        for step in range(1, RING):
+            peers.append(moved(here, **{axis: step}))
+    for first, second in PLANE:
+        for step in range(1, RING):
+            for other in range(1, RING):
+                peers.append(moved(here, **{first: step, second: other}))
+    meet(peers)
+    sources, targets = (p0, p1, p2), (q0, q1, q2)
+    copies = []
+    for place in (10, 5, 15, 7, 13, 9, 11, 6, 14, 2, 8, 1, 3, 4, 12):
+        for k in range(3):
+            copy = pltpu.make_async_remote_copy(
+                src_ref=sources[k].at[place],
+                dst_ref=targets[k].at[place],
+                send_sem=send.at[k, place],
+                recv_sem=recv.at[k, place],
+                device_id=device_at(
+                    moved(here, **{PLANE[k][0]: place // RING, PLANE[k][1]: place % RING})
+                ),
+                device_id_type=MESH,
+            )
+            copy.start()
+            copies.append(copy)
+    own = []
+    for k in range(3):
+        copy = pltpu.make_async_copy(sources[k].at[0], targets[k].at[0], local.at[k])
+        copy.start()
+        own.append(copy)
+    for copy in own + copies:
+        copy.wait()
+
+
+def plane_scatter(parts, collective_id):
+    anywhere = pl.BlockSpec(memory_space=pl.ANY)
+    return pl.pallas_call(
+        plane_body,
+        out_shape=[jax.ShapeDtypeStruct(part.shape, part.dtype) for part in parts],
+        in_specs=[anywhere] * 3,
+        out_specs=[anywhere] * 3,
+        scratch_shapes=[
+            pltpu.SemaphoreType.DMA((3, 16)),
+            pltpu.SemaphoreType.DMA((3, 16)),
+            pltpu.SemaphoreType.DMA((3,)),
+        ],
+        compiler_params=pltpu.CompilerParams(collective_id=collective_id, has_side_effects=True),
+        name="plane_scatter",
+    )(*parts)
+
+
+def gather_body(grad, u0, u1, u2, send, recv, local):
+    here = torus_position()
+    peers = []
+    for axis in LINE:
+        for step in range(1, RING):
+            peers.append(moved(here, **{axis: step}))
+    meet(peers)
+    targets = (u0, u1, u2)
+
+    def sent(k, source, place, axis, step):
+        copy = pltpu.make_async_remote_copy(
+            src_ref=source,
+            dst_ref=targets[k].at[place],
+            send_sem=send.at[k, place],
+            recv_sem=recv.at[k, place],
+            device_id=device_at(moved(here, **{axis: -step})),
+            device_id_type=MESH,
+        )
+        copy.start()
+        return copy
+
+    first, later = {}, []
+    mine = [grad.at[:, pl.ds(start, count)] for start, count in PARTS]
+    for step in (2, 1, 3):
+        for k in range(3):
+            first[k, step] = sent(k, mine[k], step, PLANE[k][1], step)
+    for step in (2, 1, 3):
+        for k in range(3):
+            later.append(sent(k, mine[k], step * RING, PLANE[k][0], step))
+    own = []
+    for k in range(3):
+        copy = pltpu.make_async_copy(mine[k], targets[k].at[0], local.at[k])
+        copy.start()
+        own.append(copy)
+    for step in (1, 3, 2):
+        for k in range(3):
+            first[k, step].wait_recv()
+            for hop in (2, 1, 3):
+                later.append(sent(k, targets[k].at[step], hop * RING + step, PLANE[k][0], hop))
+    for copy in own + later:
+        copy.wait()
+    for copy in first.values():
+        copy.wait_send()
+
+
+def plane_gather(grad, collective_id):
+    anywhere = pl.BlockSpec(memory_space=pl.ANY)
+    return pl.pallas_call(
+        gather_body,
+        out_shape=[
+            jax.ShapeDtypeStruct((16, HALVES, count, grad.shape[2]), grad.dtype)
+            for _, count in PARTS
+        ],
+        in_specs=[anywhere],
+        out_specs=[anywhere] * 3,
+        scratch_shapes=[
+            pltpu.SemaphoreType.DMA((3, 16)),
+            pltpu.SemaphoreType.DMA((3, 16)),
+            pltpu.SemaphoreType.DMA((3,)),
+        ],
+        compiler_params=pltpu.CompilerParams(collective_id=collective_id, has_side_effects=True),
+        name="plane_gather",
+    )(grad)
+
+
+def spread_body(table, hidden, blocks, o0, o1, o2, turned, stage, sems):
+    step = pl.program_id(0)
+    last = pl.num_programs(0) - 1
+    slot = step % 2
+    outs = (o0, o1, o2)
+
+    def drained(which):
+        pltpu.make_async_copy(stage.at[which], stage.at[which], sems.at[which]).wait()
+
+    @pl.when(step == 0)
+    def _():
+        for k in range(turned.shape[0]):
+            turned[k] = hidden[:, k * BLOCK : (k + 1) * BLOCK].T
+
+    @pl.when(step >= 2)
+    def _():
+        drained(slot)
+
+    for b in range(blocks.shape[0]):
+        block = step * blocks.shape[0] + b
+        stage[slot, b] = jnp.dot(
+            blocks[b], turned[table[0, block]], preferred_element_type=jnp.float32
+        ).astype(stage.dtype)
+        for k, (start, count) in enumerate(PARTS):
+            pltpu.make_async_copy(
+                stage.at[slot, b, pl.ds(start, count)],
+                outs[k].at[table[1 + 2 * k, block], table[2 + 2 * k, block]],
+                sems.at[slot],
+            ).start()
+
+    @pl.when(step == last)
+    def _():
+        drained(1 - slot)
+        drained(slot)
+
+
+def spread(table, hidden, regrid_blocks):
+    count, rows, cells = regrid_blocks.shape
+    width = hidden.shape[0]
+    group = 8
+    return pl.pallas_call(
+        spread_body,
+        grid_spec=pltpu.PrefetchScalarGridSpec(
+            num_scalar_prefetch=1,
+            grid=(count // group,),
+            in_specs=[
+                pl.BlockSpec(hidden.shape, lambda i, t: (0, 0)),
+                pl.BlockSpec((group, rows, cells), lambda i, t: (i, 0, 0)),
+            ],
+            out_specs=[pl.BlockSpec(memory_space=pl.ANY)] * 3,
+            scratch_shapes=[
+                pltpu.VMEM((hidden.shape[1] // BLOCK, cells, width), jnp.bfloat16),
+                pltpu.VMEM((2, group, rows, width), jnp.bfloat16),
+                pltpu.SemaphoreType.DMA((2,)),
+            ],
+        ),
+        out_shape=[jax.ShapeDtypeStruct((8, 32, n, width), jnp.bfloat16) for _, n in PARTS],
+        name="spread",
+    )(table, hidden, regrid_blocks)
+
+
+def source_and_place(spot, k, chunk, place):
+    here = {"z": spot[0], "x": spot[1], "c": spot[2], "y": spot[3]}
+    line = (here[LINE[k]] + RING - chunk // 2) % RING
+    core = (here["c"] + chunk % 2) % 2
+    source = core * RING + line if k == 0 else line * 2 + core
+    first = (here[PLANE[k][0]] + place // RING) % RING
+    second = (here[PLANE[k][1]] + place % RING) % RING
+    return k * 256 + source * 32 + (first * RING + second) * 2
+
+
+def combine_body(spot, table, r0, r1, r2, p0, p1, p2, a0, a1, a2):
+    place = pl.program_id(0)
+    ins, outs, sums = (r0, r1, r2), (p0, p1, p2), (a0, a1, a2)
+    for total in sums:
+        total[...] = jnp.zeros_like(total)
+    for chunk in range(8):
+        for k in range(3):
+            entry = source_and_place(spot, k, chunk, place)
+            for rank in range(2):
+                half = table[entry + rank]
+                sums[k][half] += ins[k][chunk, rank].astype(jnp.float32)
+    for k in range(3):
+        outs[k][0] = sums[k][:HALVES].astype(jnp.bfloat16)
+
+
+def combine(spot, table, parts):
+    width = parts[0].shape[-1]
+    return pl.pallas_call(
+        combine_body,
+        grid_spec=pltpu.PrefetchScalarGridSpec(
+            num_scalar_prefetch=2,
+            grid=(16,),
+            in_specs=[pl.BlockSpec((8, 2, n, width), lambda i, s, t: (0, i, 0, 0)) for _, n in PARTS],
+            out_specs=[
+                pl.BlockSpec((1, HALVES, n, width), lambda i, s, t: (i, 0, 0, 0)) for _, n in PARTS
+            ],
+            scratch_shapes=[pltpu.VMEM((HALVES + 1, n, width), jnp.float32) for _, n in PARTS],
+        ),
+        out_shape=[jax.ShapeDtypeStruct((16, HALVES, n, width), jnp.bfloat16) for _, n in PARTS],
+        name="combine",
+    )(spot, table, *parts)
+
+
+def total_body(q0, q1, q2, out):
+    for (start, count), part in zip(PARTS, (q0, q1, q2)):
+        out[0, start : start + count] = jnp.sum(part[:, 0].astype(jnp.float32), axis=0).astype(
+            out.dtype
+        )
+
+
+def total(parts):
+    width = parts[0].shape[-1]
+    return pl.pallas_call(
+        total_body,
+        grid=(HALVES,),
+        in_specs=[pl.BlockSpec((16, 1, n, width), lambda i: (0, i, 0, 0)) for _, n in PARTS],
+        out_specs=pl.BlockSpec((1, BLOCK, width), lambda i: (i, 0, 0)),
+        out_shape=jax.ShapeDtypeStruct((HALVES, BLOCK, width), jnp.bfloat16),
+        name="total",
+    )(*parts)
+
+
+def serve_body(spot, table, u0, u1, u2, v0, v1, v2):
+    chunk = pl.program_id(0)
+    ins, outs = (u0, u1, u2), (v0, v1, v2)
+    for place in range(16):
+        for k in range(3):
+            entry = source_and_place(spot, k, chunk, place)
+            for rank in range(2):
+                half = jnp.minimum(table[entry + rank], HALVES - 1)
+                outs[k][0, place * 2 + rank] = ins[k][place, half]
+
+
+def serve(spot, table, parts):
+    width = parts[0].shape[-1]
+    return pl.pallas_call(
+        serve_body,
+        grid_spec=pltpu.PrefetchScalarGridSpec(
+            num_scalar_prefetch=2,
+            grid=(8,),
+            in_specs=[
+                pl.BlockSpec((16, HALVES, n, width), lambda i, s, t: (0, 0, 0, 0))
+                for _, n in PARTS
+            ],
+            out_specs=[pl.BlockSpec((1, 32, n, width), lambda i, s, t: (i, 0, 0, 0)) for _, n in PARTS],
+        ),
+        out_shape=[jax.ShapeDtypeStruct((8, 32, n, width), jnp.bfloat16) for _, n in PARTS],
+        name="serve",
+    )(spot, table, *parts)
+
+
+def pull_body(table, blocks, pre_conv, w0, w1, w2, out, stage, sums, sems):
+    step = pl.program_id(0)
+    steps = pl.num_programs(0)
+    group = blocks.shape[0]
+    slot = step % 2
+    ins = (w0, w1, w2)
+
+    def fetch(which, into):
+        for b in range(group):
+            block = which * group + b
+            for k, (start, count) in enumerate(PARTS):
+                pltpu.make_async_copy(
+                    ins[k].at[table[1 + 2 * k, block], table[2 + 2 * k, block]],
+                    stage.at[into, b, pl.ds(start, count)],
+                    sems.at[into],
+                ).start()
+
+    @pl.when(step == 0)
+    def _():
+        fetch(0, 0)
+        sums[...] = jnp.zeros_like(sums)
+
+    @pl.when(step + 1 < steps)
+    def _():
+        fetch(step + 1, 1 - slot)
+
+    pltpu.make_async_copy(stage.at[slot], stage.at[slot], sems.at[slot]).wait()
+    for b in range(group):
+        source = table[0, step * group + b]
+        sums[source] += lax.dot_general(
+            stage[slot, b],
+            blocks[b],
+            (((0,), (0,)), ((), ())),
+            preferred_element_type=jnp.float32,
+        )
+
+    @pl.when(step + 1 == steps)
+    def _():
+        for k in range(sums.shape[0]):
+            cells = slice(k * BLOCK, (k + 1) * BLOCK)
+            out[:, cells] = (sums[k] * silu_slope(pre_conv[:, cells])).astype(out.dtype)
+
+
+def pull(table, regrid_blocks, pre_conv, parts):
+    count, rows, cells = regrid_blocks.shape
+    width = pre_conv.shape[0]
+    group = 8
+    return pl.pallas_call(
+        pull_body,
+        grid_spec=pltpu.PrefetchScalarGridSpec(
+            num_scalar_prefetch=1,
+            grid=(count // group,),
+            in_specs=[
+                pl.BlockSpec((group, rows, cells), lambda i, t: (i, 0, 0)),
+                pl.BlockSpec(pre_conv.shape, lambda i, t: (0, 0)),
+            ]
+            + [pl.BlockSpec(memory_space=pl.ANY)] * 3,
+            out_specs=pl.BlockSpec(pre_conv.shape, lambda i, t: (0, 0)),
+            scratch_shapes=[
+                pltpu.VMEM((2, group, rows, width), jnp.bfloat16),
+                pltpu.VMEM((pre_conv.shape[1] // BLOCK, width, cells), jnp.float32),
+                pltpu.SemaphoreType.DMA((2,)),
+            ],
+        ),
+        out_shape=jax.ShapeDtypeStruct(pre_conv.shape, jnp.bfloat16),
+        name="pull",
+    )(table, regrid_blocks, pre_conv, *parts)
+
+
+def routing(source_block, target_device, target_half):
+    here = torus_position()
+    count = source_block.shape[0]
+
+    def rows_of(values):
+        grid = values.reshape(4, 4, 2, 4, count)
+        picks = []
+        for k in range(3):
+            start = [here["z"], here["x"], 0, here["y"], 0]
+            size = [1, 1, 2, 1, count]
+            at = {"z": 0, "x": 1, "y": 3}[LINE[k]]
+            start[at], size[at] = 0, 4
+            picks.append(lax.dynamic_slice(grid, start, size).reshape(8, count))
+        own = lax.dynamic_slice(
+            grid, [here["z"], here["x"], here["c"], here["y"], 0], [1, 1, 1, 1, count]
+        )
+        return jnp.concatenate(picks + [own.reshape(1, count)], axis=0)
+
+    targets = rows_of(target_device[:, 0])
+    halves = rows_of(target_half)[:24]
+    ids = jnp.arange(count, dtype=jnp.int32)
+    rank = jnp.sum(
+        (targets[:, :, None] == targets[:, None, :]) & (ids[None, None, :] < ids[None, :, None]),
+        axis=2,
+        dtype=jnp.int32,
+    )
+    to = {"z": targets // 32, "x": (targets // 8) % 4, "c": (targets // 4) % 2, "y": targets % 4}
+    codes = []
+    for k in range(3):
+        rows = slice(8 * k, 8 * k + 8)
+        fits = (to["c"][rows] == here["c"]) & (to[LINE[k]][rows] == here[LINE[k]])
+        code = (to[PLANE[k][0]][rows] * RING + to[PLANE[k][1]][rows]) * 2 + rank[rows]
+        codes.append(jnp.where(fits, code, -1))
+    codes = jnp.concatenate(codes, axis=0)
+    slots = jnp.arange(32, dtype=jnp.int32)
+    table = HALVES + jnp.sum(
+        jnp.where(codes[:, None, :] == slots[None, :, None], (halves - HALVES)[:, None, :], 0),
+        axis=2,
+    )
+    own = {axis: value[24] for axis, value in to.items()}
+    away = {axis: (own[axis] - here[axis] + RING) % RING for axis in ("z", "x", "y")}
+    flip = (own["c"] + here["c"]) % 2
+    lines = [source_block]
+    for k in range(3):
+        lines.append(away[LINE[k]] * 2 + flip)
+        lines.append((away[PLANE[k][0]] * RING + away[PLANE[k][1]]) * 2 + rank[24])
+    spot = jnp.stack([here["z"], here["x"], here["c"], here["y"]]).astype(jnp.int32)
+    return spot, table.reshape(-1), jnp.stack(lines)
 
 
 def on_device(
@@ -167,55 +636,14 @@
 ):
     channels, lon_cells, lat_cells = fields.shape
     latent_width = conv_weight.shape[1]
-    block_rows = regrid_blocks.shape[1]
-    block_count = regrid_blocks.shape[0]
-    device_count = lax.axis_size("lon") * lax.axis_size("lat")
-    device_pos = lax.axis_index(("lon", "lat"))
-    source_count = lon_cells * lat_cells // block_rows
     tile_count = neighbours.shape[0]
-    half_count = tile_count * TS * TS // block_rows
+    spot, table, lines = routing(source_block, target_device, target_half)
     pre_conv = conv_taps(conv_weight, grid_rims(fields), False)
     hidden = jax.nn.silu(pre_conv).astype(jnp.bfloat16)
-    sources = jnp.take(hidden.reshape(latent_width, source_count, block_rows), source_block, axis=1)
-    contrib = jnp.einsum(
-        "bij,cbj->bic", regrid_blocks, sources, preferred_element_type=jnp.float32
-    ).astype(jnp.bfloat16)
-    all_targets = target_device[:, 0].reshape(device_count, block_count)
-    all_halves = target_half.reshape(device_count, block_count)
-    device_ids = jnp.arange(device_count, dtype=jnp.int32)
-    target_hits = all_targets[:, :, None] == device_ids
-    arrival_rank = jnp.sum(
-        jnp.where(target_hits, jnp.cumsum(target_hits.astype(jnp.int32), axis=1) - 1, 0), axis=2
-    )
-    own_targets = lax.dynamic_index_in_dim(all_targets, device_pos, 0, False)
-    own_ranks = lax.dynamic_index_in_dim(arrival_rank, device_pos, 0, False)
-    slot_of_block = own_targets * CAP + own_ranks
-    slot_count = device_count * CAP
-    slot_ids = jnp.arange(slot_count, dtype=jnp.int32)
-    slot_match = slot_of_block[None, :] == slot_ids[:, None]
-    block_of_slot = jnp.sum(
-        jnp.where(slot_match, jnp.arange(block_count, dtype=jnp.int32)[None, :], 0), axis=1
-    )
-    slot_used = jnp.any(slot_match, axis=1)
-    outgoing = jnp.where(
-        slot_used[:, None, None],
-        jnp.take(contrib, block_of_slot, axis=0),
-        jnp.zeros((), jnp.bfloat16),
-    )
-    incoming = route(outgoing)
-    to_me = all_targets == device_pos
-    arrival = to_me[:, :, None] & (arrival_rank[:, :, None] == jnp.arange(CAP, dtype=jnp.int32))
-    half_of_slot = jnp.sum(jnp.where(arrival, all_halves[:, :, None], 0), axis=1).reshape(
-        slot_count
-    )
-    slot_live = jnp.any(arrival, axis=1).reshape(slot_count)
-    placing = (
-        (half_of_slot[None, :] == jnp.arange(half_count, dtype=jnp.int32)[:, None])
-        & slot_live[None, :]
-    ).astype(jnp.bfloat16)
-    latent_in = jnp.einsum(
-        "hs,sic->hic", placing, incoming, preferred_element_type=jnp.float32
-    ).astype(jnp.bfloat16)
+    outgoing = spread(lines, hidden, regrid_blocks)
+    arrived = line_exchange(outgoing, 1, 0)
+    partial = combine(spot, table, arrived)
+    latent_in = total(plane_scatter(partial, 1))
     tiles_in = latent_in.reshape(tile_count, TS, TS, latent_width)
     flat_latent = latent_in.reshape(-1, latent_width)
     rim_values = fetch_rims(tile_edges(tiles_in), neighbours)
@@ -237,27 +665,11 @@
     latent_grad = (
         self_grad + neighbour_sum(near_grad, back_rims).reshape(-1, latent_width)
     ).astype(jnp.bfloat16)
-    halves_grad = latent_grad.reshape(half_count, block_rows, latent_width)
-    replies = jnp.where(
-        slot_live[:, None, None],
-        jnp.take(halves_grad, half_of_slot, axis=0),
-        jnp.zeros((), jnp.bfloat16),
-    )
-    answers = route(replies)
-    contrib_grad = jnp.take(answers, slot_of_block, axis=0)
-    source_grad = jnp.einsum(
-        "bij,bic->bcj", regrid_blocks, contrib_grad, preferred_element_type=jnp.float32
-    )
-    source_onehot = (
-        source_block[:, None] == jnp.arange(source_count, dtype=jnp.int32)[None, :]
-    ).astype(jnp.float32)
-    hidden_grad = jnp.einsum(
-        "bs,bcj->csj", source_onehot, source_grad, precision=lax.Precision.HIGHEST
-    ).reshape(latent_width, -1)
-    pre_grad = (
-        (hidden_grad * silu_slope(pre_conv))
-        .astype(jnp.bfloat16)
-        .reshape(latent_width, lon_cells, lat_cells)
+    halves_grad = latent_grad.reshape(HALVES, BLOCK, latent_width)
+    replies = serve(spot, table, plane_gather(halves_grad, 2))
+    answers = line_exchange(replies, -1, 3)
+    pre_grad = pull(lines, regrid_blocks, pre_conv, answers).reshape(
+        latent_width, lon_cells, lat_cells
     )
     grad_fields = conv_taps(conv_weight, grid_rims(pre_grad), True).reshape(
         channels, lon_cells, lat_cells

time: 420 us -> 302 us (0.72); the launches traced: 412 us -> 300 us
  waiting for transfers between devices: 242 us -> 24.9 us
  Pallas kernels: 0 us -> 200 us
  local copies, waits for them, and re-layouts: 50 us -> 20.2 us
  matrix products: 41.9 us -> 14.2 us
  other arithmetic: 29 us -> 5.42 us
  starting transfers between devices: 47.6 us -> 25.5 us
  blocking collectives: 0 us -> 9.2 us
    all_to_all x2 -> x0, waiting for transfers between devices: 200 us -> none  [route(): lax.all_to_all(buffer, ('lon', 'lat'), split_axis=0, concat_axis=0, tiled...]
    pallas_call x0 -> x9, Pallas kernels: none -> 200 us  [the longest x2 79.3 us: line_exchange(): pl.pallas_call(functools.partial(line_body, sign), out_shape=[jax.ShapeDt...]
    dot_general x4 -> x0, matrix products: 29 us -> none  [the longest x1 8.5 us: on_device(): jnp.einsum('bij,cbj->bic', regrid_blocks, sources, preferred_element_type...]
    gather x4 -> x0, local copies, waits for them, and re-layouts: 28.6 us -> none  [the longest x1 10.6 us: on_device(): jnp.take(contrib, block_of_slot, axis=0)]
    all_to_all x2 -> x0, starting transfers between devices: 22.5 us -> none  [route(): lax.all_to_all(buffer, ('lon', 'lat'), split_axis=0, concat_axis=0, tiled...]
    select_n x6 -> x2, other arithmetic: 16 us -> 0.06 us  [the longest x1 0.05 us: routing(): targets // 8 % 4]
    all_to_all x0 -> x1, blocking collectives: none -> 9.2 us  [from_everyone(): lax.all_to_all(jnp.broadcast_to(x[None], (peers, *x.shape)), axis, 0, 0,...]
    ppermute x4, waiting for transfers between devices: 10.1 us -> 3.43 us  [extended(): lax.ppermute(tail, axis, [(i, (i + 1) % count) for i in range(count)])]
  transfers between devices with their start and end apart: 16 -> 13, of which waited for: 14 -> 7; matrix products, arithmetic and copies ran while one was open for 3% -> 3% of each run, Pallas kernels for 0% -> 0%
where the time goes in v1:
time: 302 us; the launch traced here: 300 us
  Pallas kernels  200 us (66%)
  starting transfers between devices  25.5 us (8%)
  waiting for transfers between devices  24.9 us (8%)
  local copies, waits for them, and re-layouts  20.2 us (7%)
  matrix products  14.2 us (5%)
  blocking collectives  9.2 us (3%)
  other arithmetic  5.42 us (2%)
    pallas_call x2, Pallas kernels, line_exchange(): pl.pallas_call(functools.partial(line_body, sign), out_shape=[jax.ShapeDt...  79.3 us
    pallas_call x1, Pallas kernels, plane_scatter(): pl.pallas_call(plane_body, out_shape=[jax.ShapeDtypeStruct(part.shape, pa...  42 us
    pallas_call x1, Pallas kernels, plane_gather(): pl.pallas_call(gather_body, out_shape=[jax.ShapeDtypeStruct((16, HALVES,...  22.9 us
    ppermute x4, waiting for transfers between devices, passed_along(): return lax.ppermute(value, axis, pairs)  15.7 us
    pallas_call x1, Pallas kernels, pull(): pl.pallas_call(pull_body, grid_spec=pltpu.PrefetchScalarGridSpec(num_scal...  15.3 us
    ppermute x4, starting transfers between devices, extended(): lax.ppermute(head, axis, [((i + 1) % count, i) for i in range(count)])  15.2 us
    pallas_call x1, Pallas kernels, combine(): pl.pallas_call(combine_body, grid_spec=pltpu.PrefetchScalarGridSpec(num_s...  13.2 us
    pallas_call x1, Pallas kernels, spread(): pl.pallas_call(spread_body, grid_spec=pltpu.PrefetchScalarGridSpec(num_sc...  12 us
  transfers between devices with their start and end apart: 13, of which 7 were waited for; matrix products, arithmetic and copies ran while one was open for 3% of the time, Pallas kernels for 0%

profile of v1, /device:TPU:0, one launch (start us, length us, event | category | flops | bytes accessed | tf_op | source)
XLA Modules:
  0.0 300.5 jit_solution(11254378739918894526)
XLA Ops:
  0.7 2.1 copy.91
  3.1 5.9 %collective-permute-start.1 = (bf16[222,1,128]{0,1,2:T(2,128)(2,1)S(1)}, bf16[222,1,128]{0,1,2:T(2,128)(2,1)S(1)}, u32[]{:S(2)}, u32[]{:S(2)}) collective-permute-start(bf16[222,1,128]{0,1,2:T(2,128)(2,1)S(1)} %get-tuple-element.62), channel_id=1, source_target_pairs={{4,0},{8,4},{12,8},{16,12},{20,16},{24,20},{28,24},{32,28},{36,32}... | collective-permute-start | bytes 170504 | tf_op jit(solution)/shard_map/ppermute | solution.py:31
  9.0 0.7 constant_dynamic-slice_fusion
  9.8 0.7 constant_dynamic-slice_fusion.1
  10.5 0.7 constant_dynamic-slice_fusion.2
  11.3 1.2 convert_reduce_fusion
  13.1 1.0 pad_maximum_fusion
  14.1 1.6 collective-permute-start.2
  15.8 1.7 collective-permute-start.3
  18.3 0.7 add.360.table
  19.0 0.6 stack.39.table
  19.9 0.7 maximum_select_fusion
  20.6 2.4 fusion.120
  27.0 1.6 multiply_convert_fusion
  28.6 12.0 %spread.1 = (bf16[8,32,48,128]{3,2,1,0:T(8,128)(2,1)}, bf16[8,32,48,128]{3,2,1,0:T(8,128)(2,1)}, bf16[8,32,32,128]{3,2,1,0:T(8,128)(2,1)}) custom-call(s32[7,128]{1,0:T(8,128)} %stack.39.table, bf16[128,2048]{1,0:T(8,128)(2,1)} %get-tuple-element.117.hidden, bf16[128,128,128]{2,1,0:T(8,128)(2,1)} %blocks.3), custom_call_target="tpu_custom_call" | custom-call | tf_op jit(solution)/shard_map/spread/pallas_call | solution.py:395
  40.6 40.2 %line_exchange_0.1 = (bf16[8,32,48,128]{3,2,1,0:T(8,128)(2,1)}, bf16[8,32,48,128]{3,2,1,0:T(8,128)(2,1)}, bf16[8,32,32,128]{3,2,1,0:T(8,128)(2,1)}) custom-call(bf16[8,32,48,128]{3,2,1,0:T(8,128)(2,1)} %get-tuple-element.23.s0, bf16[8,32,48,128]{3,2,1,0:T(8,128)(2,1)} %get-tuple-element.24.s1, bf16[8,32,32,128]{3,2,1,0:T(8,128)(2,1)} %get-tuple-element.25.s2), custom_call_target="tpu_custom_call" | custom-call | tf_op jit(solution)/shard_map/line_exchange_0/pallas_call | solution.py:222
  80.8 13.2 %combine.1 = (bf16[16,8,48,128]{3,2,1,0:T(8,128)(2,1)}, bf16[16,8,48,128]{3,2,1,0:T(8,128)(2,1)}, bf16[16,8,32,128]{3,2,1,0:T(8,128)(2,1)}) custom-call(s32[4]{0:T(128)} %pad_add_fusion.2.spot, s32[768]{0:T(1024)} %add.360.table, bf16[8,32,48,128]{3,2,1,0:T(8,128)(2,1)} %get-tuple-element.26.r0, bf16[8,32,48,128]{3,2,1,0:T(8,128)(2,1)} %get-tuple-element.27.r1, ...), custom_call_target="tpu_custom_call" | custom-call | tf_op jit(solution)/shard_map/combine/pallas_call | solution.py:443
  94.0 42.0 %plane_scatter.1 = (bf16[16,8,48,128]{3,2,1,0:T(8,128)(2,1)}, bf16[16,8,48,128]{3,2,1,0:T(8,128)(2,1)}, bf16[16,8,32,128]{3,2,1,0:T(8,128)(2,1)}) custom-call(bf16[16,8,48,128]{3,2,1,0:T(8,128)(2,1)} %get-tuple-element.29.p0, bf16[16,8,48,128]{3,2,1,0:T(8,128)(2,1)} %get-tuple-element.30.p1, bf16[16,8,32,128]{3,2,1,0:T(8,128)(2,1)} %get-tuple-element.31.p2), custom_call_target="tpu_custom_call" | custom-call | tf_op jit(solution)/shard_map/plane_scatter/pallas_call | solution.py:275
  136.0 5.9 %total.1 = bf16[8,128,128]{2,1,0:T(8,128)(2,1)} custom-call(bf16[16,8,48,128]{3,2,1,0:T(8,128)(2,1)} %get-tuple-element.32.q0, bf16[16,8,48,128]{3,2,1,0:T(8,128)(2,1)} %get-tuple-element.33.q1, bf16[16,8,32,128]{3,2,1,0:T(8,128)(2,1)} %get-tuple-element.34.q2), custom_call_target="tpu_custom_call" | custom-call | tf_op jit(solution)/shard_map/total/pallas_call | solution.py:468
  141.9 0.8 slice_bitcast_fusion.3
  142.6 1.0 fusion.130
  143.7 0.8 broadcast_in_dim.44
  144.5 3.4 %all-to-all-start = ((bf16[4,4,4,16,128]{4,3,2,1,0:T(8,128)(2,1)}), bf16[4,4,4,16,128]{4,3,2,1,0:T(8,128)(2,1)S(1)}, u32[]{:S(2)}, u32[]{:S(2)}) async-start(bf16[4,4,4,16,128]{4,3,2,1,0:T(8,128)(2,1)} %broadcast_in_dim.44), calls=%async_computation | async-start | bytes 524288 | tf_op jit(solution)/shard_map/all_to_all | solution.py:46
  147.9 0.9 fusion.129
  148.8 5.8 %all-to-all-done = bf16[4,4,4,16,128]{4,3,2,1,0:T(8,128)(2,1)S(1)} async-done(((bf16[4,4,4,16,128]{4,3,2,1,0:T(8,128)(2,1)}), bf16[4,4,4,16,128]{4,3,2,1,0:T(8,128)(2,1)S(1)}, u32[]{:S(2)}, u32[]{:S(2)}) %all-to-all-start) | async-done | bytes 262176 | tf_op jit(solution)/shard_map/all_to_all | solution.py:46
  154.5 3.9 %collective-permute-start.5 = (bf16[16,4,16,128]{3,2,1,0:T(8,128)(2,1)S(1)}, bf16[16,4,16,128]{3,2,1,0:T(8,128)(2,1)S(1)}, u32[]{:S(2)}, u32[]{:S(2)}) collective-permute-start(bf16[16,4,16,128]{3,2,1,0:T(8,128)(2,1)S(1)} %bitcast.236), channel_id=1, source_target_pairs={{0,124},{4,0},{8,4},{12,8},{16,12},{20,16},{24,20},{28,24},{32,28}... | collective-permute-start | bytes 786440 | tf_op jit(solution)/shard_map/ppermute | solution.py:56
  158.5 1.0 fusion.67
  159.6 2.8 collective-permute-done.5
  162.3 5.2 %collective-permute-done.4 = bf16[16,4,16,128]{3,2,1,0:T(8,128)(2,1)S(1)} collective-permute-done((bf16[16,4,16,128]{3,2,1,0:T(8,128)(2,1)S(1)}, bf16[16,4,16,128]{3,2,1,0:T(8,128)(2,1)S(1)}, u32[]{:S(2)}, u32[]{:S(2)}) %collective-permute-start.4) | collective-permute-done | bytes 262176 | tf_op jit(solution)/shard_map/ppermute | solution.py:56
  169.5 1.9 multiply_convert_fusion.1
  171.8 9.2 %all_to_all.10 = bf16[4,4,4,16,128]{4,3,2,1,0:T(8,128)(2,1)S(1)} all-to-all(bf16[4,4,4,16,128]{4,3,2,1,0:T(8,128)(2,1)S(1)} %broadcast_in_dim.47), channel_id=1, replica_groups=mesh['lon'=32,'lat'=4] {'lat'}, dimensions={0} | all-to-all | bytes 524288 | tf_op jit(solution)/shard_map/all_to_all | solution.py:46
  181.5 0.8 fusion.126
  182.5 2.4 collective-permute-done.7
  184.9 5.2 %collective-permute-done.6 = bf16[16,4,16,128]{3,2,1,0:T(8,128)(2,1)S(1)} collective-permute-done((bf16[16,4,16,128]{3,2,1,0:T(8,128)(2,1)S(1)}, bf16[16,4,16,128]{3,2,1,0:T(8,128)(2,1)S(1)}, u32[]{:S(2)}, u32[]{:S(2)}) %collective-permute-start.6) | collective-permute-done | bytes 262176 | tf_op jit(solution)/shard_map/ppermute | solution.py:56
  191.9 0.9 fusion.1
  192.8 22.9 %plane_gather.1 = (bf16[16,8,48,128]{3,2,1,0:T(8,128)(2,1)}, bf16[16,8,48,128]{3,2,1,0:T(8,128)(2,1)}, bf16[16,8,32,128]{3,2,1,0:T(8,128)(2,1)}) custom-call(bf16[8,128,128]{2,1,0:T(8,128)(2,1)} %bitcast.242), custom_call_target="tpu_custom_call" | custom-call | tf_op jit(solution)/shard_map/plane_gather/pallas_call | solution.py:337
  215.7 8.9 %serve.1 = (bf16[8,32,48,128]{3,2,1,0:T(8,128)(2,1)}, bf16[8,32,48,128]{3,2,1,0:T(8,128)(2,1)}, bf16[8,32,32,128]{3,2,1,0:T(8,128)(2,1)}) custom-call(s32[4]{0:T(128)} %pad_add_fusion.2.spot, s32[768]{0:T(1024)} %add.360.table, bf16[16,8,48,128]{3,2,1,0:T(8,128)(2,1)} %get-tuple-element.35.u0, bf16[16,8,48,128]{3,2,1,0:T(8,128)(2,1)} %get-tuple-element.36.u1, ...), custom_call_target="tpu_custom_call" | custom-call | tf_op jit(solution)/shard_map/serve/pallas_call | solution.py:491
  224.7 39.2 %line_exchange_3.1 = (bf16[8,32,48,128]{3,2,1,0:T(8,128)(2,1)}, bf16[8,32,48,128]{3,2,1,0:T(8,128)(2,1)}, bf16[8,32,32,128]{3,2,1,0:T(8,128)(2,1)}) custom-call(bf16[8,32,48,128]{3,2,1,0:T(8,128)(2,1)} %get-tuple-element.38.s0, bf16[8,32,48,128]{3,2,1,0:T(8,128)(2,1)} %get-tuple-element.39.s1, bf16[8,32,32,128]{3,2,1,0:T(8,128)(2,1)} %get-tuple-element.40.s2), custom_call_target="tpu_custom_call" | custom-call | tf_op jit(solution)/shard_map/line_exchange_3/pallas_call | solution.py:222
  263.9 15.3 %pull.1 = bf16[128,2048]{1,0:T(8,128)(2,1)} custom-call(s32[7,128]{1,0:T(8,128)} %stack.39.table, bf16[128,128,128]{2,1,0:T(8,128)(2,1)} %blocks.3, f32[128,2048]{1,0:T(8,128)} %get-tuple-element.118.pre_conv, bf16[8,32,48,128]{3,2,1,0:T(8,128)(2,1)} %get-tuple-element.41.w0, bf16[8,32,48,128]{3,2,1,0:T(8,128)(2,1)} %get-tuple-element.42.w1, ...), custom_call_target="tpu_custom_call" | custom-call | tf_op jit(solution)/shard_map/pull/pallas_call | solution.py:554
  279.2 1.1 copy.151
  280.4 0.7 copy.120
  281.4 5.0 %collective-permute-start.9 = (bf16[128,1,128]{0,1,2:T(2,128)(2,1)S(1)}, bf16[128,1,128]{0,1,2:T(2,128)(2,1)S(1)}, u32[]{:S(2)}, u32[]{:S(2)}) collective-permute-start(bf16[128,1,128]{0,1,2:T(2,128)(2,1)S(1)} %get-tuple-element.75), channel_id=1, source_target_pairs={{4,0},{8,4},{12,8},{16,12},{20,16},{24,20},{28,24},{32,28},{36,32}... | collective-permute-start | bytes 98312 | tf_op jit(solution)/shard_map/ppermute | solution.py:31
  286.4 1.9 collective-permute-done.8
  288.8 0.6 collective-permute-start.10
  289.4 2.7 collective-permute-start.11
  292.2 1.5 collective-permute-done.10
  294.1 0.9 fusion.123
  299.1 1.3 slice.424
  (114 shorter events, 15.9 us)
Async XLA Ops:
  0.6 8.3 %copy-start = (s32[16384,1]{0,1:T(1,128)S(1)}, s32[16384,1]{0,1:T(1,128)}, u32[]{:S(2)}) copy-start(s32[16384,1]{0,1:T(1,128)} %param.13) | copy-start | bytes 196612
  0.6 8.3 %copy-start.9 = (s32[4,4,3]{1,0,2:T(4,128)S(1)}, s32[4,4,3]{1,0,2:T(4,128)}, u32[]{:S(2)}) copy-start(s32[4,4,3]{1,0,2:T(4,128)} %param.15) | copy-start | bytes 580
  0.7 11.9 %copy-start.11 = (f32[128]{0:T(128)S(1)}, f32[128]{0:T(128)}, u32[]{:S(2)}) copy-start(f32[128]{0:T(128)} %param.17) | copy-start | bytes 1540
  3.0 16.0 %copy-start.10 = (s32[128]{0:T(128)S(1)}, s32[128]{0:T(128)}, u32[]{:S(2)}) copy-start(s32[128]{0:T(128)} %param.12) | copy-start | bytes 1540
  3.0 10.1 %collective-permute-start = (bf16[222,1,128]{0,1,2:T(2,128)(2,1)S(1)}, bf16[222,1,128]{0,1,2:T(2,128)(2,1)S(1)}, u32[]{:S(2)}, u32[]{:S(2)}) collective-permute-start(bf16[222,1,128]{0,1,2:T(2,128)(2,1)S(1)} %get-tuple-element.61), channel_id=1, source_target_pairs={{0,4},{4,8},{8,12},{12,16},{16,20},{20,24},{24,28},{28,32},{32,36}... | collective-permute-start | bytes 170504 | tf_op jit(solution)/shard_map/ppermute | solution.py:29
  3.1 10.0 %collective-permute-start.1 = (bf16[222,1,128]{0,1,2:T(2,128)(2,1)S(1)}, bf16[222,1,128]{0,1,2:T(2,128)(2,1)S(1)}, u32[]{:S(2)}, u32[]{:S(2)}) collective-permute-start(bf16[222,1,128]{0,1,2:T(2,128)(2,1)S(1)} %get-tuple-element.62), channel_id=1, source_target_pairs={{4,0},{8,4},{12,8},{16,12},{20,16},{24,20},{28,24},{32,28},{36,32}... | collective-permute-start | bytes 170504 | tf_op jit(solution)/shard_map/ppermute | solution.py:31
  14.1 5.7 %collective-permute-start.2 = (bf16[222,18,1]{0,1,2:T(8,128)(2,1)S(1)}, bf16[222,18,1]{0,1,2:T(8,128)(2,1)S(1)}, u32[]{:S(2)}, u32[]{:S(2)}) collective-permute-start(bf16[222,18,1]{0,1,2:T(8,128)(2,1)S(1)} %get-tuple-element.50), channel_id=1, source_target_pairs={{0,1},{1,2},{2,3},{3,0},{4,5},{5,6},{6,7},{7,4},{8,9},{9,10},{10,1... | collective-permute-start | bytes 23984 | tf_op jit(solution)/shard_map/ppermute | solution.py:29
  15.8 4.1 %collective-permute-start.3 = (bf16[222,18,1]{0,1,2:T(8,128)(2,1)S(1)}, bf16[222,18,1]{0,1,2:T(8,128)(2,1)S(1)}, u32[]{:S(2)}, u32[]{:S(2)}) collective-permute-start(bf16[222,18,1]{0,1,2:T(8,128)(2,1)S(1)} %get-tuple-element.51), channel_id=1, source_target_pairs={{1,0},{2,1},{3,2},{0,3},{5,4},{6,5},{7,6},{4,7},{9,8},{10,9},{11,1... | collective-permute-start | bytes 23984 | tf_op jit(solution)/shard_map/ppermute | solution.py:31
  20.6 2.4 copy-start.5
  141.9 6.1 %copy-start.2 = (bf16[8,128,128]{2,1,0:T(8,128)(2,1)S(1)}, bf16[8,128,128]{2,1,0:T(8,128)(2,1)}, u32[]{:S(2)}) copy-start(bf16[8,128,128]{2,1,0:T(8,128)(2,1)} %total.1) | copy-start | bytes 786436
  141.9 16.6 %copy-start.8 = (bf16[2,128,128]{2,1,0:T(8,128)(2,1)S(1)}, bf16[2,128,128]{2,1,0:T(8,128)(2,1)}, u32[]{:S(2)}) copy-start(bf16[2,128,128]{2,1,0:T(8,128)(2,1)} %param.16) | copy-start | bytes 196612
  144.5 10.1 %all-to-all-start = ((bf16[4,4,4,16,128]{4,3,2,1,0:T(8,128)(2,1)}), bf16[4,4,4,16,128]{4,3,2,1,0:T(8,128)(2,1)S(1)}, u32[]{:S(2)}, u32[]{:S(2)}) async-start(bf16[4,4,4,16,128]{4,3,2,1,0:T(8,128)(2,1)} %broadcast_in_dim.44), calls=%async_computation | async-start | bytes 524288 | tf_op jit(solution)/shard_map/all_to_all | solution.py:46
  154.5 7.8 %collective-permute-start.5 = (bf16[16,4,16,128]{3,2,1,0:T(8,128)(2,1)S(1)}, bf16[16,4,16,128]{3,2,1,0:T(8,128)(2,1)S(1)}, u32[]{:S(2)}, u32[]{:S(2)}) collective-permute-start(bf16[16,4,16,128]{3,2,1,0:T(8,128)(2,1)S(1)} %bitcast.236), channel_id=1, source_target_pairs={{0,124},{4,0},{8,4},{12,8},{16,12},{20,16},{24,20},{28,24},{32,28}... | collective-permute-start | bytes 786440 | tf_op jit(solution)/shard_map/ppermute | solution.py:56
  158.5 9.1 %collective-permute-start.4 = (bf16[16,4,16,128]{3,2,1,0:T(8,128)(2,1)S(1)}, bf16[16,4,16,128]{3,2,1,0:T(8,128)(2,1)S(1)}, u32[]{:S(2)}, u32[]{:S(2)}) collective-permute-start(bf16[16,4,16,128]{3,2,1,0:T(8,128)(2,1)S(1)} %bitcast.237), channel_id=1, source_target_pairs={{0,4},{4,8},{8,12},{12,16},{16,20},{20,24},{24,28},{28,32},{32,36}... | collective-permute-start | bytes 786440 | tf_op jit(solution)/shard_map/ppermute | solution.py:56
  168.1 1.0 copy-start.3
  168.4 1.1 copy-start.7
  181.0 3.9 %collective-permute-start.7 = (bf16[16,4,16,128]{3,2,1,0:T(8,128)(2,1)S(1)}, bf16[16,4,16,128]{3,2,1,0:T(8,128)(2,1)S(1)}, u32[]{:S(2)}, u32[]{:S(2)}) collective-permute-start(bf16[16,4,16,128]{3,2,1,0:T(8,128)(2,1)S(1)} %bitcast.239), channel_id=1, source_target_pairs={{0,124},{4,0},{8,4},{12,8},{16,12},{20,16},{24,20},{28,24},{32,28}... | collective-permute-start | bytes 786440 | tf_op jit(solution)/shard_map/ppermute | solution.py:56
  181.0 9.1 %collective-permute-start.6 = (bf16[16,4,16,128]{3,2,1,0:T(8,128)(2,1)S(1)}, bf16[16,4,16,128]{3,2,1,0:T(8,128)(2,1)S(1)}, u32[]{:S(2)}, u32[]{:S(2)}) collective-permute-start(bf16[16,4,16,128]{3,2,1,0:T(8,128)(2,1)S(1)} %bitcast.240), channel_id=1, source_target_pairs={{0,4},{4,8},{8,12},{12,16},{16,20},{20,24},{24,28},{28,32},{32,36}... | collective-permute-start | bytes 786440 | tf_op jit(solution)/shard_map/ppermute | solution.py:56
  190.7 1.0 copy-start.4
  281.2 7.1 %collective-permute-start.8 = (bf16[128,1,128]{0,1,2:T(2,128)(2,1)S(1)}, bf16[128,1,128]{0,1,2:T(2,128)(2,1)S(1)}, u32[]{:S(2)}, u32[]{:S(2)}) collective-permute-start(bf16[128,1,128]{0,1,2:T(2,128)(2,1)S(1)} %get-tuple-element.74), channel_id=1, source_target_pairs={{0,4},{4,8},{8,12},{12,16},{16,20},{20,24},{24,28},{28,32},{32,36}... | collective-permute-start | bytes 98312 | tf_op jit(solution)/shard_map/ppermute | solution.py:29
  281.4 6.9 %collective-permute-start.9 = (bf16[128,1,128]{0,1,2:T(2,128)(2,1)S(1)}, bf16[128,1,128]{0,1,2:T(2,128)(2,1)S(1)}, u32[]{:S(2)}, u32[]{:S(2)}) collective-permute-start(bf16[128,1,128]{0,1,2:T(2,128)(2,1)S(1)} %get-tuple-element.75), channel_id=1, source_target_pairs={{4,0},{8,4},{12,8},{16,12},{20,16},{24,20},{28,24},{32,28},{36,32}... | collective-permute-start | bytes 98312 | tf_op jit(solution)/shard_map/ppermute | solution.py:31
  288.8 4.9 %collective-permute-start.10 = (bf16[128,18,1]{0,1,2:T(8,128)(2,1)S(1)}, bf16[128,18,1]{0,1,2:T(8,128)(2,1)S(1)}, u32[]{:S(2)}, u32[]{:S(2)}) collective-permute-start(bf16[128,18,1]{0,1,2:T(8,128)(2,1)S(1)} %get-tuple-element.63), channel_id=1, source_target_pairs={{0,1},{1,2},{2,3},{3,0},{4,5},{5,6},{6,7},{7,4},{8,9},{9,10},{10,1... | collective-permute-start | bytes 13832 | tf_op jit(solution)/shard_map/ppermute | solution.py:29
  289.4 4.3 %collective-permute-start.11 = (bf16[128,18,1]{0,1,2:T(8,128)(2,1)S(1)}, bf16[128,18,1]{0,1,2:T(8,128)(2,1)S(1)}, u32[]{:S(2)}, u32[]{:S(2)}) collective-permute-start(bf16[128,18,1]{0,1,2:T(8,128)(2,1)S(1)} %get-tuple-element.64), channel_id=1, source_target_pairs={{1,0},{2,1},{3,2},{0,3},{5,4},{6,5},{7,6},{4,7},{9,8},{10,9},{11,1... | collective-permute-start | bytes 13832 | tf_op jit(solution)/shard_map/ppermute | solution.py:31
  294.1 1.0 copy-start.6
  298.8 1.7 copy-start.1

commit v2 on v1

v2 whole, which is shorter than its diff:
```python
import functools

import jax
import jax.numpy as jnp
from jax import lax
from jax.experimental import pallas as pl
from jax.experimental.pallas import tpu as pltpu
from jax.sharding import PartitionSpec as P

TS = 16
RING = 4
BLOCK = 128
HALVES = 8
GROUP = 8
MESH = pl.DeviceIdType.MESH
LOG_TWO = 0.6931471805599453

PARTS = ((0, 48), (48, 48), (96, 32))
LINE = ("y", "z", "x")
PLANE = (("z", "x"), ("x", "y"), ("y", "z"))


def extended(cells, sides, width):
    for axis, dim in sides:
        count = lax.axis_size(axis)
        head = lax.slice_in_dim(cells, 0, width, axis=dim)
        tail = lax.slice_in_dim(cells, cells.shape[dim] - width, cells.shape[dim], axis=dim)
        cells = jnp.concatenate(
            [
                lax.ppermute(tail, axis, [(i, (i + 1) % count) for i in range(count)]),
                cells,
                lax.ppermute(head, axis, [((i + 1) % count, i) for i in range(count)]),
            ],
            axis=dim,
        )
    return cells


def silu_slope(values):
    sigma = jax.nn.sigmoid(values)
    return sigma * (1.0 + values * (1.0 - sigma))


def laplace_slope(latent, spread):
    magnitude = jnp.abs(latent)
    edge_mass = jnp.exp(-0.5 / spread)
    scaled = jnp.clip(latent, -0.5, 0.5) / spread
    grown, shrunk = jnp.exp(scaled), jnp.exp(-scaled)
    near_mass = 1.0 - edge_mass * (0.5 * (grown + shrunk))
    slope_near = edge_mass * (0.5 * (grown - shrunk)) / (spread * near_mass * LOG_TWO)
    side = jnp.where(latent > 0.0, 1.0, jnp.where(latent < 0.0, -1.0, 0.0))
    return jnp.where(magnitude < 0.5, slope_near, side / (spread * LOG_TWO))


def conv_taps(kernel, padded, reverse):
    lon_cells = padded.shape[1] - 2
    lat_cells = padded.shape[2] - 2
    out_rows = kernel.shape[2] if reverse else kernel.shape[1]
    result = jnp.zeros((out_rows, lon_cells * lat_cells), jnp.float32)
    for tap_index in range(9):
        lon_shift = tap_index // 3
        lat_shift = tap_index % 3
        if reverse:
            lon_shift = 2 - lon_shift
            lat_shift = 2 - lat_shift
        window = padded[
            :, lon_shift : lon_shift + lon_cells, lat_shift : lat_shift + lat_cells
        ].reshape(padded.shape[0], lon_cells * lat_cells)
        if reverse:
            result = result + lax.dot_general(
                kernel[tap_index],
                window,
                (((0,), (0,)), ((), ())),
                preferred_element_type=jnp.float32,
            )
        else:
            result = result + jnp.dot(kernel[tap_index], window, preferred_element_type=jnp.float32)
    return result


def grid_rims(values):
    padded = extended(values, (("lon", 1), ("lat", 2)), 1)
    lat_pos = lax.axis_index("lat")
    lat_last = lax.axis_size("lat") - 1
    column = lax.broadcasted_iota(jnp.int32, (1, 1, padded.shape[2]), 2)
    outside = (column == 0) & (lat_pos == 0) | (column == padded.shape[2] - 1) & (
        lat_pos == lat_last
    )
    return jnp.where(outside, jnp.zeros_like(padded), padded)


def torus_position():
    lon = lax.axis_index("lon")
    return {"z": lon // 8, "x": (lon // 2) % 4, "c": lon % 2, "y": lax.axis_index("lat")}


def moved(here, **steps):
    place = dict(here)
    for axis, step in steps.items():
        if axis == "c":
            place["c"] = (here["c"] + step) % 2
        else:
            place[axis] = (here[axis] + step + RING) % RING
    return place


def device_at(place):
    return (place["z"] * 8 + place["x"] * 2 + place["c"], place["y"])


def meet(peers):
    barrier = pltpu.get_barrier_semaphore()
    for peer in peers:
        pl.semaphore_signal(barrier, inc=1, device_id=device_at(peer), device_id_type=MESH)
    pl.semaphore_wait(barrier, len(peers))


def line_body(sign, s0, s1, s2, r0, r1, r2, send, recv, local):
    here = torus_position()
    peers = [moved(here, c=1)]
    for axis in LINE:
        for step in range(1, RING):
            for flip in range(2):
                peers.append(moved(here, **{axis: step, "c": flip}))
    meet(peers)
    sources, targets = (s0, s1, s2), (r0, r1, r2)
    copies = []
    for chunk in (4, 5, 2, 3, 6, 7, 1):
        step, flip = chunk // 2, chunk % 2
        for k in range(3):
            copy = pltpu.make_async_remote_copy(
                src_ref=sources[k].at[chunk],
                dst_ref=targets[k].at[chunk],
                send_sem=send.at[k, chunk],
                recv_sem=recv.at[k, chunk],
                device_id=device_at(moved(here, **{LINE[k]: sign * step, "c": flip})),
                device_id_type=MESH,
            )
            copy.start()
            copies.append(copy)
    own = []
    for k in range(3):
        copy = pltpu.make_async_copy(sources[k].at[0], targets[k].at[0], local.at[k])
        copy.start()
        own.append(copy)
    for copy in own + copies:
        copy.wait()


def line_exchange(parts, sign, collective_id):
    anywhere = pl.BlockSpec(memory_space=pl.ANY)
    return pl.pallas_call(
        functools.partial(line_body, sign),
        out_shape=[jax.ShapeDtypeStruct(part.shape, part.dtype) for part in parts],
        in_specs=[anywhere] * 3,
        out_specs=[anywhere] * 3,
        scratch_shapes=[
            pltpu.SemaphoreType.DMA((3, 8)),
            pltpu.SemaphoreType.DMA((3, 8)),
            pltpu.SemaphoreType.DMA((3,)),
        ],
        compiler_params=pltpu.CompilerParams(collective_id=collective_id, has_side_effects=True, vmem_limit_bytes=4 << 20),
        name="line_exchange_%d" % collective_id,
    )(*parts)


def plane_body(p0, p1, p2, q0, q1, q2, send, recv, local):
    here = torus_position()
    peers = []
    for axis in LINE:
        for step in range(1, RING):
            peers.append(moved(here, **{axis: step}))
    for first, second in PLANE:
        for step in range(1, RING):
            for other in range(1, RING):
                peers.append(moved(here, **{first: step, second: other}))
    meet(peers)
    sources, targets = (p0, p1, p2), (q0, q1, q2)
    copies = []
    for place in (10, 5, 15, 7, 13, 9, 11, 6, 14, 2, 8, 1, 3, 4, 12):
        for k in range(3):
            copy = pltpu.make_async_remote_copy(
                src_ref=sources[k].at[place],
                dst_ref=targets[k].at[place],
                send_sem=send.at[k, place],
                recv_sem=recv.at[k, place],
                device_id=device_at(
                    moved(here, **{PLANE[k][0]: place // RING, PLANE[k][1]: place % RING})
                ),
                device_id_type=MESH,
            )
            copy.start()
            copies.append(copy)
    own = []
    for k in range(3):
        copy = pltpu.make_async_copy(sources[k].at[0], targets[k].at[0], local.at[k])
        copy.start()
        own.append(copy)
    for copy in own + copies:
        copy.wait()


def plane_scatter(parts, collective_id):
    anywhere = pl.BlockSpec(memory_space=pl.ANY)
    return pl.pallas_call(
        plane_body,
        out_shape=[jax.ShapeDtypeStruct(part.shape, part.dtype) for part in parts],
        in_specs=[anywhere] * 3,
        out_specs=[anywhere] * 3,
        scratch_shapes=[
            pltpu.SemaphoreType.DMA((3, 16)),
            pltpu.SemaphoreType.DMA((3, 16)),
            pltpu.SemaphoreType.DMA((3,)),
        ],
        compiler_params=pltpu.CompilerParams(collective_id=collective_id, has_side_effects=True, vmem_limit_bytes=4 << 20),
        name="plane_scatter",
    )(*parts)


def gather_body(grad, u0, u1, u2, send, recv, local):
    here = torus_position()
    peers = []
    for axis in LINE:
        for step in range(1, RING):
            peers.append(moved(here, **{axis: step}))
    meet(peers)
    targets = (u0, u1, u2)

    def sent(k, source, place, axis, step):
        copy = pltpu.make_async_remote_copy(
            src_ref=source,
            dst_ref=targets[k].at[place],
            send_sem=send.at[k, place],
            recv_sem=recv.at[k, place],
            device_id=device_at(moved(here, **{axis: -step})),
            device_id_type=MESH,
        )
        copy.start()
        return copy

    first, later = {}, []
    mine = [grad.at[:, pl.ds(start, count)] for start, count in PARTS]
    for step in (2, 1, 3):
        for k in range(3):
            first[k, step] = sent(k, mine[k], step, PLANE[k][1], step)
    for step in (2, 1, 3):
        for k in range(3):
            later.append(sent(k, mine[k], step * RING, PLANE[k][0], step))
    own = []
    for k in range(3):
        copy = pltpu.make_async_copy(mine[k], targets[k].at[0], local.at[k])
        copy.start()
        own.append(copy)
    for step in (1, 3, 2):
        for k in range(3):
            first[k, step].wait_recv()
            for hop in (2, 1, 3):
                later.append(sent(k, targets[k].at[step], hop * RING + step, PLANE[k][0], hop))
    for copy in own + later:
        copy.wait()
    for copy in first.values():
        copy.wait_send()


def plane_gather(grad, collective_id):
    anywhere = pl.BlockSpec(memory_space=pl.ANY)
    return pl.pallas_call(
        gather_body,
        out_shape=[
            jax.ShapeDtypeStruct((16, HALVES, count, grad.shape[2]), grad.dtype)
            for _, count in PARTS
        ],
        in_specs=[anywhere],
        out_specs=[anywhere] * 3,
        scratch_shapes=[
            pltpu.SemaphoreType.DMA((3, 16)),
            pltpu.SemaphoreType.DMA((3, 16)),
            pltpu.SemaphoreType.DMA((3,)),
        ],
        compiler_params=pltpu.CompilerParams(collective_id=collective_id, has_side_effects=True, vmem_limit_bytes=4 << 20),
        name="plane_gather",
    )(grad)


def spread_body(table, hidden, blocks, o0, o1, o2, turned):
    outs = (o0, o1, o2)
    for k in range(turned.shape[0]):
        turned[k] = hidden[:, k * BLOCK : (k + 1) * BLOCK].T

    def some(step, carry):
        for b in range(GROUP):
            block = step * GROUP + b
            made = jnp.dot(
                blocks[block], turned[table[0, block]], preferred_element_type=jnp.float32
            ).astype(jnp.bfloat16)
            for k, (start, count) in enumerate(PARTS):
                outs[k][table[1 + k, block]] = made[start : start + count]
        return carry

    lax.fori_loop(0, blocks.shape[0] // GROUP, some, 0)


def spread(table, hidden, regrid_blocks):
    cells, width = regrid_blocks.shape[2], hidden.shape[0]
    vmem = pl.BlockSpec(memory_space=pltpu.VMEM)
    parts = pl.pallas_call(
        spread_body,
        in_specs=[pl.BlockSpec(memory_space=pltpu.SMEM), vmem, vmem],
        out_specs=[vmem] * 3,
        scratch_shapes=[pltpu.VMEM((hidden.shape[1] // BLOCK, cells, width), jnp.bfloat16)],
        out_shape=[jax.ShapeDtypeStruct((256, n, width), jnp.bfloat16) for _, n in PARTS],
        compiler_params=pltpu.CompilerParams(vmem_limit_bytes=24 << 20),
        name="spread",
    )(table, hidden, regrid_blocks)
    return [part.reshape(8, 32, *part.shape[1:]) for part in parts]


def combine_body(table, r0, r1, r2, p0, p1, p2, a0, a1, a2):
    place = pl.program_id(0)
    ins, outs, sums = (r0, r1, r2), (p0, p1, p2), (a0, a1, a2)
    for total in sums:
        total[...] = jnp.zeros_like(total)
    for chunk in range(8):
        for k in range(3):
            entry = k * 256 + chunk * 32 + place * 2
            for rank in range(2):
                half = table[entry + rank]
                sums[k][half] += ins[k][chunk, rank].astype(jnp.float32)
    for k in range(3):
        outs[k][0] = sums[k][:HALVES].astype(jnp.bfloat16)


def combine(table, parts):
    width = parts[0].shape[-1]
    return pl.pallas_call(
        combine_body,
        grid_spec=pltpu.PrefetchScalarGridSpec(
            num_scalar_prefetch=1,
            grid=(16,),
            in_specs=[pl.BlockSpec((8, 2, n, width), lambda i, t: (0, i, 0, 0)) for _, n in PARTS],
            out_specs=[
                pl.BlockSpec((1, HALVES, n, width), lambda i, t: (i, 0, 0, 0)) for _, n in PARTS
            ],
            scratch_shapes=[pltpu.VMEM((HALVES + 1, n, width), jnp.float32) for _, n in PARTS],
        ),
        out_shape=[jax.ShapeDtypeStruct((16, HALVES, n, width), jnp.bfloat16) for _, n in PARTS],
        compiler_params=pltpu.CompilerParams(vmem_limit_bytes=8 << 20),
        name="combine",
    )(table, *parts)


def total_body(q0, q1, q2, out):
    for (start, count), part in zip(PARTS, (q0, q1, q2)):
        out[0, start : start + count] = jnp.sum(part[:, 0].astype(jnp.float32), axis=0).astype(
            out.dtype
        )


def total(parts):
    width = parts[0].shape[-1]
    return pl.pallas_call(
        total_body,
        grid=(HALVES,),
        in_specs=[pl.BlockSpec((16, 1, n, width), lambda i: (0, i, 0, 0)) for _, n in PARTS],
        out_specs=pl.BlockSpec((1, BLOCK, width), lambda i: (i, 0, 0)),
        out_shape=jax.ShapeDtypeStruct((HALVES, BLOCK, width), jnp.bfloat16),
        compiler_params=pltpu.CompilerParams(vmem_limit_bytes=8 << 20),
        name="total",
    )(*parts)


def serve_body(table, u0, u1, u2, v0, v1, v2):
    chunk = pl.program_id(0)
    ins, outs = (u0, u1, u2), (v0, v1, v2)
    for place in range(16):
        for k in range(3):
            entry = k * 256 + chunk * 32 + place * 2
            for rank in range(2):
                half = jnp.minimum(table[entry + rank], HALVES - 1)
                outs[k][0, place * 2 + rank] = ins[k][place, half]


def serve(table, parts):
    width = parts[0].shape[-1]
    return pl.pallas_call(
        serve_body,
        grid_spec=pltpu.PrefetchScalarGridSpec(
            num_scalar_prefetch=1,
            grid=(8,),
            in_specs=[
                pl.BlockSpec((16, HALVES, n, width), lambda i, t: (0, 0, 0, 0))
                for _, n in PARTS
            ],
            out_specs=[pl.BlockSpec((1, 32, n, width), lambda i, t: (i, 0, 0, 0)) for _, n in PARTS],
        ),
        out_shape=[jax.ShapeDtypeStruct((8, 32, n, width), jnp.bfloat16) for _, n in PARTS],
        compiler_params=pltpu.CompilerParams(vmem_limit_bytes=16 << 20),
        name="serve",
    )(table, *parts)


def pull_body(table, blocks, pre_conv, w0, w1, w2, out, sums):
    ins = (w0, w1, w2)
    sums[...] = jnp.zeros_like(sums)

    def some(step, carry):
        for b in range(GROUP):
            block = step * GROUP + b
            grad = jnp.concatenate([ins[k][table[1 + k, block]] for k in range(3)], axis=0)
            sums[table[0, block]] += jnp.dot(
                grad, blocks[block], preferred_element_type=jnp.float32
            )
        return carry

    lax.fori_loop(0, blocks.shape[0] // GROUP, some, 0)
    for k in range(sums.shape[0]):
        cells = slice(k * BLOCK, (k + 1) * BLOCK)
        out[:, cells] = (sums[k] * silu_slope(pre_conv[:, cells])).astype(out.dtype)


def pull(table, regrid_blocks, pre_conv, parts):
    cells, width = regrid_blocks.shape[2], pre_conv.shape[0]
    vmem = pl.BlockSpec(memory_space=pltpu.VMEM)
    return pl.pallas_call(
        pull_body,
        in_specs=[pl.BlockSpec(memory_space=pltpu.SMEM)] + [vmem] * 5,
        out_specs=vmem,
        scratch_shapes=[pltpu.VMEM((pre_conv.shape[1] // BLOCK, width, cells), jnp.float32)],
        out_shape=jax.ShapeDtypeStruct(pre_conv.shape, jnp.bfloat16),
        compiler_params=pltpu.CompilerParams(vmem_limit_bytes=24 << 20),
        name="pull",
    )(table, regrid_blocks, pre_conv, *[part.reshape(256, *part.shape[2:]) for part in parts])


def tiles_body(beside, latent, weights, scale, codes, grad, edges, rims0, rims1, near_grad, sends, recvs):
    lon, lat = lax.axis_index("lon"), lax.axis_index("lat")
    lons, lats = lax.axis_size("lon"), lax.axis_size("lat")
    above, below = (lon + 1) % lons, (lon + lons - 1) % lons
    barrier = pltpu.get_barrier_semaphore()
    peers = []
    for step in range(lats):
        row = (lat + step) % lats
        peers += [(above, row), (below, row)] + ([(lon, row)] if step else [])
    for peer in peers:
        pl.semaphore_signal(barrier, inc=1, device_id=peer, device_id_type=MESH)

    pixels = TS * TS
    tiles = latent.shape[0] // pixels
    rims = (rims0, rims1)

    def iota(shape, dim):
        return lax.broadcasted_iota(jnp.int32, shape, dim)

    edge, cell = iota((4 * TS, pixels), 0), iota((4 * TS, pixels), 1)
    side, spot = edge >> 4, edge & 15
    wanted = jnp.where(
        side == 0,
        spot,
        jnp.where(side == 1, TS * spot + TS - 1, jnp.where(side == 2, pixels - TS + spot, TS * spot)),
    )
    take_edges = (cell == wanted).astype(jnp.float32).astype(jnp.bfloat16)
    one, other = iota((pixels, pixels), 0), iota((pixels, pixels), 1)
    apart = jnp.abs((one >> 4) - (other >> 4)) + jnp.abs((one & 15) - (other & 15))
    adjacent = (apart == 1).astype(jnp.float32).astype(jnp.bfloat16)
    cell, edge = iota((pixels, 4 * TS), 0), iota((pixels, 4 * TS), 1)
    side, spot = edge >> 4, edge & 15
    row, column = cell >> 4, cell & 15
    along = jnp.where((side & 1) == 0, column, row)
    inward = jnp.where(
        side == 0,
        row,
        jnp.where(side == 1, TS - 1 - column, jnp.where(side == 2, TS - 1 - row, column)),
    )

    def dot(a, b):
        return jnp.dot(a, b, preferred_element_type=jnp.float32)

    def dot_turned(a, b):
        return lax.dot_general(a, b, (((1,), (1,)), ((), ())), preferred_element_type=jnp.float32)

    def swap(turn, values):
        for t in range(tiles):
            picked = dot(take_edges, values[t * pixels : (t + 1) * pixels, :]).astype(jnp.bfloat16)
            for s in range(4):
                edges[turn, s, t] = picked[s * TS : (s + 1) * TS]
        mine = pl.ds(lat * tiles, tiles)
        copies = []
        for step in range(lats):
            row = (lat + step) % lats
            ways = [(2, 0, below), (0, 2, above)] + ([(1, 3, lon), (3, 1, lon)] if step else [])
            for from_side, to_side, column in ways:
                copy = pltpu.make_async_remote_copy(
                    src_ref=edges.at[turn, from_side],
                    dst_ref=rims[turn].at[to_side, mine],
                    send_sem=sends.at[turn, to_side, step],
                    recv_sem=recvs.at[turn, to_side, step],
                    device_id=(column, row),
                    device_id_type=MESH,
                )
                copy.start()
                copies.append(copy)
        rims[turn][3, mine] = edges[turn, 1]
        rims[turn][1, mine] = edges[turn, 3]
        return copies

    def around(turn, t, values):
        flips = jnp.zeros_like(edge)
        found = []
        for s in range(4):
            flips = jnp.where(side == s, beside[t * 8 + s * 2 + 1], flips)
            found.append(rims[turn][s, beside[t * 8 + s * 2]])
        hit = (inward == 0) & (spot == jnp.where(flips == 1, TS - 1 - along, along))
        place = hit.astype(jnp.float32).astype(jnp.bfloat16)
        return dot(adjacent, values[t * pixels : (t + 1) * pixels, :]) + dot(
            place, jnp.concatenate(found, axis=0)
        )

    pl.semaphore_wait(barrier, len(peers))
    copies = swap(0, latent)
    for copy in copies:
        copy.wait()
    mix_grads = []
    for t in range(tiles):
        cells = slice(t * pixels, (t + 1) * pixels)
        near_sum = around(0, t, latent).astype(jnp.bfloat16)
        pre_mix = dot(latent[cells, :], weights[0]) + dot(near_sum, weights[1])
        mixed = pre_mix * jax.nn.sigmoid(pre_mix)
        codes[cells, :] = mixed.astype(jnp.bfloat16)
        mix_grad = (laplace_slope(mixed, scale[...]) * silu_slope(pre_mix)).astype(jnp.bfloat16)
        near_grad[cells, :] = dot_turned(mix_grad, weights[1]).astype(jnp.bfloat16)
        mix_grads.append(mix_grad)
    copies = swap(1, near_grad)
    own = [dot_turned(mix_grad, weights[0]) for mix_grad in mix_grads]
    for copy in copies:
        copy.wait()
    for t in range(tiles):
        found = own[t] + around(1, t, near_grad)
        for h in range(pixels // BLOCK):
            part = found[h * BLOCK : (h + 1) * BLOCK, :]
            grad[t * (pixels // BLOCK) + h] = part.T.astype(jnp.bfloat16)


def tile_stage(latent, neighbours, hp_weight, rate_scale, collective_id):
    tiles, width = neighbours.shape[0], latent.shape[1]
    column_tiles = tiles * lax.axis_size("lat")
    beside = jnp.stack([neighbours[:, :, 0] % column_tiles, neighbours[:, :, 2]], axis=-1)
    vmem = pl.BlockSpec(memory_space=pltpu.VMEM)
    return pl.pallas_call(
        tiles_body,
        out_shape=[
            jax.ShapeDtypeStruct(latent.shape, jnp.bfloat16),
            jax.ShapeDtypeStruct((latent.shape[0] // BLOCK, width, BLOCK), jnp.bfloat16),
        ],
        in_specs=[pl.BlockSpec(memory_space=pltpu.SMEM), vmem, vmem, vmem],
        out_specs=[vmem, vmem],
        scratch_shapes=[
            pltpu.VMEM((2, 4, tiles, TS, width), jnp.bfloat16),
            pltpu.VMEM((4, column_tiles, TS, width), jnp.bfloat16),
            pltpu.VMEM((4, column_tiles, TS, width), jnp.bfloat16),
            pltpu.VMEM(latent.shape, jnp.bfloat16),
            pltpu.SemaphoreType.DMA((2, 4, 4)),
            pltpu.SemaphoreType.DMA((2, 4, 4)),
        ],
        compiler_params=pltpu.CompilerParams(collective_id=collective_id, has_side_effects=True, vmem_limit_bytes=4 << 20),
        name="tile_stage",
    )(beside.reshape(-1), latent, hp_weight, rate_scale.reshape(1, width))


def routing(source_block, target_device, target_half):
    here = torus_position()
    count = source_block.shape[0]

    def rows_of(values):
        grid = values.reshape(4, 4, 2, 4, count)
        picks = []
        for k in range(3):
            start = [here["z"], here["x"], 0, here["y"], 0]
            size = [1, 1, 2, 1, count]
            at = {"z": 0, "x": 1, "y": 3}[LINE[k]]
            start[at], size[at] = 0, 4
            picks.append(lax.dynamic_slice(grid, start, size).reshape(8, count))
        own = lax.dynamic_slice(
            grid, [here["z"], here["x"], here["c"], here["y"], 0], [1, 1, 1, 1, count]
        )
        return jnp.concatenate(picks + [own.reshape(1, count)], axis=0)

    targets = rows_of(target_device[:, 0])
    halves = rows_of(target_half)[:24]
    ids = jnp.arange(count, dtype=jnp.int32)
    rank = jnp.sum(
        (targets[:, :, None] == targets[:, None, :]) & (ids[None, None, :] < ids[None, :, None]),
        axis=2,
        dtype=jnp.int32,
    )
    to = {"z": targets // 32, "x": (targets // 8) % 4, "c": (targets // 4) % 2, "y": targets % 4}
    codes, order = [], []
    for k in range(3):
        rows = slice(8 * k, 8 * k + 8)
        fits = (to["c"][rows] == here["c"]) & (to[LINE[k]][rows] == here[LINE[k]])
        first, second = [
            (to[axis][rows] - here[axis] + RING) % RING for axis in PLANE[k]
        ]
        codes.append(jnp.where(fits, (first * RING + second) * 2 + rank[rows], -1))
        index = jnp.arange(8, dtype=jnp.int32)
        line, core = (index % RING, index // RING) if k == 0 else (index // 2, index % 2)
        order.append((here[LINE[k]] - line + RING) % RING * 2 + (core + here["c"]) % 2)
    codes = jnp.concatenate(codes, axis=0)
    slots = jnp.arange(32, dtype=jnp.int32)
    found = jnp.sum(
        jnp.where(codes[:, None, :] == slots[None, :, None], (halves - HALVES)[:, None, :], 0),
        axis=2,
    )
    chunk = jnp.arange(8, dtype=jnp.int32)
    table = HALVES + jnp.sum(
        jnp.where(
            jnp.stack(order)[:, None, :, None] == chunk[None, :, None, None],
            found.reshape(3, 1, 8, 32),
            0,
        ),
        axis=2,
    )
    own = {axis: value[24] for axis, value in to.items()}
    away = {axis: (own[axis] - here[axis] + RING) % RING for axis in ("z", "x", "y")}
    flip = (own["c"] + here["c"]) % 2
    lines = [source_block]
    for k in range(3):
        place = away[PLANE[k][0]] * RING + away[PLANE[k][1]]
        lines.append((away[LINE[k]] * 2 + flip) * 32 + place * 2 + rank[24])
    return table.reshape(-1), jnp.stack(lines)


def on_device(
    fields,
    conv_weight,
    regrid_blocks,
    source_block,
    target_device,
    target_half,
    neighbours,
    hp_weight,
    rate_scale,
):
    channels, lon_cells, lat_cells = fields.shape
    latent_width = conv_weight.shape[1]
    table, lines = routing(source_block, target_device, target_half)
    pre_conv = conv_taps(conv_weight, grid_rims(fields), False)
    hidden = jax.nn.silu(pre_conv).astype(jnp.bfloat16)
    outgoing = spread(lines, hidden, regrid_blocks)
    arrived = line_exchange(outgoing, 1, 0)
    partial = combine(table, arrived)
    latent_in = total(plane_scatter(partial, 1))
    codes, halves_grad = tile_stage(
        latent_in.reshape(-1, latent_width), neighbours, hp_weight, rate_scale, 4
    )
    replies = serve(table, plane_gather(halves_grad, 2))
    answers = line_exchange(replies, -1, 3)
    pre_grad = pull(lines, regrid_blocks, pre_conv, answers).reshape(
        latent_width, lon_cells, lat_cells
    )
    grad_fields = conv_taps(conv_weight, grid_rims(pre_grad), True).reshape(
        channels, lon_cells, lat_cells
    )
    return (codes, grad_fields)


def solution(mesh):
    placed = (
        P(None, "lon", "lat"),
        P(),
        P(("lon", "lat"), None, None),
        P(("lon", "lat")),
        P(),
        P(),
        P(("lon", "lat"), None, None),
        P(),
        P(),
    )
    return jax.shard_map(
        on_device,
        mesh=mesh,
        in_specs=placed,
        out_specs=(P(("lon", "lat"), None), P(None, "lon", "lat")),
        check_vma=False,
    )
```

time: 302 us -> 236 us (0.78)
  waiting for transfers between devices: 24.9 us -> 4.9 us
  Pallas kernels: 200 us -> 184 us
  blocking collectives: 9.2 us -> 0 us
  starting transfers between devices: 25.5 us -> 17.9 us
  matrix products: 14.2 us -> 8.03 us
  local copies, waits for them, and re-layouts: 20.2 us -> 14.5 us
    ppermute x4 -> x0, waiting for transfers between devices: 15.7 us -> none  [passed_along(): return lax.ppermute(value, axis, pairs)]
    all_to_all x1 -> x0, blocking collectives: 9.2 us -> none  [from_everyone(): lax.all_to_all(jnp.broadcast_to(x[None], (peers, *x.shape)), axis, 0, 0,...]
    pallas_call x1, Pallas kernels: 13.2 us -> 4.12 us  [combine(): pl.pallas_call(combine_body, grid_spec=pltpu.PrefetchScalarGridSpec(num_s...]
    pallas_call x1, Pallas kernels: 8.94 us -> 1.93 us  [serve(): pl.pallas_call(serve_body, grid_spec=pltpu.PrefetchScalarGridSpec(num_sca...]
    all_to_all x1 -> x0, waiting for transfers between devices: 5.77 us -> none  [from_everyone(): lax.all_to_all(jnp.broadcast_to(x[None], (peers, *x.shape)), axis, 0, 0,...]
    dot_general x8 -> x0, matrix products: 5.14 us -> none  [the longest x1 1.93 us: on_device(): jnp.dot(near_sum, hp_weight[1], preferred_element_type=jnp.float32)]
    pallas_call x1, Pallas kernels: 5.88 us -> 1.05 us  [total(): pl.pallas_call(total_body, grid=(HALVES,), in_specs=[pl.BlockSpec((16, 1,...]
    ppermute x4 -> x0, starting transfers between devices: 4.42 us -> none  [passed_along(): return lax.ppermute(value, axis, pairs)]
  transfers between devices with their start and end apart: 13 -> 8, of which waited for: 7 -> 4; matrix products, arithmetic and copies ran while one was open for 3% -> 2% of each run, Pallas kernels for 0% -> 0%
where the time goes in v2:
time: 236 us; the launch traced here: 235 us
  Pallas kernels  184 us (78%)
  starting transfers between devices  17.9 us (8%)
  local copies, waits for them, and re-layouts  14.5 us (6%)
  matrix products  8.03 us (3%)
  waiting for transfers between devices  4.9 us (2%)
  other arithmetic  4.46 us (2%)
    pallas_call x2, Pallas kernels, line_exchange(): pl.pallas_call(functools.partial(line_body, sign), out_shape=[jax.ShapeDt...  80 us
    pallas_call x1, Pallas kernels, plane_scatter(): pl.pallas_call(plane_body, out_shape=[jax.ShapeDtypeStruct(part.shape, pa...  42 us
    pallas_call x1, Pallas kernels, plane_gather(): pl.pallas_call(gather_body, out_shape=[jax.ShapeDtypeStruct((16, HALVES,...  24.1 us
    pallas_call x1, Pallas kernels, tile_stage(): pl.pallas_call(tiles_body, out_shape=[jax.ShapeDtypeStruct(latent.shape,...  22 us
    ppermute x4, starting transfers between devices, extended(): lax.ppermute(head, axis, [((i + 1) % count, i) for i in range(count)])  15.7 us
    unnamed x16, local copies, waits for them, and re-layouts  4.87 us
  transfers between devices with their start and end apart: 8, of which 4 were waited for; matrix products, arithmetic and copies ran while one was open for 2% of the time, Pallas kernels for 0%

profile of v2, /device:TPU:0, one launch (start us, length us, event | category | flops | bytes accessed | tf_op | source)
XLA Modules:
  0.0 235.3 jit_solution(17613431246554840646)
XLA Ops:
  0.6 2.1 copy.55
  3.0 5.9 %collective-permute-start.1 = (bf16[222,1,128]{0,1,2:T(2,128)(2,1)S(1)}, bf16[222,1,128]{0,1,2:T(2,128)(2,1)S(1)}, u32[]{:S(2)}, u32[]{:S(2)}) collective-permute-start(bf16[222,1,128]{0,1,2:T(2,128)(2,1)S(1)} %get-tuple-element.65), channel_id=1, source_target_pairs={{4,0},{8,4},{12,8},{16,12},{20,16},{24,20},{28,24},{32,28},{36,32}... | collective-permute-start | bytes 170504 | tf_op jit(solution)/shard_map/ppermute | solution.py:32
  8.9 0.8 constant_dynamic-slice_fusion
  9.7 0.8 constant_dynamic-slice_fusion.1
  10.4 0.7 constant_dynamic-slice_fusion.2
  11.2 0.7 fusion.79
  11.9 1.2 convert_reduce_fusion
  13.3 0.5 select_reduce_fusion
  13.9 1.0 pad_maximum_fusion
  15.0 1.6 collective-permute-start.2
  16.6 1.7 collective-permute-start.3
  18.9 1.1 collective-permute-done.2
  20.4 0.7 maximum_select_fusion
  21.0 2.6 %fusion.101 = (bf16[222,16,128]{0,2,1:T(8,128)(2,1)S(1)}, bf16[222,16,128]{0,2,1:T(8,128)(2,1)S(1)}, bf16[222,16,128]{0,2,1:T(8,128)(2,1)S(1)}, bf16[222,16,128]...) fusion(bf16[222,18,130]{0,2,1:T(8,128)(2,1)S(1)} %maximum_selec, ...), kind=kLoop, calls=%fused_computation.236 | loop fusion | bytes 16367616 | tf_op jit(solution)/shard_map/slice | solution.py:66
  23.7 0.5 fusion.19
  24.2 0.5 convolution_add_fusion.15
  24.7 0.5 convolution_add_fusion.14
  25.2 0.5 convolution_add_fusion.13
  25.7 0.5 convolution_add_fusion.12
  26.2 0.5 convolution_add_fusion.11
  26.7 0.5 convolution_add_fusion.10
  27.2 0.5 convolution_add_fusion.9
  27.7 0.5 multiply_convert_fusion
  28.2 1.6 copy-done
  29.8 4.4 %spread.1 = (bf16[256,48,128]{2,1,0:T(8,128)(2,1)S(1)}, bf16[256,48,128]{2,1,0:T(8,128)(2,1)S(1)}, bf16[256,32,128]{2,1,0:T(8,128)(2,1)S(1)}) custom-call(s32[4,128]{1,0:T(4,128)S(1)} %pad_add_fusion.4.table, bf16[128,2048]{1,0:T(8,128)(2,1)S(1)} %get-tuple-element.90.hidden, bf16[128,128,128]{2,1,0:T(8,128)(2,1)S(1)} %copy-done), custom_call_target="tpu_custom_call" | custom-call | tf_op jit(solution)/shard_map/spread/pallas_call | solution.py:306
  34.2 40.2 %line_exchange_0.1 = (bf16[8,32,48,128]{3,2,1,0:T(8,128)(2,1)S(1)}, bf16[8,32,48,128]{3,2,1,0:T(8,128)(2,1)S(1)}, bf16[8,32,32,128]{3,2,1,0:T(8,128)(2,1)S(1)}) custom-call(bf16[8,32,48,128]{3,2,1,0:T(8,128)(2,1)S(1)} %bitcast.111, bf16[8,32,48,128]{3,2,1,0:T(8,128)(2,1)S(1)} %bitcast.112, bf16[8,32,32,128]{3,2,1,0:T(8,128)(2,1)S(1)} %bitcast.115), custom_call_target="tpu_custom_call" | custom-call | tf_op jit(solution)/shard_map/line_exchange_0/pallas_call | solution.py:152
  74.5 4.1 %combine.1 = (bf16[16,8,48,128]{3,2,1,0:T(8,128)(2,1)S(1)}, bf16[16,8,48,128]{3,2,1,0:T(8,128)(2,1)S(1)}, bf16[16,8,32,128]{3,2,1,0:T(8,128)(2,1)S(1)}) custom-call(s32[768]{0:T(1024)S(1)} %add.550.table, bf16[8,32,48,128]{3,2,1,0:T(8,128)(2,1)S(1)} %get-tuple-element.28.r0, bf16[8,32,48,128]{3,2,1,0:T(8,128)(2,1)S(1)} %get-tuple-element.29.r1, ...), custom_call_target="tpu_custom_call" | custom-call | tf_op jit(solution)/shard_map/combine/pallas_call | solution.py:335
  78.6 42.0 %plane_scatter.1 = (bf16[16,8,48,128]{3,2,1,0:T(8,128)(2,1)S(1)}, bf16[16,8,48,128]{3,2,1,0:T(8,128)(2,1)S(1)}, bf16[16,8,32,128]{3,2,1,0:T(8,128)(2,1)S(1)}) custom-call(bf16[16,8,48,128]{3,2,1,0:T(8,128)(2,1)S(1)} %get-tuple-element.31.p0, bf16[16,8,48,128]{3,2,1,0:T(8,128)(2,1)S(1)} %get-tuple-element.32.p1, bf16[16,8,32,128]{3,2,1,0:T(8,128)(2,1)S(1)} %get-tuple-element.33.p2), custom_call_target="tpu_custom_call" | custom-call | tf_op jit(solution)/shard_map/plane_scatter/pallas_call | solution.py:205
  120.6 1.1 total.1
  121.7 22.0 %tile_stage.1 = (bf16[1024,128]{1,0:T(8,128)(2,1)S(1)}, bf16[8,128,128]{2,1,0:T(8,128)(2,1)S(1)}) custom-call(s32[32]{0:T(128)S(1)} %reshape.480.beside, bf16[1024,128]{1,0:T(8,128)(2,1)S(1)} %bitcast.118, bf16[2,128,128]{2,1,0:T(8,128)(2,1)S(1)} %copy-done.1, f32[1,128]{1,0:T(1,128)S(1)} %bitcast.119), custom_call_target="tpu_custom_call" | custom-call | tf_op jit(solution)/shard_map/tile_stage/pallas_call | solution.py:548
  143.7 24.1 %plane_gather.1 = (bf16[16,8,48,128]{3,2,1,0:T(8,128)(2,1)S(1)}, bf16[16,8,48,128]{3,2,1,0:T(8,128)(2,1)S(1)}, bf16[16,8,32,128]{3,2,1,0:T(8,128)(2,1)S(1)}) custom-call(bf16[8,128,128]{2,1,0:T(8,128)(2,1)S(1)} %get-tuple-element.38.grad), custom_call_target="tpu_custom_call" | custom-call | tf_op jit(solution)/shard_map/plane_gather/pallas_call | solution.py:267
  167.8 1.9 serve.1
  169.8 39.8 %line_exchange_3.1 = (bf16[8,32,48,128]{3,2,1,0:T(8,128)(2,1)S(1)}, bf16[8,32,48,128]{3,2,1,0:T(8,128)(2,1)S(1)}, bf16[8,32,32,128]{3,2,1,0:T(8,128)(2,1)S(1)}) custom-call(bf16[8,32,48,128]{3,2,1,0:T(8,128)(2,1)S(1)} %get-tuple-element.42.s0, bf16[8,32,48,128]{3,2,1,0:T(8,128)(2,1)S(1)} %get-tuple-element.43.s1, ...), custom_call_target="tpu_custom_call" | custom-call | tf_op jit(solution)/shard_map/line_exchange_3/pallas_call | solution.py:152
  209.6 4.7 %pull.1 = bf16[128,2048]{1,0:T(8,128)(2,1)S(1)} custom-call(s32[4,128]{1,0:T(4,128)S(1)} %pad_add_fusion.4.table, bf16[128,128,128]{2,1,0:T(8,128)(2,1)S(1)} %copy-done, f32[128,2048]{1,0:T(8,128)S(1)} %get-tuple-element.91.pre_conv, bf16[256,48,128]{2,1,0:T(8,128)(2,1)S(1)} %bitcast.113, bf16[256,48,128]{2,1,0:T(8,128)(2,1)S(1)} %bitcast.114, ...), custom_call_target="tpu_custom_call" | custom-call | tf_op jit(solution)/shard_map/pull/pallas_call | solution.py:424
  214.4 0.7 copy.70
  215.2 0.4 collective-permute-start.4
  215.6 4.9 %collective-permute-start.5 = (bf16[128,1,128]{0,1,2:T(2,128)(2,1)S(1)}, bf16[128,1,128]{0,1,2:T(2,128)(2,1)S(1)}, u32[]{:S(2)}, u32[]{:S(2)}) collective-permute-start(bf16[128,1,128]{0,1,2:T(2,128)(2,1)S(1)} %get-tuple-element.78), channel_id=1, source_target_pairs={{4,0},{8,4},{12,8},{16,12},{20,16},{24,20},{28,24},{32,28},{36,32}... | collective-permute-start | bytes 98312 | tf_op jit(solution)/shard_map/ppermute | solution.py:32
  220.6 1.9 collective-permute-done.4
  222.5 0.5 pad_maximum_fusion.1
  223.1 3.2 %collective-permute-start.7 = (bf16[128,18,1]{0,1,2:T(8,128)(2,1)S(1)}, bf16[128,18,1]{0,1,2:T(8,128)(2,1)S(1)}, u32[]{:S(2)}, u32[]{:S(2)}) collective-permute-start(bf16[128,18,1]{0,1,2:T(8,128)(2,1)S(1)} %get-tuple-element.67), channel_id=1, source_target_pairs={{1,0},{2,1},{3,2},{0,3},{5,4},{6,5},{7,6},{4,7},{9,8},{10,9},{11,1... | collective-permute-start | bytes 13832 | tf_op jit(solution)/shard_map/ppermute | solution.py:32
  226.4 1.5 collective-permute-done.6
  228.3 0.9 fusion.104
  229.2 0.4 fusion.17
  229.6 0.4 convolution_add_fusion.7
  230.4 0.4 convolution_add_fusion.5
  231.7 0.4 convolution_add_fusion.2
  233.2 1.3 slice.285
  234.6 0.7 copy.88
  (57 shorter events, 4.6 us)
Async XLA Ops:
  0.6 12.6 %copy-start.4 = (s32[4,4,3]{1,0,2:T(4,128)S(1)}, s32[4,4,3]{1,0,2:T(4,128)}, u32[]{:S(2)}) copy-start(s32[4,4,3]{1,0,2:T(4,128)} %param.15) | copy-start | bytes 580
  0.6 13.3 %copy-start.5 = (s32[128]{0:T(128)S(1)}, s32[128]{0:T(128)}, u32[]{:S(2)}) copy-start(s32[128]{0:T(128)} %param.12) | copy-start | bytes 1540
  2.9 11.0 %collective-permute-start = (bf16[222,1,128]{0,1,2:T(2,128)(2,1)S(1)}, bf16[222,1,128]{0,1,2:T(2,128)(2,1)S(1)}, u32[]{:S(2)}, u32[]{:S(2)}) collective-permute-start(bf16[222,1,128]{0,1,2:T(2,128)(2,1)S(1)} %get-tuple-element.64), channel_id=1, source_target_pairs={{0,4},{4,8},{8,12},{12,16},{16,20},{20,24},{24,28},{28,32},{32,36}... | collective-permute-start | bytes 170504 | tf_op jit(solution)/shard_map/ppermute | solution.py:30
  3.0 10.9 %collective-permute-start.1 = (bf16[222,1,128]{0,1,2:T(2,128)(2,1)S(1)}, bf16[222,1,128]{0,1,2:T(2,128)(2,1)S(1)}, u32[]{:S(2)}, u32[]{:S(2)}) collective-permute-start(bf16[222,1,128]{0,1,2:T(2,128)(2,1)S(1)} %get-tuple-element.65), channel_id=1, source_target_pairs={{4,0},{8,4},{12,8},{16,12},{20,16},{24,20},{28,24},{32,28},{36,32}... | collective-permute-start | bytes 170504 | tf_op jit(solution)/shard_map/ppermute | solution.py:32
  15.0 5.0 %collective-permute-start.2 = (bf16[222,18,1]{0,1,2:T(8,128)(2,1)S(1)}, bf16[222,18,1]{0,1,2:T(8,128)(2,1)S(1)}, u32[]{:S(2)}, u32[]{:S(2)}) collective-permute-start(bf16[222,18,1]{0,1,2:T(8,128)(2,1)S(1)} %get-tuple-element.53), channel_id=1, source_target_pairs={{0,1},{1,2},{2,3},{3,0},{4,5},{5,6},{6,7},{7,4},{8,9},{9,10},{10,1... | collective-permute-start | bytes 23984 | tf_op jit(solution)/shard_map/ppermute | solution.py:30
  16.6 3.7 %collective-permute-start.3 = (bf16[222,18,1]{0,1,2:T(8,128)(2,1)S(1)}, bf16[222,18,1]{0,1,2:T(8,128)(2,1)S(1)}, u32[]{:S(2)}, u32[]{:S(2)}) collective-permute-start(bf16[222,18,1]{0,1,2:T(8,128)(2,1)S(1)} %get-tuple-element.54), channel_id=1, source_target_pairs={{1,0},{2,1},{3,2},{0,3},{5,4},{6,5},{7,6},{4,7},{9,8},{10,9},{11,1... | collective-permute-start | bytes 23984 | tf_op jit(solution)/shard_map/ppermute | solution.py:32
  21.0 2.7 %copy-start.3 = (bf16[9,128,222]{1,2,0:T(8,128)(2,1)S(1)}, bf16[9,128,222]{1,2,0:T(8,128)(2,1)}, u32[]{:S(2)}) copy-start(bf16[9,128,222]{1,2,0:T(8,128)(2,1)} %param.10) | copy-start | bytes 1534468
  27.7 2.2 copy-start
  120.6 1.1 copy-start.1
  120.6 1.1 copy-start.2
  215.2 7.3 %collective-permute-start.4 = (bf16[128,1,128]{0,1,2:T(2,128)(2,1)S(1)}, bf16[128,1,128]{0,1,2:T(2,128)(2,1)S(1)}, u32[]{:S(2)}, u32[]{:S(2)}) collective-permute-start(bf16[128,1,128]{0,1,2:T(2,128)(2,1)S(1)} %get-tuple-element.77), channel_id=1, source_target_pairs={{0,4},{4,8},{8,12},{12,16},{16,20},{20,24},{24,28},{28,32},{32,36}... | collective-permute-start | bytes 98312 | tf_op jit(solution)/shard_map/ppermute | solution.py:30
  215.6 6.9 %collective-permute-start.5 = (bf16[128,1,128]{0,1,2:T(2,128)(2,1)S(1)}, bf16[128,1,128]{0,1,2:T(2,128)(2,1)S(1)}, u32[]{:S(2)}, u32[]{:S(2)}) collective-permute-start(bf16[128,1,128]{0,1,2:T(2,128)(2,1)S(1)} %get-tuple-element.78), channel_id=1, source_target_pairs={{4,0},{8,4},{12,8},{16,12},{20,16},{24,20},{28,24},{32,28},{36,32}... | collective-permute-start | bytes 98312 | tf_op jit(solution)/shard_map/ppermute | solution.py:32
  223.0 4.9 %collective-permute-start.6 = (bf16[128,18,1]{0,1,2:T(8,128)(2,1)S(1)}, bf16[128,18,1]{0,1,2:T(8,128)(2,1)S(1)}, u32[]{:S(2)}, u32[]{:S(2)}) collective-permute-start(bf16[128,18,1]{0,1,2:T(8,128)(2,1)S(1)} %get-tuple-element.66), channel_id=1, source_target_pairs={{0,1},{1,2},{2,3},{3,0},{4,5},{5,6},{6,7},{7,4},{8,9},{9,10},{10,1... | collective-permute-start | bytes 13832 | tf_op jit(solution)/shard_map/ppermute | solution.py:30
  223.1 4.8 %collective-permute-start.7 = (bf16[128,18,1]{0,1,2:T(8,128)(2,1)S(1)}, bf16[128,18,1]{0,1,2:T(8,128)(2,1)S(1)}, u32[]{:S(2)}, u32[]{:S(2)}) collective-permute-start(bf16[128,18,1]{0,1,2:T(8,128)(2,1)S(1)} %get-tuple-element.67), channel_id=1, source_target_pairs={{1,0},{2,1},{3,2},{0,3},{5,4},{6,5},{7,6},{4,7},{9,8},{10,9},{11,1... | collective-permute-start | bytes 13832 | tf_op jit(solution)/shard_map/ppermute | solution.py:32

commit v3 on v2

--- a/solution.py
+++ b/solution.py
@@ -42,14 +42,14 @@
 
 
 def laplace_slope(latent, spread):
-    magnitude = jnp.abs(latent)
-    edge_mass = jnp.exp(-0.5 / spread)
-    scaled = jnp.clip(latent, -0.5, 0.5) / spread
+    inverse = 1.0 / spread
+    half_mass = 0.5 * jnp.exp(-0.5 * inverse)
+    far = inverse * (1.0 / LOG_TWO)
+    scaled = jnp.clip(latent, -0.5, 0.5) * inverse
     grown, shrunk = jnp.exp(scaled), jnp.exp(-scaled)
-    near_mass = 1.0 - edge_mass * (0.5 * (grown + shrunk))
-    slope_near = edge_mass * (0.5 * (grown - shrunk)) / (spread * near_mass * LOG_TWO)
-    side = jnp.where(latent > 0.0, 1.0, jnp.where(latent < 0.0, -1.0, 0.0))
-    return jnp.where(magnitude < 0.5, slope_near, side / (spread * LOG_TWO))
+    slope_near = (half_mass * far) * (grown - shrunk) / (1.0 - half_mass * (grown + shrunk))
+    slope_far = jnp.where(latent > 0.0, far, -far)
+    return jnp.where(jnp.abs(latent) < 0.5, slope_near, slope_far)
 
 
 def conv_taps(kernel, padded, reverse):
@@ -164,124 +164,6 @@
     )(*parts)
 
 
-def plane_body(p0, p1, p2, q0, q1, q2, send, recv, local):
-    here = torus_position()
-    peers = []
-    for axis in LINE:
-        for step in range(1, RING):
-            peers.append(moved(here, **{axis: step}))
-    for first, second in PLANE:
-        for step in range(1, RING):
-            for other in range(1, RING):
-                peers.append(moved(here, **{first: step, second: other}))
-    meet(peers)
-    sources, targets = (p0, p1, p2), (q0, q1, q2)
-    copies = []
-    for place in (10, 5, 15, 7, 13, 9, 11, 6, 14, 2, 8, 1, 3, 4, 12):
-        for k in range(3):
-            copy = pltpu.make_async_remote_copy(
-                src_ref=sources[k].at[place],
-                dst_ref=targets[k].at[place],
-                send_sem=send.at[k, place],
-                recv_sem=recv.at[k, place],
-                device_id=device_at(
-                    moved(here, **{PLANE[k][0]: place // RING, PLANE[k][1]: place % RING})
-                ),
-                device_id_type=MESH,
-            )
-            copy.start()
-            copies.append(copy)
-    own = []
-    for k in range(3):
-        copy = pltpu.make_async_copy(sources[k].at[0], targets[k].at[0], local.at[k])
-        copy.start()
-        own.append(copy)
-    for copy in own + copies:
-        copy.wait()
-
-
-def plane_scatter(parts, collective_id):
-    anywhere = pl.BlockSpec(memory_space=pl.ANY)
-    return pl.pallas_call(
-        plane_body,
-        out_shape=[jax.ShapeDtypeStruct(part.shape, part.dtype) for part in parts],
-        in_specs=[anywhere] * 3,
-        out_specs=[anywhere] * 3,
-        scratch_shapes=[
-            pltpu.SemaphoreType.DMA((3, 16)),
-            pltpu.SemaphoreType.DMA((3, 16)),
-            pltpu.SemaphoreType.DMA((3,)),
-        ],
-        compiler_params=pltpu.CompilerParams(collective_id=collective_id, has_side_effects=True, vmem_limit_bytes=4 << 20),
-        name="plane_scatter",
-    )(*parts)
-
-
-def gather_body(grad, u0, u1, u2, send, recv, local):
-    here = torus_position()
-    peers = []
-    for axis in LINE:
-        for step in range(1, RING):
-            peers.append(moved(here, **{axis: step}))
-    meet(peers)
-    targets = (u0, u1, u2)
-
-    def sent(k, source, place, axis, step):
-        copy = pltpu.make_async_remote_copy(
-            src_ref=source,
-            dst_ref=targets[k].at[place],
-            send_sem=send.at[k, place],
-            recv_sem=recv.at[k, place],
-            device_id=device_at(moved(here, **{axis: -step})),
-            device_id_type=MESH,
-        )
-        copy.start()
-        return copy
-
-    first, later = {}, []
-    mine = [grad.at[:, pl.ds(start, count)] for start, count in PARTS]
-    for step in (2, 1, 3):
-        for k in range(3):
-            first[k, step] = sent(k, mine[k], step, PLANE[k][1], step)
-    for step in (2, 1, 3):
-        for k in range(3):
-            later.append(sent(k, mine[k], step * RING, PLANE[k][0], step))
-    own = []
-    for k in range(3):
-        copy = pltpu.make_async_copy(mine[k], targets[k].at[0], local.at[k])
-        copy.start()
-        own.append(copy)
-    for step in (1, 3, 2):
-        for k in range(3):
-            first[k, step].wait_recv()
-            for hop in (2, 1, 3):
-                later.append(sent(k, targets[k].at[step], hop * RING + step, PLANE[k][0], hop))
-    for copy in own + later:
-        copy.wait()
-    for copy in first.values():
-        copy.wait_send()
-
-
-def plane_gather(grad, collective_id):
-    anywhere = pl.BlockSpec(memory_space=pl.ANY)
-    return pl.pallas_call(
-        gather_body,
-        out_shape=[
-            jax.ShapeDtypeStruct((16, HALVES, count, grad.shape[2]), grad.dtype)
-            for _, count in PARTS
-        ],
-        in_specs=[anywhere],
-        out_specs=[anywhere] * 3,
-        scratch_shapes=[
-            pltpu.SemaphoreType.DMA((3, 16)),
-            pltpu.SemaphoreType.DMA((3, 16)),
-            pltpu.SemaphoreType.DMA((3,)),
-        ],
-        compiler_params=pltpu.CompilerParams(collective_id=collective_id, has_side_effects=True, vmem_limit_bytes=4 << 20),
-        name="plane_gather",
-    )(grad)
-
-
 def spread_body(table, hidden, blocks, o0, o1, o2, turned):
     outs = (o0, o1, o2)
     for k in range(turned.shape[0]):
@@ -349,56 +231,6 @@
     )(table, *parts)
 
 
-def total_body(q0, q1, q2, out):
-    for (start, count), part in zip(PARTS, (q0, q1, q2)):
-        out[0, start : start + count] = jnp.sum(part[:, 0].astype(jnp.float32), axis=0).astype(
-            out.dtype
-        )
-
-
-def total(parts):
-    width = parts[0].shape[-1]
-    return pl.pallas_call(
-        total_body,
-        grid=(HALVES,),
-        in_specs=[pl.BlockSpec((16, 1, n, width), lambda i: (0, i, 0, 0)) for _, n in PARTS],
-        out_specs=pl.BlockSpec((1, BLOCK, width), lambda i: (i, 0, 0)),
-        out_shape=jax.ShapeDtypeStruct((HALVES, BLOCK, width), jnp.bfloat16),
-        compiler_params=pltpu.CompilerParams(vmem_limit_bytes=8 << 20),
-        name="total",
-    )(*parts)
-
-
-def serve_body(table, u0, u1, u2, v0, v1, v2):
-    chunk = pl.program_id(0)
-    ins, outs = (u0, u1, u2), (v0, v1, v2)
-    for place in range(16):
-        for k in range(3):
-            entry = k * 256 + chunk * 32 + place * 2
-            for rank in range(2):
-                half = jnp.minimum(table[entry + rank], HALVES - 1)
-                outs[k][0, place * 2 + rank] = ins[k][place, half]
-
-
-def serve(table, parts):
-    width = parts[0].shape[-1]
-    return pl.pallas_call(
-        serve_body,
-        grid_spec=pltpu.PrefetchScalarGridSpec(
-            num_scalar_prefetch=1,
-            grid=(8,),
-            in_specs=[
-                pl.BlockSpec((16, HALVES, n, width), lambda i, t: (0, 0, 0, 0))
-                for _, n in PARTS
-            ],
-            out_specs=[pl.BlockSpec((1, 32, n, width), lambda i, t: (i, 0, 0, 0)) for _, n in PARTS],
-        ),
-        out_shape=[jax.ShapeDtypeStruct((8, 32, n, width), jnp.bfloat16) for _, n in PARTS],
-        compiler_params=pltpu.CompilerParams(vmem_limit_bytes=16 << 20),
-        name="serve",
-    )(table, *parts)
-
-
 def pull_body(table, blocks, pre_conv, w0, w1, w2, out, sums):
     ins = (w0, w1, w2)
     sums[...] = jnp.zeros_like(sums)
@@ -432,25 +264,32 @@
     )(table, regrid_blocks, pre_conv, *[part.reshape(256, *part.shape[2:]) for part in parts])
 
 
-def tiles_body(beside, latent, weights, scale, codes, grad, edges, rims0, rims1, near_grad, sends, recvs):
-    lon, lat = lax.axis_index("lon"), lax.axis_index("lat")
-    lons, lats = lax.axis_size("lon"), lax.axis_size("lat")
-    above, below = (lon + 1) % lons, (lon + lons - 1) % lons
-    barrier = pltpu.get_barrier_semaphore()
-    peers = []
-    for step in range(lats):
-        row = (lat + step) % lats
-        peers += [(above, row), (below, row)] + ([(lon, row)] if step else [])
-    for peer in peers:
-        pl.semaphore_signal(barrier, inc=1, device_id=peer, device_id_type=MESH)
-
-    pixels = TS * TS
-    tiles = latent.shape[0] // pixels
-    rims = (rims0, rims1)
-
-    def iota(shape, dim):
-        return lax.broadcasted_iota(jnp.int32, shape, dim)
-
+def remote(source, target, send, recv, place):
+    copy = pltpu.make_async_remote_copy(
+        src_ref=source,
+        dst_ref=target,
+        send_sem=send,
+        recv_sem=recv,
+        device_id=place,
+        device_id_type=MESH,
+    )
+    copy.start()
+    return copy
+
+
+def iota(shape, dim):
+    return lax.broadcasted_iota(jnp.int32, shape, dim)
+
+
+def dot(a, b):
+    return jnp.dot(a, b, preferred_element_type=jnp.float32)
+
+
+def dot_turned(a, b):
+    return lax.dot_general(a, b, (((1,), (1,)), ((), ())), preferred_element_type=jnp.float32)
+
+
+def edge_masks(pixels):
     edge, cell = iota((4 * TS, pixels), 0), iota((4 * TS, pixels), 1)
     side, spot = edge >> 4, edge & 15
     wanted = jnp.where(
@@ -471,99 +310,251 @@
         row,
         jnp.where(side == 1, TS - 1 - column, jnp.where(side == 2, TS - 1 - row, column)),
     )
-
-    def dot(a, b):
-        return jnp.dot(a, b, preferred_element_type=jnp.float32)
-
-    def dot_turned(a, b):
-        return lax.dot_general(a, b, (((1,), (1,)), ((), ())), preferred_element_type=jnp.float32)
+    return take_edges, adjacent, side, spot, along, inward
+
+
+def middle_body(
+    table, beside, p0, p1, p2, weights, scale, codes, w0, w1, w2,
+    a0, a1, a2, b0, b1, b2, c0, c1, c2, latent, grad, edges, rims0, rims1, near_grad,
+    u0, u1, u2, v0, v1, v2, first_sems, second_sems, edge_sems, gather_sems, line_sems,
+):
+    ps, ws, arrived, sums, landed = (p0, p1, p2), (w0, w1, w2), (a0, a1, a2), (b0, b1, b2), (c0, c1, c2)
+    us, vs, rims = (u0, u1, u2), (v0, v1, v2), (rims0, rims1)
+    here = torus_position()
+    lon, lat = lax.axis_index("lon"), lax.axis_index("lat")
+    lons, lats = lax.axis_size("lon"), lax.axis_size("lat")
+    above, below = (lon + 1) % lons, (lon + lons - 1) % lons
+    pixels = TS * TS
+    per_tile = pixels // BLOCK
+    tiles = latent.shape[0] // per_tile
+    columns = [(k, start, count) for k, (start, count) in enumerate(PARTS)]
+
+    barrier = pltpu.get_barrier_semaphore()
+    peers = [device_at(moved(here, c=1))]
+    for axis in LINE:
+        for step in range(1, RING):
+            for flip in range(2):
+                peers.append(device_at(moved(here, **{axis: step, "c": flip})))
+    for step in range(lats):
+        row = (lat + step) % lats
+        peers += [(above, row), (below, row)]
+    for peer in peers:
+        pl.semaphore_signal(barrier, inc=1, device_id=peer, device_id_type=MESH)
+    pl.semaphore_wait(barrier, len(peers))
+
+    copies = {}
+    for step in (2, 1, 3):
+        for k in range(3):
+            copies[k, step] = remote(
+                ps[k].at[:, step],
+                arrived[k].at[step],
+                first_sems.at[0, k, step],
+                first_sems.at[1, k, step],
+                device_at(moved(here, **{PLANE[k][1]: step})),
+            )
+    take_edges, adjacent, side, spot, along, inward = edge_masks(pixels)
+    for copy in copies.values():
+        copy.wait()
+    copies = []
+    for step in (2, 1, 3, 0):
+        for k in range(3):
+            total = ps[k][step, 0].astype(jnp.float32)
+            for other in range(1, RING):
+                total += arrived[k][other, step].astype(jnp.float32)
+            sums[k][step] = total.astype(jnp.bfloat16)
+            if step:
+                copies.append(
+                    remote(
+                        sums[k].at[step],
+                        landed[k].at[step],
+                        second_sems.at[0, k, step],
+                        second_sems.at[1, k, step],
+                        device_at(moved(here, **{PLANE[k][0]: step})),
+                    )
+                )
+    for copy in copies:
+        copy.wait()
+    for k, start, count in columns:
+        total = sums[k][0].astype(jnp.float32)
+        for step in range(1, RING):
+            total += landed[k][step].astype(jnp.float32)
+        latent[:, start : start + count] = total.astype(jnp.bfloat16)
+
+    def tile_of(values, t):
+        return values[t * per_tile : (t + 1) * per_tile].reshape(pixels, values.shape[2])
 
     def swap(turn, values):
         for t in range(tiles):
-            picked = dot(take_edges, values[t * pixels : (t + 1) * pixels, :]).astype(jnp.bfloat16)
+            picked = dot(take_edges, tile_of(values, t)).astype(jnp.bfloat16)
             for s in range(4):
                 edges[turn, s, t] = picked[s * TS : (s + 1) * TS]
         mine = pl.ds(lat * tiles, tiles)
-        copies = []
-        for step in range(lats):
+        sent = []
+        for step in (2, 1, 3, 0):
             row = (lat + step) % lats
             ways = [(2, 0, below), (0, 2, above)] + ([(1, 3, lon), (3, 1, lon)] if step else [])
             for from_side, to_side, column in ways:
-                copy = pltpu.make_async_remote_copy(
-                    src_ref=edges.at[turn, from_side],
-                    dst_ref=rims[turn].at[to_side, mine],
-                    send_sem=sends.at[turn, to_side, step],
-                    recv_sem=recvs.at[turn, to_side, step],
-                    device_id=(column, row),
-                    device_id_type=MESH,
+                sent.append(
+                    remote(
+                        edges.at[turn, from_side],
+                        rims[turn].at[to_side, mine],
+                        edge_sems.at[0, turn, to_side, step],
+                        edge_sems.at[1, turn, to_side, step],
+                        (column, row),
+                    )
                 )
-                copy.start()
-                copies.append(copy)
         rims[turn][3, mine] = edges[turn, 1]
         rims[turn][1, mine] = edges[turn, 3]
-        return copies
-
-    def around(turn, t, values):
-        flips = jnp.zeros_like(edge)
-        found = []
+        return sent
+
+    def placed(t):
+        flips = jnp.zeros_like(side)
         for s in range(4):
             flips = jnp.where(side == s, beside[t * 8 + s * 2 + 1], flips)
-            found.append(rims[turn][s, beside[t * 8 + s * 2]])
         hit = (inward == 0) & (spot == jnp.where(flips == 1, TS - 1 - along, along))
-        place = hit.astype(jnp.float32).astype(jnp.bfloat16)
-        return dot(adjacent, values[t * pixels : (t + 1) * pixels, :]) + dot(
-            place, jnp.concatenate(found, axis=0)
-        )
-
-    pl.semaphore_wait(barrier, len(peers))
+        return hit.astype(jnp.float32).astype(jnp.bfloat16)
+
+    def outer(turn, t, place):
+        found = [rims[turn][s, beside[t * 8 + s * 2]] for s in range(4)]
+        return dot(place, jnp.concatenate(found, axis=0))
+
     copies = swap(0, latent)
+    places = [placed(t) for t in range(tiles)]
+    inner = [dot(adjacent, tile_of(latent, t)) for t in range(tiles)]
+    mixes = [dot(tile_of(latent, t), weights[0]) for t in range(tiles)]
     for copy in copies:
         copy.wait()
     mix_grads = []
     for t in range(tiles):
-        cells = slice(t * pixels, (t + 1) * pixels)
-        near_sum = around(0, t, latent).astype(jnp.bfloat16)
-        pre_mix = dot(latent[cells, :], weights[0]) + dot(near_sum, weights[1])
+        near_sum = (inner[t] + outer(0, t, places[t])).astype(jnp.bfloat16)
+        pre_mix = mixes[t] + dot(near_sum, weights[1])
         mixed = pre_mix * jax.nn.sigmoid(pre_mix)
-        codes[cells, :] = mixed.astype(jnp.bfloat16)
+        codes[t * pixels : (t + 1) * pixels, :] = mixed.astype(jnp.bfloat16)
         mix_grad = (laplace_slope(mixed, scale[...]) * silu_slope(pre_mix)).astype(jnp.bfloat16)
-        near_grad[cells, :] = dot_turned(mix_grad, weights[1]).astype(jnp.bfloat16)
+        made = dot_turned(mix_grad, weights[1]).astype(jnp.bfloat16)
+        near_grad[t * per_tile : (t + 1) * per_tile] = made.reshape(per_tile, BLOCK, -1)
         mix_grads.append(mix_grad)
     copies = swap(1, near_grad)
-    own = [dot_turned(mix_grad, weights[0]) for mix_grad in mix_grads]
+    own = [
+        dot_turned(mix_grads[t], weights[0]) + dot(adjacent, tile_of(near_grad, t))
+        for t in range(tiles)
+    ]
     for copy in copies:
         copy.wait()
     for t in range(tiles):
-        found = own[t] + around(1, t, near_grad)
-        for h in range(pixels // BLOCK):
+        found = own[t] + outer(1, t, places[t])
+        for h in range(per_tile):
             part = found[h * BLOCK : (h + 1) * BLOCK, :]
-            grad[t * (pixels // BLOCK) + h] = part.T.astype(jnp.bfloat16)
-
-
-def tile_stage(latent, neighbours, hp_weight, rate_scale, collective_id):
-    tiles, width = neighbours.shape[0], latent.shape[1]
+            grad[t * per_tile + h] = part.T.astype(jnp.bfloat16)
+
+    def gathered(k, source, place, axis, step):
+        return remote(
+            source,
+            us[k].at[place],
+            gather_sems.at[0, k, place],
+            gather_sems.at[1, k, place],
+            device_at(moved(here, **{axis: -step})),
+        )
+
+    first, later = {}, []
+    mine = [grad.at[:, pl.ds(start, count)] for start, count in PARTS]
+    for step in (2, 1, 3):
+        for k in range(3):
+            first[k, step] = gathered(k, mine[k], step, PLANE[k][1], step)
+    for step in (2, 1, 3):
+        for k in range(3):
+            later.append(gathered(k, mine[k], step * RING, PLANE[k][0], step))
+    for k, start, count in columns:
+        us[k][0] = grad[:, start : start + count]
+    for step in (1, 3, 2):
+        for k in range(3):
+            first[k, step].wait_recv()
+            for hop in (2, 1, 3):
+                later.append(gathered(k, us[k].at[step], hop * RING + step, PLANE[k][0], hop))
+    for copy in later:
+        copy.wait()
+    for copy in first.values():
+        copy.wait_send()
+
+    copies = []
+    for chunk in (4, 5, 2, 3, 6, 7, 1, 0):
+        step, flip = chunk // 2, chunk % 2
+
+        def fill(place, carry):
+            for k in range(3):
+                for rank in range(2):
+                    half = jnp.minimum(table[k * 256 + chunk * 32 + place * 2 + rank], HALVES - 1)
+                    found = us[k][place, half]
+                    if chunk:
+                        vs[k][chunk - 1, place * 2 + rank] = found
+                    else:
+                        ws[k][0, place * 2 + rank] = found
+            return carry
+
+        lax.fori_loop(0, RING * RING, fill, 0)
+        if chunk:
+            for k in range(3):
+                copies.append(
+                    remote(
+                        vs[k].at[chunk - 1],
+                        ws[k].at[chunk],
+                        line_sems.at[0, k, chunk],
+                        line_sems.at[1, k, chunk],
+                        device_at(moved(here, **{LINE[k]: -step, "c": flip})),
+                    )
+                )
+    for copy in copies:
+        copy.wait()
+
+
+def middle(table, neighbours, parts, hp_weight, rate_scale, collective_id):
+    tiles, width = neighbours.shape[0], hp_weight.shape[1]
     column_tiles = tiles * lax.axis_size("lat")
+    pixels = tiles * TS * TS
     beside = jnp.stack([neighbours[:, :, 0] % column_tiles, neighbours[:, :, 2]], axis=-1)
-    vmem = pl.BlockSpec(memory_space=pltpu.VMEM)
+    smem, vmem = pl.BlockSpec(memory_space=pltpu.SMEM), pl.BlockSpec(memory_space=pltpu.VMEM)
+    counts = [count for _, count in PARTS]
+
+    def buffers(*lead):
+        return [pltpu.VMEM((*lead, n, width), jnp.bfloat16) for n in counts]
+
     return pl.pallas_call(
-        tiles_body,
-        out_shape=[
-            jax.ShapeDtypeStruct(latent.shape, jnp.bfloat16),
-            jax.ShapeDtypeStruct((latent.shape[0] // BLOCK, width, BLOCK), jnp.bfloat16),
-        ],
-        in_specs=[pl.BlockSpec(memory_space=pltpu.SMEM), vmem, vmem, vmem],
-        out_specs=[vmem, vmem],
-        scratch_shapes=[
+        middle_body,
+        out_shape=[jax.ShapeDtypeStruct((pixels, width), jnp.bfloat16)]
+        + [jax.ShapeDtypeStruct((8, 32, n, width), jnp.bfloat16) for n in counts],
+        in_specs=[smem, smem] + [vmem] * 5,
+        out_specs=[vmem] * 4,
+        scratch_shapes=buffers(RING, RING, HALVES)
+        + buffers(RING, HALVES)
+        + buffers(RING, HALVES)
+        + [
+            pltpu.VMEM((HALVES, BLOCK, width), jnp.bfloat16),
+            pltpu.VMEM((HALVES, width, BLOCK), jnp.bfloat16),
             pltpu.VMEM((2, 4, tiles, TS, width), jnp.bfloat16),
             pltpu.VMEM((4, column_tiles, TS, width), jnp.bfloat16),
             pltpu.VMEM((4, column_tiles, TS, width), jnp.bfloat16),
-            pltpu.VMEM(latent.shape, jnp.bfloat16),
-            pltpu.SemaphoreType.DMA((2, 4, 4)),
-            pltpu.SemaphoreType.DMA((2, 4, 4)),
+            pltpu.VMEM((HALVES, BLOCK, width), jnp.bfloat16),
+        ]
+        + buffers(RING * RING, HALVES)
+        + buffers(7, 32)
+        + [
+            pltpu.SemaphoreType.DMA((2, 3, RING)),
+            pltpu.SemaphoreType.DMA((2, 3, RING)),
+            pltpu.SemaphoreType.DMA((2, 2, 4, 4)),
+            pltpu.SemaphoreType.DMA((2, 3, RING * RING)),
+            pltpu.SemaphoreType.DMA((2, 3, 8)),
         ],
-        compiler_params=pltpu.CompilerParams(collective_id=collective_id, has_side_effects=True, vmem_limit_bytes=4 << 20),
-        name="tile_stage",
-    )(beside.reshape(-1), latent, hp_weight, rate_scale.reshape(1, width))
+        compiler_params=pltpu.CompilerParams(
+            collective_id=collective_id, has_side_effects=True, vmem_limit_bytes=36 << 20
+        ),
+        name="middle",
+    )(
+        table,
+        beside.reshape(-1),
+        *[part.reshape(RING, RING, *part.shape[1:]) for part in parts],
+        hp_weight,
+        rate_scale.reshape(1, width),
+    )
 
 
 def routing(source_block, target_device, target_half):
@@ -648,12 +639,7 @@
     outgoing = spread(lines, hidden, regrid_blocks)
     arrived = line_exchange(outgoing, 1, 0)
     partial = combine(table, arrived)
-    latent_in = total(plane_scatter(partial, 1))
-    codes, halves_grad = tile_stage(
-        latent_in.reshape(-1, latent_width), neighbours, hp_weight, rate_scale, 4
-    )
-    replies = serve(table, plane_gather(halves_grad, 2))
-    answers = line_exchange(replies, -1, 3)
+    codes, *answers = middle(table, neighbours, partial, hp_weight, rate_scale, 1)
     pre_grad = pull(lines, regrid_blocks, pre_conv, answers).reshape(
         latent_width, lon_cells, lat_cells
     )

time: 236 us -> 209 us (0.89)
  Pallas kernels: 184 us -> 158 us
    pallas_call x2 -> x1, Pallas kernels: 80 us -> 40.2 us  [line_exchange(): pl.pallas_call(functools.partial(line_body, sign), out_shape=[jax.ShapeDt...]
    pallas_call x5 -> x1, Pallas kernels: 91.1 us -> 104 us  [middle(): pl.pallas_call(middle_body, out_shape=[jax.ShapeDtypeStruct((pixels, widt...]
  transfers between devices with their start and end apart: 8 -> 8, of which waited for: 4 -> 4; matrix products, arithmetic and copies ran while one was open for 2% -> 3% of each run, Pallas kernels for 0% -> 0%
where the time goes in v3:
time: 209 us; the launch traced here: 208 us
  Pallas kernels  158 us (76%)
  starting transfers between devices  17.7 us (8%)
  local copies, waits for them, and re-layouts  14.4 us (7%)
  matrix products  8.03 us (4%)
  waiting for transfers between devices  4.9 us (2%)
  other arithmetic  4.46 us (2%)
    pallas_call x1, Pallas kernels, middle(): pl.pallas_call(middle_body, out_shape=[jax.ShapeDtypeStruct((pixels, widt...  104 us
    pallas_call x1, Pallas kernels, line_exchange(): pl.pallas_call(functools.partial(line_body, sign), out_shape=[jax.ShapeDt...  40.2 us
    ppermute x4, starting transfers between devices, extended(): lax.ppermute(head, axis, [((i + 1) % count, i) for i in range(count)])  15.3 us
    unnamed x16, local copies, waits for them, and re-layouts  4.88 us
    pallas_call x1, Pallas kernels, pull(): pl.pallas_call(pull_body, in_specs=[pl.BlockSpec(memory_space=pltpu.SMEM)...  4.68 us
    ppermute x4, waiting for transfers between devices, extended(): lax.ppermute(tail, axis, [(i, (i + 1) % count) for i in range(count)])  4.55 us
    dot_general x9, matrix products, conv_taps(): jnp.dot(kernel[tap_index], window, preferred_element_type=jnp.float32)  4.44 us
    pallas_call x1, Pallas kernels, spread(): pl.pallas_call(spread_body, in_specs=[pl.BlockSpec(memory_space=pltpu.SME...  4.39 us
  transfers between devices with their start and end apart: 8, of which 4 were waited for; matrix products, arithmetic and copies ran while one was open for 3% of the time, Pallas kernels for 0%

profile of v3, /device:TPU:0, one launch (start us, length us, event | category | flops | bytes accessed | tf_op | source)
XLA Modules:
  0.0 208.2 jit_solution(2320959223384200831)
XLA Ops:
  0.6 2.1 copy.55
  3.0 5.9 %collective-permute-start.1 = (bf16[222,1,128]{0,1,2:T(2,128)(2,1)S(1)}, bf16[222,1,128]{0,1,2:T(2,128)(2,1)S(1)}, u32[]{:S(2)}, u32[]{:S(2)}) collective-permute-start(bf16[222,1,128]{0,1,2:T(2,128)(2,1)S(1)} %get-tuple-element.45), channel_id=1, source_target_pairs={{4,0},{8,4},{12,8},{16,12},{20,16},{24,20},{28,24},{32,28},{36,32}... | collective-permute-start | bytes 170504 | tf_op jit(solution)/shard_map/ppermute | solution.py:32
  8.9 0.8 constant_dynamic-slice_fusion
  9.7 0.8 constant_dynamic-slice_fusion.1
  10.4 0.7 constant_dynamic-slice_fusion.2
  11.2 0.7 fusion.79
  11.9 1.2 convert_reduce_fusion
  13.3 0.5 select_reduce_fusion
  13.9 1.0 pad_maximum_fusion
  15.0 1.6 collective-permute-start.2
  16.6 1.7 collective-permute-start.3
  18.9 1.1 collective-permute-done.2
  20.4 0.7 maximum_select_fusion
  21.0 2.6 %fusion.101 = (bf16[222,16,128]{0,2,1:T(8,128)(2,1)S(1)}, bf16[222,16,128]{0,2,1:T(8,128)(2,1)S(1)}, bf16[222,16,128]{0,2,1:T(8,128)(2,1)S(1)}, bf16[222,16,128]...) fusion(bf16[222,18,130]{0,2,1:T(8,128)(2,1)S(1)} %maximum_selec, ...), kind=kLoop, calls=%fused_computation.236 | loop fusion | bytes 16367616 | tf_op jit(solution)/shard_map/slice | solution.py:66
  23.6 0.5 fusion.19
  24.1 0.5 convolution_add_fusion.15
  24.6 0.5 convolution_add_fusion.14
  25.1 0.5 convolution_add_fusion.13
  25.6 0.5 convolution_add_fusion.12
  26.1 0.5 convolution_add_fusion.11
  26.6 0.5 convolution_add_fusion.10
  27.1 0.5 convolution_add_fusion.9
  27.6 0.5 multiply_convert_fusion
  28.2 1.6 copy-done
  29.8 4.4 %spread.1 = (bf16[256,48,128]{2,1,0:T(8,128)(2,1)S(1)}, bf16[256,48,128]{2,1,0:T(8,128)(2,1)S(1)}, bf16[256,32,128]{2,1,0:T(8,128)(2,1)S(1)}) custom-call(s32[4,128]{1,0:T(4,128)S(1)} %pad_add_fusion.4.table, bf16[128,2048]{1,0:T(8,128)(2,1)S(1)} %get-tuple-element.70.hidden, bf16[128,128,128]{2,1,0:T(8,128)(2,1)S(1)} %copy-done), custom_call_target="tpu_custom_call" | custom-call | tf_op jit(solution)/shard_map/spread/pallas_call | solution.py:188
  34.2 40.2 %line_exchange_0.1 = (bf16[8,32,48,128]{3,2,1,0:T(8,128)(2,1)S(1)}, bf16[8,32,48,128]{3,2,1,0:T(8,128)(2,1)S(1)}, bf16[8,32,32,128]{3,2,1,0:T(8,128)(2,1)S(1)}) custom-call(bf16[8,32,48,128]{3,2,1,0:T(8,128)(2,1)S(1)} %bitcast.113, bf16[8,32,48,128]{3,2,1,0:T(8,128)(2,1)S(1)} %bitcast.114, bf16[8,32,32,128]{3,2,1,0:T(8,128)(2,1)S(1)} %bitcast.117), custom_call_target="tpu_custom_call" | custom-call | tf_op jit(solution)/shard_map/line_exchange_0/pallas_call | solution.py:152
  74.4 4.2 %combine.1 = (bf16[16,8,48,128]{3,2,1,0:T(8,128)(2,1)S(1)}, bf16[16,8,48,128]{3,2,1,0:T(8,128)(2,1)S(1)}, bf16[16,8,32,128]{3,2,1,0:T(8,128)(2,1)S(1)}) custom-call(s32[768]{0:T(1024)S(1)} %add.549.table, bf16[8,32,48,128]{3,2,1,0:T(8,128)(2,1)S(1)} %get-tuple-element.18.r0, bf16[8,32,48,128]{3,2,1,0:T(8,128)(2,1)S(1)} %get-tuple-element.19.r1, ...), custom_call_target="tpu_custom_call" | custom-call | tf_op jit(solution)/shard_map/combine/pallas_call | solution.py:217
  78.6 104.1 %middle.1 = (bf16[1024,128]{1,0:T(8,128)(2,1)S(1)}, bf16[8,32,48,128]{3,2,1,0:T(8,128)(2,1)S(1)}, bf16[8,32,48,128]{3,2,1,0:T(8,128)(2,1)S(1)}, bf16[8,32,32,128]{3,2,1,0:T(8,128)(2,1)S(1)}) custom-call(s32[768]{0:T(1024)S(1)} %add.549.table, s32[32]{0:T(128)S(1)} %reshape.491.beside, bf16[4,4,8,48,128]{4,3,2,1,0:T(8,128)(2,1)S(1)} %bitcast.120, ...), custom_call_target="tpu_custom_call" | custom-call | tf_op jit(solution)/shard_map/middle/pallas_call | solution.py:521
  182.7 4.7 %pull.1 = bf16[128,2048]{1,0:T(8,128)(2,1)S(1)} custom-call(s32[4,128]{1,0:T(4,128)S(1)} %pad_add_fusion.4.table, bf16[128,128,128]{2,1,0:T(8,128)(2,1)S(1)} %copy-done, f32[128,2048]{1,0:T(8,128)S(1)} %get-tuple-element.71.pre_conv, bf16[256,48,128]{2,1,0:T(8,128)(2,1)S(1)} %bitcast.115, bf16[256,48,128]{2,1,0:T(8,128)(2,1)S(1)} %bitcast.116, ...), custom_call_target="tpu_custom_call" | custom-call | tf_op jit(solution)/shard_map/pull/pallas_call | solution.py:256
  187.5 0.7 copy.70
  188.5 4.9 %collective-permute-start.5 = (bf16[128,1,128]{0,1,2:T(2,128)(2,1)S(1)}, bf16[128,1,128]{0,1,2:T(2,128)(2,1)S(1)}, u32[]{:S(2)}, u32[]{:S(2)}) collective-permute-start(bf16[128,1,128]{0,1,2:T(2,128)(2,1)S(1)} %get-tuple-element.58), channel_id=1, source_target_pairs={{4,0},{8,4},{12,8},{16,12},{20,16},{24,20},{28,24},{32,28},{36,32}... | collective-permute-start | bytes 98312 | tf_op jit(solution)/shard_map/ppermute | solution.py:32
  193.5 1.9 collective-permute-done.4
  195.4 0.5 pad_maximum_fusion.1
  195.9 0.4 collective-permute-start.6
  196.4 2.9 %collective-permute-start.7 = (bf16[128,18,1]{0,1,2:T(8,128)(2,1)S(1)}, bf16[128,18,1]{0,1,2:T(8,128)(2,1)S(1)}, u32[]{:S(2)}, u32[]{:S(2)}) collective-permute-start(bf16[128,18,1]{0,1,2:T(8,128)(2,1)S(1)} %get-tuple-element.47), channel_id=1, source_target_pairs={{1,0},{2,1},{3,2},{0,3},{5,4},{6,5},{7,6},{4,7},{9,8},{10,9},{11,1... | collective-permute-start | bytes 13832 | tf_op jit(solution)/shard_map/ppermute | solution.py:32
  199.3 1.5 collective-permute-done.6
  201.2 0.9 fusion.104
  202.1 0.4 fusion.17
  202.5 0.4 convolution_add_fusion.7
  202.9 0.4 convolution_add_fusion.6
  203.3 0.4 convolution_add_fusion.5
  203.8 0.4 convolution_add_fusion.4
  204.2 0.4 convolution_add_fusion.3
  204.6 0.4 convolution_add_fusion.2
  205.0 0.4 convolution_add_fusion.1
  205.4 0.4 convolution_add_fusion
  206.1 1.3 slice.285
  207.5 0.7 copy.88
  (52 shorter events, 2.8 us)
Async XLA Ops:
  0.6 12.6 %copy-start.4 = (s32[4,4,3]{1,0,2:T(4,128)S(1)}, s32[4,4,3]{1,0,2:T(4,128)}, u32[]{:S(2)}) copy-start(s32[4,4,3]{1,0,2:T(4,128)} %param.15) | copy-start | bytes 580
  0.6 13.3 %copy-start.5 = (s32[128]{0:T(128)S(1)}, s32[128]{0:T(128)}, u32[]{:S(2)}) copy-start(s32[128]{0:T(128)} %param.12) | copy-start | bytes 1540
  2.9 11.0 %collective-permute-start = (bf16[222,1,128]{0,1,2:T(2,128)(2,1)S(1)}, bf16[222,1,128]{0,1,2:T(2,128)(2,1)S(1)}, u32[]{:S(2)}, u32[]{:S(2)}) collective-permute-start(bf16[222,1,128]{0,1,2:T(2,128)(2,1)S(1)} %get-tuple-element.44), channel_id=1, source_target_pairs={{0,4},{4,8},{8,12},{12,16},{16,20},{20,24},{24,28},{28,32},{32,36}... | collective-permute-start | bytes 170504 | tf_op jit(solution)/shard_map/ppermute | solution.py:30
  3.0 10.9 %collective-permute-start.1 = (bf16[222,1,128]{0,1,2:T(2,128)(2,1)S(1)}, bf16[222,1,128]{0,1,2:T(2,128)(2,1)S(1)}, u32[]{:S(2)}, u32[]{:S(2)}) collective-permute-start(bf16[222,1,128]{0,1,2:T(2,128)(2,1)S(1)} %get-tuple-element.45), channel_id=1, source_target_pairs={{4,0},{8,4},{12,8},{16,12},{20,16},{24,20},{28,24},{32,28},{36,32}... | collective-permute-start | bytes 170504 | tf_op jit(solution)/shard_map/ppermute | solution.py:32
  15.0 5.0 %collective-permute-start.2 = (bf16[222,18,1]{0,1,2:T(8,128)(2,1)S(1)}, bf16[222,18,1]{0,1,2:T(8,128)(2,1)S(1)}, u32[]{:S(2)}, u32[]{:S(2)}) collective-permute-start(bf16[222,18,1]{0,1,2:T(8,128)(2,1)S(1)} %get-tuple-element.33), channel_id=1, source_target_pairs={{0,1},{1,2},{2,3},{3,0},{4,5},{5,6},{6,7},{7,4},{8,9},{9,10},{10,1... | collective-permute-start | bytes 23984 | tf_op jit(solution)/shard_map/ppermute | solution.py:30
  16.6 3.7 %collective-permute-start.3 = (bf16[222,18,1]{0,1,2:T(8,128)(2,1)S(1)}, bf16[222,18,1]{0,1,2:T(8,128)(2,1)S(1)}, u32[]{:S(2)}, u32[]{:S(2)}) collective-permute-start(bf16[222,18,1]{0,1,2:T(8,128)(2,1)S(1)} %get-tuple-element.34), channel_id=1, source_target_pairs={{1,0},{2,1},{3,2},{0,3},{5,4},{6,5},{7,6},{4,7},{9,8},{10,9},{11,1... | collective-permute-start | bytes 23984 | tf_op jit(solution)/shard_map/ppermute | solution.py:32
  21.0 2.6 %copy-start.3 = (bf16[9,128,222]{1,2,0:T(8,128)(2,1)S(1)}, bf16[9,128,222]{1,2,0:T(8,128)(2,1)}, u32[]{:S(2)}) copy-start(bf16[9,128,222]{1,2,0:T(8,128)(2,1)} %param.10) | copy-start | bytes 1534468
  27.6 2.2 %copy-start = (bf16[128,128,128]{2,1,0:T(8,128)(2,1)S(1)}, bf16[128,128,128]{2,1,0:T(8,128)(2,1)}, u32[]{:S(2)}) copy-start(bf16[128,128,128]{2,1,0:T(8,128)(2,1)} %blocks.3) | copy-start | bytes 12582916
  74.4 4.2 %copy-start.1 = (bf16[2,128,128]{2,1,0:T(8,128)(2,1)S(1)}, bf16[2,128,128]{2,1,0:T(8,128)(2,1)}, u32[]{:S(2)}) copy-start(bf16[2,128,128]{2,1,0:T(8,128)(2,1)} %weights.1) | copy-start | bytes 196612
  74.4 4.2 %copy-start.2 = (f32[128]{0:T(128)S(1)}, f32[128]{0:T(128)}, u32[]{:S(2)}) copy-start(f32[128]{0:T(128)} %param.17) | copy-start | bytes 1540
  188.4 7.1 %collective-permute-start.4 = (bf16[128,1,128]{0,1,2:T(2,128)(2,1)S(1)}, bf16[128,1,128]{0,1,2:T(2,128)(2,1)S(1)}, u32[]{:S(2)}, u32[]{:S(2)}) collective-permute-start(bf16[128,1,128]{0,1,2:T(2,128)(2,1)S(1)} %get-tuple-element.57), channel_id=1, source_target_pairs={{0,4},{4,8},{8,12},{12,16},{16,20},{20,24},{24,28},{28,32},{32,36}... | collective-permute-start | bytes 98312 | tf_op jit(solution)/shard_map/ppermute | solution.py:30
  188.5 6.9 %collective-permute-start.5 = (bf16[128,1,128]{0,1,2:T(2,128)(2,1)S(1)}, bf16[128,1,128]{0,1,2:T(2,128)(2,1)S(1)}, u32[]{:S(2)}, u32[]{:S(2)}) collective-permute-start(bf16[128,1,128]{0,1,2:T(2,128)(2,1)S(1)} %get-tuple-element.58), channel_id=1, source_target_pairs={{4,0},{8,4},{12,8},{16,12},{20,16},{24,20},{28,24},{32,28},{36,32}... | collective-permute-start | bytes 98312 | tf_op jit(solution)/shard_map/ppermute | solution.py:32
  195.9 4.9 %collective-permute-start.6 = (bf16[128,18,1]{0,1,2:T(8,128)(2,1)S(1)}, bf16[128,18,1]{0,1,2:T(8,128)(2,1)S(1)}, u32[]{:S(2)}, u32[]{:S(2)}) collective-permute-start(bf16[128,18,1]{0,1,2:T(8,128)(2,1)S(1)} %get-tuple-element.46), channel_id=1, source_target_pairs={{0,1},{1,2},{2,3},{3,0},{4,5},{5,6},{6,7},{7,4},{8,9},{9,10},{10,1... | collective-permute-start | bytes 13832 | tf_op jit(solution)/shard_map/ppermute | solution.py:30
  196.4 4.5 %collective-permute-start.7 = (bf16[128,18,1]{0,1,2:T(8,128)(2,1)S(1)}, bf16[128,18,1]{0,1,2:T(8,128)(2,1)S(1)}, u32[]{:S(2)}, u32[]{:S(2)}) collective-permute-start(bf16[128,18,1]{0,1,2:T(8,128)(2,1)S(1)} %get-tuple-element.47), channel_id=1, source_target_pairs={{1,0},{2,1},{3,2},{0,3},{5,4},{6,5},{7,6},{4,7},{9,8},{10,9},{11,1... | collective-permute-start | bytes 13832 | tf_op jit(solution)/shard_map/ppermute | solution.py:32

commit v4 on v3

--- a/solution.py
+++ b/solution.py
@@ -18,22 +18,6 @@
 PARTS = ((0, 48), (48, 48), (96, 32))
 LINE = ("y", "z", "x")
 PLANE = (("z", "x"), ("x", "y"), ("y", "z"))
-
-
-def extended(cells, sides, width):
-    for axis, dim in sides:
-        count = lax.axis_size(axis)
-        head = lax.slice_in_dim(cells, 0, width, axis=dim)
-        tail = lax.slice_in_dim(cells, cells.shape[dim] - width, cells.shape[dim], axis=dim)
-        cells = jnp.concatenate(
-            [
-                lax.ppermute(tail, axis, [(i, (i + 1) % count) for i in range(count)]),
-                cells,
-                lax.ppermute(head, axis, [((i + 1) % count, i) for i in range(count)]),
-            ],
-            axis=dim,
-        )
-    return cells
 
 
 def silu_slope(values):
@@ -50,43 +34,6 @@
     slope_near = (half_mass * far) * (grown - shrunk) / (1.0 - half_mass * (grown + shrunk))
     slope_far = jnp.where(latent > 0.0, far, -far)
     return jnp.where(jnp.abs(latent) < 0.5, slope_near, slope_far)
-
-
-def conv_taps(kernel, padded, reverse):
-    lon_cells = padded.shape[1] - 2
-    lat_cells = padded.shape[2] - 2
-    out_rows = kernel.shape[2] if reverse else kernel.shape[1]
-    result = jnp.zeros((out_rows, lon_cells * lat_cells), jnp.float32)
-    for tap_index in range(9):
-        lon_shift = tap_index // 3
-        lat_shift = tap_index % 3
-        if reverse:
-            lon_shift = 2 - lon_shift
-            lat_shift = 2 - lat_shift
-        window = padded[
-            :, lon_shift : lon_shift + lon_cells, lat_shift : lat_shift + lat_cells
-        ].reshape(padded.shape[0], lon_cells * lat_cells)
-        if reverse:
-            result = result + lax.dot_general(
-                kernel[tap_index],
-                window,
-                (((0,), (0,)), ((), ())),
-                preferred_element_type=jnp.float32,
-            )
-        else:
-            result = result + jnp.dot(kernel[tap_index], window, preferred_element_type=jnp.float32)
-    return result
-
-
-def grid_rims(values):
-    padded = extended(values, (("lon", 1), ("lat", 2)), 1)
-    lat_pos = lax.axis_index("lat")
-    lat_last = lax.axis_size("lat") - 1
-    column = lax.broadcasted_iota(jnp.int32, (1, 1, padded.shape[2]), 2)
-    outside = (column == 0) & (lat_pos == 0) | (column == padded.shape[2] - 1) & (
-        lat_pos == lat_last
-    )
-    return jnp.where(outside, jnp.zeros_like(padded), padded)
 
 
 def torus_position():
@@ -557,6 +504,137 @@
     )
 
 
+def conv_body(reverse, lon_cells, x, taps, *refs):
+    if reverse:
+        out, wide, q0, q1, q2, pack, got, sends, recvs = refs
+        weight = [taps.at[8 - t] for t in range(9)]
+    else:
+        out, hidden, wide, q0, q1, q2, pack, got, sends, recvs, turned = refs
+        weight = [turned.at[t] for t in range(9)]
+    lon, lat = lax.axis_index("lon"), lax.axis_index("lat")
+    lons, lats = lax.axis_size("lon"), lax.axis_size("lat")
+    above, below = ((lon + 1) % lons, lat), ((lon + lons - 1) % lons, lat)
+    north, south = (lon, (lat + 1) % lats), (lon, (lat + lats - 1) % lats)
+    barrier = pltpu.get_barrier_semaphore()
+    for peer in (above, below, north, south):
+        pl.semaphore_signal(barrier, inc=1, device_id=peer, device_id_type=MESH)
+    span = lon_cells * BLOCK
+    if not reverse:
+        for t in range(9):
+            turned[t] = taps[t].T
+    wide[:, BLOCK : BLOCK + span] = x[...]
+    pl.semaphore_wait(barrier, 4)
+    rows = [
+        remote(
+            x.at[:, pl.ds(0, BLOCK)],
+            wide.at[:, pl.ds(BLOCK + span, BLOCK)],
+            sends.at[0],
+            recvs.at[0],
+            below,
+        ),
+        remote(
+            x.at[:, pl.ds(span - BLOCK, BLOCK)],
+            wide.at[:, pl.ds(0, BLOCK)],
+            sends.at[1],
+            recvs.at[1],
+            above,
+        ),
+    ]
+    shifted = (q0, q1, q2)
+
+    def products(n, offsets):
+        for e in offsets:
+            total = None
+            for a in range(3):
+                start = pl.multiple_of(n * 2 * BLOCK + a * BLOCK, BLOCK)
+                term = dot(weight[3 * a + e][...], wide[:, pl.ds(start, 2 * BLOCK)])
+                total = term if total is None else total + term
+            shifted[e][2 * n] = total[:, :BLOCK]
+            shifted[e][2 * n + 1] = total[:, BLOCK:]
+
+    pairs = lon_cells // 2
+
+    def inside(n, carry):
+        products(n, (0, 1, 2))
+        return carry
+
+    lax.fori_loop(1, pairs - 1, inside, 0)
+    for copy in rows:
+        copy.wait()
+
+    def outside(n, carry):
+        products(n * (pairs - 1), (0, 2))
+        return carry
+
+    lax.fori_loop(0, 2, outside, 0)
+    lane = iota((out.shape[0], BLOCK), 1)
+    to_north = jnp.zeros((out.shape[0], BLOCK), jnp.float32)
+    to_south = jnp.zeros((out.shape[0], BLOCK), jnp.float32)
+    for i in range(lon_cells):
+        to_north = jnp.where(lane == i, pltpu.roll(q0[i], i + 1, 1), to_north)
+        to_south = jnp.where(lane == i, pltpu.roll(q2[i], i, 1) if i else q2[i], to_south)
+    pack[0] = to_north
+    pack[1] = to_south
+    columns = [
+        remote(pack.at[0], got.at[0], sends.at[2], recvs.at[2], north),
+        remote(pack.at[1], got.at[1], sends.at[3], recvs.at[3], south),
+    ]
+
+    def middle_tap(n, carry):
+        products(n * (pairs - 1), (1,))
+        return carry
+
+    lax.fori_loop(0, 2, middle_tap, 0)
+    for i in range(lon_cells):
+        q1[i] = (
+            q1[i]
+            + jnp.where(lane == 0, 0.0, pltpu.roll(q0[i], 1, 1))
+            + jnp.where(lane == BLOCK - 1, 0.0, pltpu.roll(q2[i], BLOCK - 1, 1))
+        )
+    for copy in columns:
+        copy.wait()
+    from_south = jnp.where(lat > 0, got[0], 0.0)
+    from_north = jnp.where(lat < lats - 1, got[1], 0.0)
+    for i in range(lon_cells):
+        first = pltpu.roll(from_south, BLOCK - i, 1) if i else from_south
+        last = pltpu.roll(from_north, BLOCK - 1 - i, 1)
+        value = (
+            q1[i] + jnp.where(lane == 0, first, 0.0) + jnp.where(lane == BLOCK - 1, last, 0.0)
+        )
+        cells = slice(i * BLOCK, (i + 1) * BLOCK)
+        out[:, cells] = value
+        if not reverse:
+            hidden[:, cells] = (value * jax.nn.sigmoid(value)).astype(hidden.dtype)
+
+
+def grid_conv(cells, taps, reverse, collective_id):
+    depth, span = cells.shape
+    lon_cells = span // BLOCK
+    rows, turned = (taps.shape[1], []) if reverse else (
+        taps.shape[2],
+        [pltpu.VMEM((9, taps.shape[2], taps.shape[1]), taps.dtype)],
+    )
+    vmem = pl.BlockSpec(memory_space=pltpu.VMEM)
+    shapes = [jax.ShapeDtypeStruct((rows, span), jnp.float32)]
+    if not reverse:
+        shapes.append(jax.ShapeDtypeStruct((rows, span), jnp.bfloat16))
+    return pl.pallas_call(
+        functools.partial(conv_body, reverse, lon_cells),
+        out_shape=shapes,
+        in_specs=[vmem] * 2,
+        out_specs=[vmem] * len(shapes),
+        scratch_shapes=[pltpu.VMEM((depth, span + 2 * BLOCK), cells.dtype)]
+        + [pltpu.VMEM((lon_cells, rows, BLOCK), jnp.float32)] * 3
+        + [pltpu.VMEM((2, rows, BLOCK), jnp.float32)] * 2
+        + [pltpu.SemaphoreType.DMA((4,)), pltpu.SemaphoreType.DMA((4,))]
+        + turned,
+        compiler_params=pltpu.CompilerParams(
+            collective_id=collective_id, has_side_effects=True, vmem_limit_bytes=24 << 20
+        ),
+        name="conv_back" if reverse else "conv",
+    )(cells, taps)
+
+
 def routing(source_block, target_device, target_half):
     here = torus_position()
     count = source_block.shape[0]
@@ -632,20 +710,18 @@
     rate_scale,
 ):
     channels, lon_cells, lat_cells = fields.shape
-    latent_width = conv_weight.shape[1]
     table, lines = routing(source_block, target_device, target_half)
-    pre_conv = conv_taps(conv_weight, grid_rims(fields), False)
-    hidden = jax.nn.silu(pre_conv).astype(jnp.bfloat16)
+    extra = -channels % 16
+    taps = jnp.pad(jnp.swapaxes(conv_weight, 1, 2), ((0, 0), (0, extra), (0, 0)))
+    columns = jnp.pad(fields.reshape(channels, lon_cells * lat_cells), ((0, extra), (0, 0)))
+    pre_conv, hidden = grid_conv(columns, taps, False, 2)
     outgoing = spread(lines, hidden, regrid_blocks)
     arrived = line_exchange(outgoing, 1, 0)
     partial = combine(table, arrived)
     codes, *answers = middle(table, neighbours, partial, hp_weight, rate_scale, 1)
-    pre_grad = pull(lines, regrid_blocks, pre_conv, answers).reshape(
-        latent_width, lon_cells, lat_cells
-    )
-    grad_fields = conv_taps(conv_weight, grid_rims(pre_grad), True).reshape(
-        channels, lon_cells, lat_cells
-    )
+    pre_grad = pull(lines, regrid_blocks, pre_conv, answers)
+    (grad_columns,) = grid_conv(pre_grad, taps, True, 3)
+    grad_fields = grad_columns[:channels].reshape(channels, lon_cells, lat_cells)
     return (codes, grad_fields)
 
 

time: 209 us -> 198 us (0.947)
  Pallas kernels: 158 us -> 186 us
  starting transfers between devices: 17.7 us -> 0 us
  matrix products: 8.03 us -> 0 us
  local copies, waits for them, and re-layouts: 14.4 us -> 7.22 us
  waiting for transfers between devices: 4.9 us -> 0 us
    pallas_call x0 -> x2, Pallas kernels: none -> 29 us  [grid_conv(): pl.pallas_call(functools.partial(conv_body, reverse, lon_cells), out_shap...]
    ppermute x8 -> x0, starting transfers between devices: 17.7 us -> none  [the longest x4 15.3 us: extended(): lax.ppermute(head, axis, [((i + 1) % count, i) for i in range(count)])]
    dot_general x18 -> x0, matrix products: 8.03 us -> none  [the longest x9 4.44 us: conv_taps(): jnp.dot(kernel[tap_index], window, preferred_element_type=jnp.float32)]
    ppermute x8 -> x0, waiting for transfers between devices: 4.9 us -> none  [the longest x4 4.55 us: extended(): lax.ppermute(tail, axis, [(i, (i + 1) % count) for i in range(count)])]
    slice x6 -> x0, local copies, waits for them, and re-layouts: 3.84 us -> none  [the longest x2 3.52 us: conv_taps(): padded[:, lon_shift:lon_shift + lon_cells, lat_shift:lat_shift + lat_cells]]
    unnamed x16 -> x12, local copies, waits for them, and re-layouts: 4.88 us -> 1.45 us
  transfers between devices with their start and end apart: 8 -> 0, of which waited for: 4 -> 0; matrix products, arithmetic and copies ran while one was open for 3% -> 0% of each run, Pallas kernels for 0% -> 0%
where the time goes in v4:
time: 198 us; the launch traced here: 197 us
  Pallas kernels  186 us (94%)
  local copies, waits for them, and re-layouts  7.22 us (4%)
  other arithmetic  3.34 us (2%)
    pallas_call x1, Pallas kernels, middle(): pl.pallas_call(middle_body, out_shape=[jax.ShapeDtypeStruct((pixels, widt...  105 us
    pallas_call x1, Pallas kernels, line_exchange(): pl.pallas_call(functools.partial(line_body, sign), out_shape=[jax.ShapeDt...  39 us
    pallas_call x2, Pallas kernels, grid_conv(): pl.pallas_call(functools.partial(conv_body, reverse, lon_cells), out_shap...  29 us
    pallas_call x1, Pallas kernels, pull(): pl.pallas_call(pull_body, in_specs=[pl.BlockSpec(memory_space=pltpu.SMEM)...  4.71 us
    pallas_call x1, Pallas kernels, spread(): pl.pallas_call(spread_body, in_specs=[pl.BlockSpec(memory_space=pltpu.SME...  4.39 us
    pallas_call x1, Pallas kernels, combine(): pl.pallas_call(combine_body, grid_spec=pltpu.PrefetchScalarGridSpec(num_s...  4.11 us

profile of v4, /device:TPU:0, one launch (start us, length us, event | category | flops | bytes accessed | tf_op | source)
XLA Modules:
  0.0 197.3 jit_solution(7290938466626378452)
XLA Ops:
  0.6 0.0 copy-start.3
  0.7 0.8 fusion.40
  1.5 0.7 add_select_fusion.12
  2.3 0.1 copy.14
  2.4 0.1 reshape.422.beside
  2.5 0.8 constant_dynamic-slice_fusion
  3.2 0.8 constant_dynamic-slice_fusion.1
  4.0 0.7 constant_dynamic-slice_fusion.2
  4.7 1.2 convert_reduce_fusion
  6.0 0.5 select_reduce_fusion
  6.5 0.1 select_reduce_fusion.1
  6.6 0.1 add.489.table
  6.7 0.7 pad_add_fusion.4.table
  7.4 1.1 pad.9.taps
  8.5 0.0 copy-done.3
  8.5 0.2 pad.29
  8.7 0.0 copy-start
  8.7 0.2 copy.15
  8.9 0.1 pad.8.x
  9.0 15.5 %conv.1 = (f32[128,2048]{1,0:T(8,128)S(1)}, bf16[128,2048]{1,0:T(8,128)(2,1)S(1)}) custom-call(bf16[224,2048]{1,0:T(8,128)(2,1)S(1)} %pad.8.x, bf16[9,224,128]{2,1,0:T(8,128)(2,1)S(1)} %pad.9.taps), custom_call_target="tpu_custom_call" | custom-call | tf_op jit(solution)/shard_map/conv/pallas_call | solution.py:621
  24.5 0.0 copy-done
  24.5 4.4 %spread.1 = (bf16[256,48,128]{2,1,0:T(8,128)(2,1)S(1)}, bf16[256,48,128]{2,1,0:T(8,128)(2,1)S(1)}, bf16[256,32,128]{2,1,0:T(8,128)(2,1)S(1)}) custom-call(s32[4,128]{1,0:T(4,128)S(1)} %pad_add_fusion.4.table, bf16[128,2048]{1,0:T(8,128)(2,1)S(1)} %get-tuple-element.17.hidden, bf16[128,128,128]{2,1,0:T(8,128)(2,1)S(1)} %copy-done), custom_call_target="tpu_custom_call" | custom-call | tf_op jit(solution)/shard_map/spread/pallas_call | solution.py:135
  28.9 39.0 %line_exchange_0.1 = (bf16[8,32,48,128]{3,2,1,0:T(8,128)(2,1)S(1)}, bf16[8,32,48,128]{3,2,1,0:T(8,128)(2,1)S(1)}, bf16[8,32,32,128]{3,2,1,0:T(8,128)(2,1)S(1)}) custom-call(bf16[8,32,48,128]{3,2,1,0:T(8,128)(2,1)S(1)} %bitcast.31, bf16[8,32,48,128]{3,2,1,0:T(8,128)(2,1)S(1)} %bitcast.32, bf16[8,32,32,128]{3,2,1,0:T(8,128)(2,1)S(1)} %bitcast.35), custom_call_target="tpu_custom_call" | custom-call | tf_op jit(solution)/shard_map/line_exchange_0/pallas_call | solution.py:99
  67.9 0.0 copy-start.1
  67.9 0.0 copy-start.2
  67.9 4.1 %combine.1 = (bf16[16,8,48,128]{3,2,1,0:T(8,128)(2,1)S(1)}, bf16[16,8,48,128]{3,2,1,0:T(8,128)(2,1)S(1)}, bf16[16,8,32,128]{3,2,1,0:T(8,128)(2,1)S(1)}) custom-call(s32[768]{0:T(1024)S(1)} %add.489.table, bf16[8,32,48,128]{3,2,1,0:T(8,128)(2,1)S(1)} %get-tuple-element.21.r0, bf16[8,32,48,128]{3,2,1,0:T(8,128)(2,1)S(1)} %get-tuple-element.22.r1, ...), custom_call_target="tpu_custom_call" | custom-call | tf_op jit(solution)/shard_map/combine/pallas_call | solution.py:164
  72.0 0.0 copy-done.1
  72.0 0.0 copy-done.2
  72.0 104.7 %middle.1 = (bf16[1024,128]{1,0:T(8,128)(2,1)S(1)}, bf16[8,32,48,128]{3,2,1,0:T(8,128)(2,1)S(1)}, bf16[8,32,48,128]{3,2,1,0:T(8,128)(2,1)S(1)}, bf16[8,32,32,128]{3,2,1,0:T(8,128)(2,1)S(1)}) custom-call(s32[768]{0:T(1024)S(1)} %add.489.table, s32[32]{0:T(128)S(1)} %reshape.422.beside, bf16[4,4,8,48,128]{4,3,2,1,0:T(8,128)(2,1)S(1)} %bitcast.37, ...), custom_call_target="tpu_custom_call" | custom-call | tf_op jit(solution)/shard_map/middle/pallas_call | solution.py:468
  176.7 4.7 %pull.1.x = bf16[128,2048]{1,0:T(8,128)(2,1)S(1)} custom-call(s32[4,128]{1,0:T(4,128)S(1)} %pad_add_fusion.4.table, bf16[128,128,128]{2,1,0:T(8,128)(2,1)S(1)} %copy-done, f32[128,2048]{1,0:T(8,128)S(1)} %get-tuple-element.28.pre_conv, bf16[256,48,128]{2,1,0:T(8,128)(2,1)S(1)} %bitcast.33, bf16[256,48,128]{2,1,0:T(8,128)(2,1)S(1)} %bitcast.34, ...), custom_call_target="tpu_custom_call" | custom-call | tf_op jit(solution)/shard_map/pull/pallas_call | solution.py:203
  181.4 13.5 %conv_back.1 = f32[224,2048]{1,0:T(8,128)S(1)} custom-call(bf16[128,2048]{1,0:T(8,128)(2,1)S(1)} %pull.1.x, bf16[9,224,128]{2,1,0:T(8,128)(2,1)S(1)} %pad.9.taps), custom_call_target="tpu_custom_call" | custom-call | tf_op jit(solution)/shard_map/conv_back/pallas_call | solution.py:621
  195.0 0.3 copy.16
  195.3 1.3 slice.114
  196.6 0.7 copy.18
  (14 shorter events, 0.2 us)
Async XLA Ops:
  0.6 7.9 %copy-start.3 = (bf16[222,16,128]{2,1,0:T(8,128)(2,1)S(1)}, bf16[222,16,128]{2,1,0:T(8,128)(2,1)}, u32[]{:S(2)}) copy-start(bf16[222,16,128]{2,1,0:T(8,128)(2,1)} %param.9) | copy-start | bytes 2727940
  8.7 15.8 %copy-start = (bf16[128,128,128]{2,1,0:T(8,128)(2,1)S(1)}, bf16[128,128,128]{2,1,0:T(8,128)(2,1)}, u32[]{:S(2)}) copy-start(bf16[128,128,128]{2,1,0:T(8,128)(2,1)} %blocks.3) | copy-start | bytes 12582916
  67.9 4.1 %copy-start.1 = (bf16[2,128,128]{2,1,0:T(8,128)(2,1)S(1)}, bf16[2,128,128]{2,1,0:T(8,128)(2,1)}, u32[]{:S(2)}) copy-start(bf16[2,128,128]{2,1,0:T(8,128)(2,1)} %weights.1) | copy-start | bytes 196612
  67.9 4.1 %copy-start.2 = (f32[128]{0:T(128)S(1)}, f32[128]{0:T(128)}, u32[]{:S(2)}) copy-start(f32[128]{0:T(128)} %param.17) | copy-start | bytes 1540

commit v5 on v4

--- a/solution.py
+++ b/solution.py
@@ -12,6 +12,7 @@
 BLOCK = 128
 HALVES = 8
 GROUP = 8
+FEW, MANY = 22, 32
 MESH = pl.DeviceIdType.MESH
 LOG_TWO = 0.6931471805599453
 
@@ -123,57 +124,68 @@
                 blocks[block], turned[table[0, block]], preferred_element_type=jnp.float32
             ).astype(jnp.bfloat16)
             for k, (start, count) in enumerate(PARTS):
-                outs[k][table[1 + k, block]] = made[start : start + count]
+                spot = table[1 + k, block]
+                outs[k][spot >> 5, spot & 31] = made[start : start + count]
         return carry
 
     lax.fori_loop(0, blocks.shape[0] // GROUP, some, 0)
 
 
-def spread(table, hidden, regrid_blocks):
+def spread(table, hidden, regrid_blocks, slots):
     cells, width = regrid_blocks.shape[2], hidden.shape[0]
     vmem = pl.BlockSpec(memory_space=pltpu.VMEM)
-    parts = pl.pallas_call(
+    return pl.pallas_call(
         spread_body,
         in_specs=[pl.BlockSpec(memory_space=pltpu.SMEM), vmem, vmem],
         out_specs=[vmem] * 3,
         scratch_shapes=[pltpu.VMEM((hidden.shape[1] // BLOCK, cells, width), jnp.bfloat16)],
-        out_shape=[jax.ShapeDtypeStruct((256, n, width), jnp.bfloat16) for _, n in PARTS],
+        out_shape=[jax.ShapeDtypeStruct((8, slots, n, width), jnp.bfloat16) for _, n in PARTS],
         compiler_params=pltpu.CompilerParams(vmem_limit_bytes=24 << 20),
         name="spread",
     )(table, hidden, regrid_blocks)
-    return [part.reshape(8, 32, *part.shape[1:]) for part in parts]
 
 
 def combine_body(table, r0, r1, r2, p0, p1, p2, a0, a1, a2):
-    place = pl.program_id(0)
     ins, outs, sums = (r0, r1, r2), (p0, p1, p2), (a0, a1, a2)
-    for total in sums:
-        total[...] = jnp.zeros_like(total)
-    for chunk in range(8):
+    places = outs[0].shape[0]
+
+    def clear(place, carry):
+        for total in sums:
+            cleared = pl.ds(place * HALVES, HALVES)
+            total[cleared] = jnp.zeros((HALVES, *total.shape[1:]), jnp.float32)
+        return carry
+
+    def add(slot, carry):
+        for chunk in range(8):
+            for k in range(3):
+                spot = table[k * 256 + chunk * 32 + slot]
+                sums[k][spot] += ins[k][chunk, slot].astype(jnp.float32)
+        return carry
+
+    def give(place, carry):
         for k in range(3):
-            entry = k * 256 + chunk * 32 + place * 2
-            for rank in range(2):
-                half = table[entry + rank]
-                sums[k][half] += ins[k][chunk, rank].astype(jnp.float32)
-    for k in range(3):
-        outs[k][0] = sums[k][:HALVES].astype(jnp.bfloat16)
+            outs[k][place] = sums[k][pl.ds(place * HALVES, HALVES)].astype(jnp.bfloat16)
+        return carry
+
+    lax.fori_loop(0, places, clear, 0)
+    lax.fori_loop(0, ins[0].shape[1], add, 0)
+    lax.fori_loop(0, places, give, 0)
 
 
 def combine(table, parts):
     width = parts[0].shape[-1]
+    vmem = pl.BlockSpec(memory_space=pltpu.VMEM)
     return pl.pallas_call(
         combine_body,
-        grid_spec=pltpu.PrefetchScalarGridSpec(
-            num_scalar_prefetch=1,
-            grid=(16,),
-            in_specs=[pl.BlockSpec((8, 2, n, width), lambda i, t: (0, i, 0, 0)) for _, n in PARTS],
-            out_specs=[
-                pl.BlockSpec((1, HALVES, n, width), lambda i, t: (i, 0, 0, 0)) for _, n in PARTS
-            ],
-            scratch_shapes=[pltpu.VMEM((HALVES + 1, n, width), jnp.float32) for _, n in PARTS],
-        ),
-        out_shape=[jax.ShapeDtypeStruct((16, HALVES, n, width), jnp.bfloat16) for _, n in PARTS],
-        compiler_params=pltpu.CompilerParams(vmem_limit_bytes=8 << 20),
+        in_specs=[pl.BlockSpec(memory_space=pltpu.SMEM)] + [vmem] * 3,
+        out_specs=[vmem] * 3,
+        scratch_shapes=[
+            pltpu.VMEM((RING * RING * HALVES + 1, n, width), jnp.float32) for _, n in PARTS
+        ],
+        out_shape=[
+            jax.ShapeDtypeStruct((RING * RING, HALVES, n, width), jnp.bfloat16) for _, n in PARTS
+        ],
+        compiler_params=pltpu.CompilerParams(vmem_limit_bytes=28 << 20),
         name="combine",
     )(table, *parts)
 
@@ -185,7 +197,10 @@
     def some(step, carry):
         for b in range(GROUP):
             block = step * GROUP + b
-            grad = jnp.concatenate([ins[k][table[1 + k, block]] for k in range(3)], axis=0)
+            spots = [table[1 + k, block] for k in range(3)]
+            grad = jnp.concatenate(
+                [ins[k][spot >> 5, spot & 31] for k, spot in enumerate(spots)], axis=0
+            )
             sums[table[0, block]] += jnp.dot(
                 grad, blocks[block], preferred_element_type=jnp.float32
             )
@@ -208,7 +223,7 @@
         out_shape=jax.ShapeDtypeStruct(pre_conv.shape, jnp.bfloat16),
         compiler_params=pltpu.CompilerParams(vmem_limit_bytes=24 << 20),
         name="pull",
-    )(table, regrid_blocks, pre_conv, *[part.reshape(256, *part.shape[2:]) for part in parts])
+    )(table, regrid_blocks, pre_conv, *parts)
 
 
 def remote(source, target, send, recv, place):
@@ -427,18 +442,20 @@
     for chunk in (4, 5, 2, 3, 6, 7, 1, 0):
         step, flip = chunk // 2, chunk % 2
 
-        def fill(place, carry):
+        def fill(pair, carry):
             for k in range(3):
-                for rank in range(2):
-                    half = jnp.minimum(table[k * 256 + chunk * 32 + place * 2 + rank], HALVES - 1)
-                    found = us[k][place, half]
+                for slot in (2 * pair, 2 * pair + 1):
+                    spot = jnp.minimum(
+                        table[k * 256 + chunk * 32 + slot], RING * RING * HALVES - 1
+                    )
+                    found = us[k][spot >> 3, spot & 7]
                     if chunk:
-                        vs[k][chunk - 1, place * 2 + rank] = found
+                        vs[k][chunk - 1, slot] = found
                     else:
-                        ws[k][0, place * 2 + rank] = found
+                        ws[k][0, slot] = found
             return carry
 
-        lax.fori_loop(0, RING * RING, fill, 0)
+        lax.fori_loop(0, ws[0].shape[1] // 2, fill, 0)
         if chunk:
             for k in range(3):
                 copies.append(
@@ -454,11 +471,10 @@
         copy.wait()
 
 
-def middle(table, neighbours, parts, hp_weight, rate_scale, collective_id):
-    tiles, width = neighbours.shape[0], hp_weight.shape[1]
+def middle(table, beside, parts, hp_weight, rate_scale, slots, collective_id):
+    tiles, width = beside.shape[0] // 8, hp_weight.shape[1]
     column_tiles = tiles * lax.axis_size("lat")
     pixels = tiles * TS * TS
-    beside = jnp.stack([neighbours[:, :, 0] % column_tiles, neighbours[:, :, 2]], axis=-1)
     smem, vmem = pl.BlockSpec(memory_space=pltpu.SMEM), pl.BlockSpec(memory_space=pltpu.VMEM)
     counts = [count for _, count in PARTS]
 
@@ -468,7 +484,7 @@
     return pl.pallas_call(
         middle_body,
         out_shape=[jax.ShapeDtypeStruct((pixels, width), jnp.bfloat16)]
-        + [jax.ShapeDtypeStruct((8, 32, n, width), jnp.bfloat16) for n in counts],
+        + [jax.ShapeDtypeStruct((8, slots, n, width), jnp.bfloat16) for n in counts],
         in_specs=[smem, smem] + [vmem] * 5,
         out_specs=[vmem] * 4,
         scratch_shapes=buffers(RING, RING, HALVES)
@@ -483,7 +499,7 @@
             pltpu.VMEM((HALVES, BLOCK, width), jnp.bfloat16),
         ]
         + buffers(RING * RING, HALVES)
-        + buffers(7, 32)
+        + buffers(7, slots)
         + [
             pltpu.SemaphoreType.DMA((2, 3, RING)),
             pltpu.SemaphoreType.DMA((2, 3, RING)),
@@ -497,7 +513,7 @@
         name="middle",
     )(
         table,
-        beside.reshape(-1),
+        beside,
         *[part.reshape(RING, RING, *part.shape[1:]) for part in parts],
         hp_weight,
         rate_scale.reshape(1, width),
@@ -656,31 +672,29 @@
     targets = rows_of(target_device[:, 0])
     halves = rows_of(target_half)[:24]
     ids = jnp.arange(count, dtype=jnp.int32)
-    rank = jnp.sum(
-        (targets[:, :, None] == targets[:, None, :]) & (ids[None, None, :] < ids[None, :, None]),
-        axis=2,
-        dtype=jnp.int32,
-    )
+    earlier = ids[:, None] < ids[None, :]
     to = {"z": targets // 32, "x": (targets // 8) % 4, "c": (targets // 4) % 2, "y": targets % 4}
-    codes, order = [], []
+    fits, codes, order = [], [], []
     for k in range(3):
         rows = slice(8 * k, 8 * k + 8)
-        fits = (to["c"][rows] == here["c"]) & (to[LINE[k]][rows] == here[LINE[k]])
-        first, second = [
-            (to[axis][rows] - here[axis] + RING) % RING for axis in PLANE[k]
-        ]
-        codes.append(jnp.where(fits, (first * RING + second) * 2 + rank[rows], -1))
+        fits.append((to["c"][rows] == here["c"]) & (to[LINE[k]][rows] == here[LINE[k]]))
+        first, second = [(to[axis][rows] - here[axis] + RING) % RING for axis in PLANE[k]]
+        codes.append((first * RING + second) * HALVES)
         index = jnp.arange(8, dtype=jnp.int32)
         line, core = (index % RING, index // RING) if k == 0 else (index // 2, index % 2)
         order.append((here[LINE[k]] - line + RING) % RING * 2 + (core + here["c"]) % 2)
-    codes = jnp.concatenate(codes, axis=0)
+    fits = jnp.concatenate(fits, axis=0)
+    codes = jnp.concatenate(codes, axis=0) + halves
+    turn = jnp.sum((fits[:, :, None] & earlier[None]).astype(jnp.int32), axis=1)
+    turn = jnp.where(fits, turn, -1)
     slots = jnp.arange(32, dtype=jnp.int32)
+    unused = RING * RING * HALVES
     found = jnp.sum(
-        jnp.where(codes[:, None, :] == slots[None, :, None], (halves - HALVES)[:, None, :], 0),
+        jnp.where(turn[:, None, :] == slots[None, :, None], (codes - unused)[:, None, :], 0),
         axis=2,
     )
     chunk = jnp.arange(8, dtype=jnp.int32)
-    table = HALVES + jnp.sum(
+    table = unused + jnp.sum(
         jnp.where(
             jnp.stack(order)[:, None, :, None] == chunk[None, :, None, None],
             found.reshape(3, 1, 8, 32),
@@ -688,14 +702,26 @@
         ),
         axis=2,
     )
-    own = {axis: value[24] for axis, value in to.items()}
-    away = {axis: (own[axis] - here[axis] + RING) % RING for axis in ("z", "x", "y")}
-    flip = (own["c"] + here["c"]) % 2
-    lines = [source_block]
-    for k in range(3):
-        place = away[PLANE[k][0]] * RING + away[PLANE[k][1]]
-        lines.append((away[LINE[k]] * 2 + flip) * 32 + place * 2 + rank[24])
-    return table.reshape(-1), jnp.stack(lines)
+    flip = (to["c"][24] + here["c"]) % 2
+    chunks = jnp.stack(
+        [(to[axis][24] - here[axis] + RING) % RING * 2 + flip for axis in LINE]
+    )
+    turns = jnp.sum(
+        ((chunks[:, :, None] == chunks[:, None, :]) & earlier[None]).astype(jnp.int32), axis=1
+    )
+    lines = jnp.concatenate([source_block[None], chunks * 32 + turns], axis=0)
+    return table.reshape(-1), lines
+
+
+def all_fit(target_device, count, slots):
+    targets = target_device.reshape(-1, count)
+    core = (targets // 4) % 2
+    keys = jnp.stack([line * 2 + core for line in (targets % 4, targets // 32, (targets // 8) % 4)])
+    words = jnp.arange(3, dtype=jnp.int32)[:, None, None, None]
+    marks = jnp.where(keys // 3 == words, jnp.left_shift(1, 10 * (keys % 3)), 0)
+    sums = jnp.sum(marks, axis=3)
+    counts = jnp.maximum(jnp.maximum(sums & 1023, (sums >> 10) & 1023), sums >> 20)
+    return jnp.max(counts) <= slots
 
 
 def on_device(
@@ -714,13 +740,22 @@
     extra = -channels % 16
     taps = jnp.pad(jnp.swapaxes(conv_weight, 1, 2), ((0, 0), (0, extra), (0, 0)))
     columns = jnp.pad(fields.reshape(channels, lon_cells * lat_cells), ((0, extra), (0, 0)))
-    pre_conv, hidden = grid_conv(columns, taps, False, 2)
-    outgoing = spread(lines, hidden, regrid_blocks)
-    arrived = line_exchange(outgoing, 1, 0)
-    partial = combine(table, arrived)
-    codes, *answers = middle(table, neighbours, partial, hp_weight, rate_scale, 1)
-    pre_grad = pull(lines, regrid_blocks, pre_conv, answers)
-    (grad_columns,) = grid_conv(pre_grad, taps, True, 3)
+    column_tiles = neighbours.shape[0] * lax.axis_size("lat")
+    beside = jnp.stack([neighbours[:, :, 0] % column_tiles, neighbours[:, :, 2]], axis=-1)
+    beside = beside.reshape(-1)
+    few = all_fit(target_device, source_block.shape[0], FEW)
+    pre_conv, hidden = grid_conv(columns, taps, False, 4)
+
+    def step(slots, collective_id):
+        outgoing = spread(lines, hidden, regrid_blocks, slots)
+        partial = combine(table, line_exchange(outgoing, 1, collective_id))
+        codes, *answers = middle(
+            table, beside, partial, hp_weight, rate_scale, slots, collective_id + 1
+        )
+        return codes, pull(lines, regrid_blocks, pre_conv, answers)
+
+    codes, pre_grad = lax.cond(few, lambda: step(FEW, 0), lambda: step(MANY, 2))
+    (grad_columns,) = grid_conv(pre_grad, taps, True, 5)
     grad_fields = grad_columns[:channels].reshape(channels, lon_cells, lat_cells)
     return (codes, grad_fields)
 

time: 198 us -> 177 us (0.89)
  Pallas kernels: 186 us -> 164 us
    pallas_call x1, Pallas kernels: 105 us -> 94.1 us  [middle(): pl.pallas_call(middle_body, out_shape=[jax.ShapeDtypeStruct((pixels, widt...]
    pallas_call x1, Pallas kernels: 39 us -> 28.4 us  [line_exchange(): pl.pallas_call(functools.partial(line_body, sign), out_shape=[jax.ShapeDt...]
where the time goes in v5:
time: 177 us
  Pallas kernels  164 us (93%)
  local copies, waits for them, and re-layouts  6.22 us (4%)
  other arithmetic  5.03 us (3%)
    pallas_call x1, Pallas kernels, middle(): pl.pallas_call(middle_body, out_shape=[jax.ShapeDtypeStruct((pixels, widt...  94.1 us
    pallas_call x2, Pallas kernels, grid_conv(): pl.pallas_call(functools.partial(conv_body, reverse, lon_cells), out_shap...  29 us
    pallas_call x1, Pallas kernels, line_exchange(): pl.pallas_call(functools.partial(line_body, sign), out_shape=[jax.ShapeDt...  28.4 us
    pallas_call x1, Pallas kernels, pull(): pl.pallas_call(pull_body, in_specs=[pl.BlockSpec(memory_space=pltpu.SMEM)...  4.67 us
    pallas_call x1, Pallas kernels, spread(): pl.pallas_call(spread_body, in_specs=[pl.BlockSpec(memory_space=pltpu.SME...  4.39 us

profile of v5, /device:TPU:0, one launch (start us, length us, event | category | flops | bytes accessed | tf_op | source)
XLA Modules:
  0.0 176.6 jit_solution(17442633752715814022)
XLA Ops:
  0.6 0.0 copy-start.2
  0.6 0.0 copy-start.1
  0.7 0.8 fusion.51
  1.6 0.7 add_select_fusion.20
  2.3 0.1 copy.14
  2.4 0.1 reshape.836
  2.5 0.8 constant_dynamic-slice_fusion
  3.3 0.8 constant_dynamic-slice_fusion.1
  4.0 0.7 constant_dynamic-slice_fusion.2
  4.9 0.1 convert_reduce_fusion.1
  5.1 0.7 pad_add_fusion.5
  5.7 0.6 convert_reduce_fusion
  6.4 0.5 select_reduce_fusion.1
  6.8 0.1 select_reduce_fusion.2
  7.0 0.1 add.628
  7.0 1.0 fusion.4
  8.0 0.2 add_select_fusion.1
  8.3 0.3 select_reduce_fusion
  8.5 0.6 maximum_reduce_fusion
  9.8 0.0 copy-done.2
  9.9 0.0 copy-done.1
  9.9 0.2 pad.36
  10.0 0.0 copy-start
  10.1 0.0 copy-start.3
  10.1 0.0 copy-start.4
  10.1 0.2 copy.15
  10.3 0.1 pad.8.x
  10.4 15.5 %conv.1 = (f32[128,2048]{1,0:T(8,128)S(1)}, bf16[128,2048]{1,0:T(8,128)(2,1)S(1)}) custom-call(bf16[224,2048]{1,0:T(8,128)(2,1)S(1)} %pad.8.x, bf16[9,224,128]{2,1,0:T(8,128)(2,1)S(1)} %pad.9.taps), custom_call_target="tpu_custom_call" | custom-call | tf_op jit(solution)/shard_map/conv/pallas_call | solution.py:637
  25.9 0.0 copy-done
  25.9 0.0 copy-done.3
  25.9 0.0 copy-done.4
  25.9 134.7 %conditional.1 = (bf16[1024,128]{1,0:T(8,128)(2,1)S(1)}, bf16[128,2048]{1,0:T(8,128)(2,1)S(1)}) conditional(s32[]{:T(128)} %convert_element_type.13, (s32[4,128]{1,0:T(4,128)S(1)}, bf16[128,2048]{1,0:T(8,128)(2,1)S(1)}, bf16[128,128,128]{2,1,0:T(8,128)(2,1)S(1)}, s32[768]{0:T(1024)S(1)}, f32[128]{0:T(128)S(1)}, /*index=5*/s32[32]{0:T(128)S(1)}, ...), branch_computations={%region_6.7_spmd, %region_7.8_spmd} | conditional | bytes 16 | solution.py:757
  26.1 4.4 %spread.3 = (bf16[8,22,48,128]{3,2,1,0:T(8,128)(2,1)S(1)}, bf16[8,22,48,128]{3,2,1,0:T(8,128)(2,1)S(1)}, bf16[8,22,32,128]{3,2,1,0:T(8,128)(2,1)S(1)}) custom-call(s32[4,128]{1,0:T(4,128)S(1)} %get-tuple-element.55.table, bf16[128,2048]{1,0:T(8,128)(2,1)S(1)} %get-tuple-element.56.hidden, bf16[128,128,128]{2,1,0:T(8,128)(2,1)S(1)} %get-tuple-element.57.blocks), custom_call_target="tpu_custom_call" | custom-call | tf_op jit(solution)/shard_map/cond/branch_1_fun/spread/pallas_call | solution.py:137
  30.5 28.4 %line_exchange_0.1 = (bf16[8,22,48,128]{3,2,1,0:T(8,128)(2,1)S(1)}, bf16[8,22,48,128]{3,2,1,0:T(8,128)(2,1)S(1)}, bf16[8,22,32,128]{3,2,1,0:T(8,128)(2,1)S(1)}) custom-call(bf16[8,22,48,128]{3,2,1,0:T(8,128)(2,1)S(1)} %get-tuple-element.58.s0, bf16[8,22,48,128]{3,2,1,0:T(8,128)(2,1)S(1)} %get-tuple-element.59.s1, ...), custom_call_target="tpu_custom_call" | custom-call | tf_op jit(solution)/shard_map/cond/branch_1_fun/line_exchange_0/pallas_call | solution.py:100
  59.0 2.9 %combine.3 = (bf16[16,8,48,128]{3,2,1,0:T(8,128)(2,1)S(1)}, bf16[16,8,48,128]{3,2,1,0:T(8,128)(2,1)S(1)}, bf16[16,8,32,128]{3,2,1,0:T(8,128)(2,1)S(1)}) custom-call(s32[768]{0:T(1024)S(1)} %get-tuple-element.53.table, bf16[8,22,48,128]{3,2,1,0:T(8,128)(2,1)S(1)} %get-tuple-element.61.r0, bf16[8,22,48,128]{3,2,1,0:T(8,128)(2,1)S(1)} %get-tuple-element.62.r1, ...), custom_call_target="tpu_custom_call" | custom-call | tf_op jit(solution)/shard_map/cond/branch_1_fun/combine/pallas_call | solution.py:178
  61.9 94.1 %middle.3 = (bf16[1024,128]{1,0:T(8,128)(2,1)S(1)}, bf16[8,22,48,128]{3,2,1,0:T(8,128)(2,1)S(1)}, bf16[8,22,48,128]{3,2,1,0:T(8,128)(2,1)S(1)}, bf16[8,22,32,128]{3,2,1,0:T(8,128)(2,1)S(1)}) custom-call(s32[768]{0:T(1024)S(1)} %get-tuple-element.53.table, s32[32]{0:T(128)S(1)} %get-tuple-element.54.beside, bf16[4,4,8,48,128]{4,3,2,1,0:T(8,128)(2,1)S(1)} %bitcast.32, ...), custom_call_target="tpu_custom_call" | custom-call | tf_op jit(solution)/shard_map/cond/branch_1_fun/middle/pallas_call | solution.py:484
  156.0 4.7 %pull.3 = bf16[128,2048]{1,0:T(8,128)(2,1)S(1)} custom-call(s32[4,128]{1,0:T(4,128)S(1)} %get-tuple-element.55.table, bf16[128,128,128]{2,1,0:T(8,128)(2,1)S(1)} %get-tuple-element.57.blocks, f32[128,2048]{1,0:T(8,128)S(1)} %get-tuple-element.70.pre_conv, bf16[8,22,48,128]{3,2,1,0:T(8,128)(2,1)S(1)} %get-tuple-element.71.w0, ...), custom_call_target="tpu_custom_call" | custom-call | tf_op jit(solution)/shard_map/cond/branch_1_fun/pull/pallas_call | solution.py:218
  160.6 13.6 %conv_back.1 = f32[224,2048]{1,0:T(8,128)S(1)} custom-call(bf16[128,2048]{1,0:T(8,128)(2,1)S(1)} %get-tuple-element.83.x, bf16[9,224,128]{2,1,0:T(8,128)(2,1)S(1)} %pad.9.taps), custom_call_target="tpu_custom_call" | custom-call | tf_op jit(solution)/shard_map/conv_back/pallas_call | solution.py:637
  174.2 0.3 copy.16
  174.6 1.3 slice.92
  175.9 0.7 copy.22
  (18 shorter events, 0.3 us)
Async XLA Ops:
  0.6 9.2 %copy-start.2 = (bf16[9,128,222]{1,2,0:T(8,128)(2,1)S(1)}, bf16[9,128,222]{1,2,0:T(8,128)(2,1)}, u32[]{:S(2)}) copy-start(bf16[9,128,222]{1,2,0:T(8,128)(2,1)} %param.12) | copy-start | bytes 1534468
  0.6 9.2 %copy-start.1 = (bf16[222,16,128]{2,1,0:T(8,128)(2,1)S(1)}, bf16[222,16,128]{2,1,0:T(8,128)(2,1)}, u32[]{:S(2)}) copy-start(bf16[222,16,128]{2,1,0:T(8,128)(2,1)} %param.11) | copy-start | bytes 2727940
  10.0 15.9 %copy-start = (bf16[128,128,128]{2,1,0:T(8,128)(2,1)S(1)}, bf16[128,128,128]{2,1,0:T(8,128)(2,1)}, u32[]{:S(2)}) copy-start(bf16[128,128,128]{2,1,0:T(8,128)(2,1)} %param.13) | copy-start | bytes 12582916
  10.1 15.9 %copy-start.3 = (bf16[2,128,128]{2,1,0:T(8,128)(2,1)S(1)}, bf16[2,128,128]{2,1,0:T(8,128)(2,1)}, u32[]{:S(2)}) copy-start(bf16[2,128,128]{2,1,0:T(8,128)(2,1)} %param.18) | copy-start | bytes 196612
  10.1 15.9 %copy-start.4 = (f32[128]{0:T(128)S(1)}, f32[128]{0:T(128)}, u32[]{:S(2)}) copy-start(f32[128]{0:T(128)} %param.19) | copy-start | bytes 1540

commit v6 on v5

--- a/solution.py
+++ b/solution.py
@@ -158,7 +158,7 @@
     def add(slot, carry):
         for chunk in range(8):
             for k in range(3):
-                spot = table[k * 256 + chunk * 32 + slot]
+                spot = table[k * 8 * BLOCK + chunk * BLOCK + slot]
                 sums[k][spot] += ins[k][chunk, slot].astype(jnp.float32)
         return carry
 
@@ -446,7 +446,7 @@
             for k in range(3):
                 for slot in (2 * pair, 2 * pair + 1):
                     spot = jnp.minimum(
-                        table[k * 256 + chunk * 32 + slot], RING * RING * HALVES - 1
+                        table[k * 8 * BLOCK + chunk * BLOCK + slot], RING * RING * HALVES - 1
                     )
                     found = us[k][spot >> 3, spot & 7]
                     if chunk:
@@ -651,77 +651,90 @@
     )(cells, taps)
 
 
+def routing_body(targets, halves, sources, table, lines, most, rows_t, rows_h):
+    here = torus_position()
+    for k in range(3):
+        for chunk in range(8):
+            lon, lat = device_at(moved(here, **{LINE[k]: -(chunk // 2), "c": chunk % 2}))
+            row = pl.ds(lon * RING + lat, 1)
+            rows_t[8 * k + chunk : 8 * k + chunk + 1, :] = targets[row, :]
+            rows_h[8 * k + chunk : 8 * k + chunk + 1, :] = halves[row, :]
+    shape = rows_t.shape
+    part, lane = iota(shape, 0) >> 3, iota(shape, 1)
+
+    def coordinates(t):
+        return {"z": t >> 5, "x": (t >> 3) & 3, "c": (t >> 2) & 1, "y": t & 3}
+
+    def by_part(values, axes):
+        return jnp.where(
+            part == 0, values[axes[0]], jnp.where(part == 1, values[axes[1]], values[axes[2]])
+        )
+
+    def away(values, axes):
+        return (by_part(values, axes) - by_part(here, axes) + RING) & 3
+
+    def ones(mask):
+        return mask.astype(jnp.float32).astype(jnp.bfloat16)
+
+    size = shape[1]
+    earlier = ones(iota((size, size), 0) < iota((size, size), 1))
+    to = coordinates(rows_t[...])
+    firsts, seconds = [axes[0] for axes in PLANE], [axes[1] for axes in PLANE]
+    code = (away(to, firsts) * RING + away(to, seconds)) * HALVES + rows_h[...]
+    fits = (to["c"] == here["c"]) & (away(to, LINE) == 0)
+    turn = jnp.where(fits, dot(ones(fits), earlier), -1.0)
+    unused = RING * RING * HALVES
+    value = (code - unused).astype(jnp.float32)
+    found = jnp.full(shape, float(unused), jnp.float32)
+    for slot in range(MANY):
+        picked = jnp.sum(jnp.where(turn == slot, value, 0.0), axis=1, keepdims=True)
+        found += jnp.where(lane == slot, picked, 0.0)
+    table[...] = found.astype(jnp.int32)
+
+    own = coordinates(jnp.broadcast_to(rows_t[0:1, :], shape))
+    chunk = away(own, LINE) * 2 + jnp.where(own["c"] == here["c"], 0, 1)
+    group = iota(shape, 0) & 7
+    mine = chunk == group
+    spot = jnp.where(mine, group.astype(jnp.float32) * MANY + dot(ones(mine), earlier), 0.0)
+    lines[0:1, :] = sources[...]
+    for k in range(3):
+        lines[k + 1 : k + 2, :] = jnp.sum(
+            spot[8 * k : 8 * k + 8, :], axis=0, keepdims=True
+        ).astype(jnp.int32)
+
+    everyone = coordinates(targets[...])
+    largest = jnp.zeros((targets.shape[0], 1), jnp.float32)
+    for axis in LINE:
+        keys = everyone[axis] * 2 + everyone["c"]
+        for key in range(8):
+            held = jnp.sum((keys == key).astype(jnp.float32), axis=1, keepdims=True)
+            largest = jnp.maximum(largest, held)
+    most[...] = jnp.broadcast_to(jnp.max(largest, axis=0, keepdims=True), most.shape).astype(
+        jnp.int32
+    )
+
+
 def routing(source_block, target_device, target_half):
-    here = torus_position()
     count = source_block.shape[0]
-
-    def rows_of(values):
-        grid = values.reshape(4, 4, 2, 4, count)
-        picks = []
-        for k in range(3):
-            start = [here["z"], here["x"], 0, here["y"], 0]
-            size = [1, 1, 2, 1, count]
-            at = {"z": 0, "x": 1, "y": 3}[LINE[k]]
-            start[at], size[at] = 0, 4
-            picks.append(lax.dynamic_slice(grid, start, size).reshape(8, count))
-        own = lax.dynamic_slice(
-            grid, [here["z"], here["x"], here["c"], here["y"], 0], [1, 1, 1, 1, count]
-        )
-        return jnp.concatenate(picks + [own.reshape(1, count)], axis=0)
-
-    targets = rows_of(target_device[:, 0])
-    halves = rows_of(target_half)[:24]
-    ids = jnp.arange(count, dtype=jnp.int32)
-    earlier = ids[:, None] < ids[None, :]
-    to = {"z": targets // 32, "x": (targets // 8) % 4, "c": (targets // 4) % 2, "y": targets % 4}
-    fits, codes, order = [], [], []
-    for k in range(3):
-        rows = slice(8 * k, 8 * k + 8)
-        fits.append((to["c"][rows] == here["c"]) & (to[LINE[k]][rows] == here[LINE[k]]))
-        first, second = [(to[axis][rows] - here[axis] + RING) % RING for axis in PLANE[k]]
-        codes.append((first * RING + second) * HALVES)
-        index = jnp.arange(8, dtype=jnp.int32)
-        line, core = (index % RING, index // RING) if k == 0 else (index // 2, index % 2)
-        order.append((here[LINE[k]] - line + RING) % RING * 2 + (core + here["c"]) % 2)
-    fits = jnp.concatenate(fits, axis=0)
-    codes = jnp.concatenate(codes, axis=0) + halves
-    turn = jnp.sum((fits[:, :, None] & earlier[None]).astype(jnp.int32), axis=1)
-    turn = jnp.where(fits, turn, -1)
-    slots = jnp.arange(32, dtype=jnp.int32)
-    unused = RING * RING * HALVES
-    found = jnp.sum(
-        jnp.where(turn[:, None, :] == slots[None, :, None], (codes - unused)[:, None, :], 0),
-        axis=2,
-    )
-    chunk = jnp.arange(8, dtype=jnp.int32)
-    table = unused + jnp.sum(
-        jnp.where(
-            jnp.stack(order)[:, None, :, None] == chunk[None, :, None, None],
-            found.reshape(3, 1, 8, 32),
-            0,
-        ),
-        axis=2,
-    )
-    flip = (to["c"][24] + here["c"]) % 2
-    chunks = jnp.stack(
-        [(to[axis][24] - here[axis] + RING) % RING * 2 + flip for axis in LINE]
-    )
-    turns = jnp.sum(
-        ((chunks[:, :, None] == chunks[:, None, :]) & earlier[None]).astype(jnp.int32), axis=1
-    )
-    lines = jnp.concatenate([source_block[None], chunks * 32 + turns], axis=0)
-    return table.reshape(-1), lines
-
-
-def all_fit(target_device, count, slots):
-    targets = target_device.reshape(-1, count)
-    core = (targets // 4) % 2
-    keys = jnp.stack([line * 2 + core for line in (targets % 4, targets // 32, (targets // 8) % 4)])
-    words = jnp.arange(3, dtype=jnp.int32)[:, None, None, None]
-    marks = jnp.where(keys // 3 == words, jnp.left_shift(1, 10 * (keys % 3)), 0)
-    sums = jnp.sum(marks, axis=3)
-    counts = jnp.maximum(jnp.maximum(sums & 1023, (sums >> 10) & 1023), sums >> 20)
-    return jnp.max(counts) <= slots
+    vmem = pl.BlockSpec(memory_space=pltpu.VMEM)
+    table, lines, most = pl.pallas_call(
+        routing_body,
+        in_specs=[vmem] * 3,
+        out_specs=[vmem] * 3,
+        out_shape=[
+            jax.ShapeDtypeStruct((24, count), jnp.int32),
+            jax.ShapeDtypeStruct((4, count), jnp.int32),
+            jax.ShapeDtypeStruct((8, count), jnp.int32),
+        ],
+        scratch_shapes=[pltpu.VMEM((24, count), jnp.int32)] * 2,
+        compiler_params=pltpu.CompilerParams(vmem_limit_bytes=8 << 20),
+        name="routing",
+    )(
+        target_device.reshape(-1, count),
+        target_half.reshape(-1, count),
+        source_block.reshape(1, count),
+    )
+    return table.reshape(-1), lines, most[0, 0]
 
 
 def on_device(
@@ -736,14 +749,13 @@
     rate_scale,
 ):
     channels, lon_cells, lat_cells = fields.shape
-    table, lines = routing(source_block, target_device, target_half)
+    table, lines, most = routing(source_block, target_device, target_half)
     extra = -channels % 16
     taps = jnp.pad(jnp.swapaxes(conv_weight, 1, 2), ((0, 0), (0, extra), (0, 0)))
     columns = jnp.pad(fields.reshape(channels, lon_cells * lat_cells), ((0, extra), (0, 0)))
     column_tiles = neighbours.shape[0] * lax.axis_size("lat")
     beside = jnp.stack([neighbours[:, :, 0] % column_tiles, neighbours[:, :, 2]], axis=-1)
     beside = beside.reshape(-1)
-    few = all_fit(target_device, source_block.shape[0], FEW)
     pre_conv, hidden = grid_conv(columns, taps, False, 4)
 
     def step(slots, collective_id):
@@ -754,7 +766,7 @@
         )
         return codes, pull(lines, regrid_blocks, pre_conv, answers)
 
-    codes, pre_grad = lax.cond(few, lambda: step(FEW, 0), lambda: step(MANY, 2))
+    codes, pre_grad = lax.cond(most <= FEW, lambda: step(FEW, 0), lambda: step(MANY, 2))
     (grad_columns,) = grid_conv(pre_grad, taps, True, 5)
     grad_fields = grad_columns[:channels].reshape(channels, lon_cells, lat_cells)
     return (codes, grad_fields)

time: 177 us -> 175 us (0.989)
  other arithmetic: 5.03 us -> 0.71 us
  local copies, waits for them, and re-layouts: 6.22 us -> 8.19 us
    unnamed x14 -> x16, local copies, waits for them, and re-layouts: 1.46 us -> 4.96 us
    dynamic_slice x3 -> x0, local copies, waits for them, and re-layouts: 2.22 us -> none  [rows_of(): picks.append(lax.dynamic_slice(grid, start, size).reshape(8, count))]
where the time goes in v6:
time: 175 us
  Pallas kernels  165 us (94%)
  local copies, waits for them, and re-layouts  8.19 us (5%)
    pallas_call x1, Pallas kernels, middle(): pl.pallas_call(middle_body, out_shape=[jax.ShapeDtypeStruct((pixels, widt...  94.2 us
    pallas_call x2, Pallas kernels, grid_conv(): pl.pallas_call(functools.partial(conv_body, reverse, lon_cells), out_shap...  29 us
    pallas_call x1, Pallas kernels, line_exchange(): pl.pallas_call(functools.partial(line_body, sign), out_shape=[jax.ShapeDt...  28.4 us
    unnamed x16, local copies, waits for them, and re-layouts  4.96 us
    pallas_call x1, Pallas kernels, pull(): pl.pallas_call(pull_body, in_specs=[pl.BlockSpec(memory_space=pltpu.SMEM)...  4.68 us
    pallas_call x1, Pallas kernels, spread(): pl.pallas_call(spread_body, in_specs=[pl.BlockSpec(memory_space=pltpu.SME...  4.39 us

profile of v6, /device:TPU:0, one launch (start us, length us, event | category | flops | bytes accessed | tf_op | source)
XLA Modules:
  0.0 175.1 jit_solution(18089713668675062869)
XLA Ops:
  0.6 0.7 add_select_fusion
  1.3 0.1 copy.12
  1.5 0.1 reshape.58
  1.6 0.0 copy-start
  1.6 0.8 copy-done
  2.4 0.0 copy-start.1
  2.4 0.8 copy-done.1
  3.2 0.0 copy-start.2
  3.2 0.7 copy-done.2
  3.9 0.7 routing.1
  4.6 0.5 slice.12
  5.8 1.1 pad.9.taps
  6.9 1.3 pad.12
  8.2 0.0 copy-start.3
  8.3 0.0 copy-start.4
  8.3 0.0 copy-start.5
  8.3 0.2 copy.13
  8.5 0.1 pad.8.x
  8.6 15.5 %conv.1 = (f32[128,2048]{1,0:T(8,128)S(1)}, bf16[128,2048]{1,0:T(8,128)(2,1)S(1)}) custom-call(bf16[224,2048]{1,0:T(8,128)(2,1)S(1)} %pad.8.x, bf16[9,224,128]{2,1,0:T(8,128)(2,1)S(1)} %pad.9.taps), custom_call_target="tpu_custom_call" | custom-call | tf_op jit(solution)/shard_map/conv/pallas_call | solution.py:637
  24.1 0.0 copy-done.3
  24.1 0.0 copy-done.4
  24.1 0.0 copy-done.5
  24.1 135.0 %conditional.1 = (bf16[1024,128]{1,0:T(8,128)(2,1)S(1)}, bf16[128,2048]{1,0:T(8,128)(2,1)S(1)}) conditional(s32[]{:T(128)} %bitcast.11, (s32[4,128]{1,0:T(4,128)S(1)}, bf16[128,2048]{1,0:T(8,128)(2,1)S(1)}, bf16[128,128,128]{2,1,0:T(8,128)(2,1)S(1)}, s32[3072]{0:T(1024)S(1)}, f32[128]{0:T(128)S(1)}, /*index=5*/s32[32]{0:T(128)S(1)}, ...), branch_computations={%region_0.1_spmd, %region_1.2_spmd} | conditional | bytes 16 | solution.py:769
  24.3 4.4 %spread.3 = (bf16[8,22,48,128]{3,2,1,0:T(8,128)(2,1)S(1)}, bf16[8,22,48,128]{3,2,1,0:T(8,128)(2,1)S(1)}, bf16[8,22,32,128]{3,2,1,0:T(8,128)(2,1)S(1)}) custom-call(s32[4,128]{1,0:T(4,128)S(1)} %get-tuple-element.55.table, bf16[128,2048]{1,0:T(8,128)(2,1)S(1)} %get-tuple-element.56.hidden, bf16[128,128,128]{2,1,0:T(8,128)(2,1)S(1)} %get-tuple-element.57.blocks), custom_call_target="tpu_custom_call" | custom-call | tf_op jit(solution)/shard_map/cond/branch_1_fun/spread/pallas_call | solution.py:137
  28.7 28.4 %line_exchange_0.1 = (bf16[8,22,48,128]{3,2,1,0:T(8,128)(2,1)S(1)}, bf16[8,22,48,128]{3,2,1,0:T(8,128)(2,1)S(1)}, bf16[8,22,32,128]{3,2,1,0:T(8,128)(2,1)S(1)}) custom-call(bf16[8,22,48,128]{3,2,1,0:T(8,128)(2,1)S(1)} %get-tuple-element.58.s0, bf16[8,22,48,128]{3,2,1,0:T(8,128)(2,1)S(1)} %get-tuple-element.59.s1, ...), custom_call_target="tpu_custom_call" | custom-call | tf_op jit(solution)/shard_map/cond/branch_1_fun/line_exchange_0/pallas_call | solution.py:100
  57.2 3.1 %combine.3 = (bf16[16,8,48,128]{3,2,1,0:T(8,128)(2,1)S(1)}, bf16[16,8,48,128]{3,2,1,0:T(8,128)(2,1)S(1)}, bf16[16,8,32,128]{3,2,1,0:T(8,128)(2,1)S(1)}) custom-call(s32[3072]{0:T(1024)S(1)} %get-tuple-element.53.table, bf16[8,22,48,128]{3,2,1,0:T(8,128)(2,1)S(1)} %get-tuple-element.61.r0, bf16[8,22,48,128]{3,2,1,0:T(8,128)(2,1)S(1)} %get-tuple-element.62.r1, ...), custom_call_target="tpu_custom_call" | custom-call | tf_op jit(solution)/shard_map/cond/branch_1_fun/combine/pallas_call | solution.py:178
  60.2 94.2 %middle.3 = (bf16[1024,128]{1,0:T(8,128)(2,1)S(1)}, bf16[8,22,48,128]{3,2,1,0:T(8,128)(2,1)S(1)}, bf16[8,22,48,128]{3,2,1,0:T(8,128)(2,1)S(1)}, bf16[8,22,32,128]{3,2,1,0:T(8,128)(2,1)S(1)}) custom-call(s32[3072]{0:T(1024)S(1)} %get-tuple-element.53.table, s32[32]{0:T(128)S(1)} %get-tuple-element.54.beside, bf16[4,4,8,48,128]{4,3,2,1,0:T(8,128)(2,1)S(1)} %bitcast.24, ...), custom_call_target="tpu_custom_call" | custom-call | tf_op jit(solution)/shard_map/cond/branch_1_fun/middle/pallas_call | solution.py:484
  154.5 4.7 %pull.3 = bf16[128,2048]{1,0:T(8,128)(2,1)S(1)} custom-call(s32[4,128]{1,0:T(4,128)S(1)} %get-tuple-element.55.table, bf16[128,128,128]{2,1,0:T(8,128)(2,1)S(1)} %get-tuple-element.57.blocks, f32[128,2048]{1,0:T(8,128)S(1)} %get-tuple-element.70.pre_conv, bf16[8,22,48,128]{3,2,1,0:T(8,128)(2,1)S(1)} %get-tuple-element.71.w0, ...), custom_call_target="tpu_custom_call" | custom-call | tf_op jit(solution)/shard_map/cond/branch_1_fun/pull/pallas_call | solution.py:218
  159.2 13.5 %conv_back.1 = f32[224,2048]{1,0:T(8,128)S(1)} custom-call(bf16[128,2048]{1,0:T(8,128)(2,1)S(1)} %get-tuple-element.89.x, bf16[9,224,128]{2,1,0:T(8,128)(2,1)S(1)} %pad.9.taps), custom_call_target="tpu_custom_call" | custom-call | tf_op jit(solution)/shard_map/conv_back/pallas_call | solution.py:637
  172.7 0.3 copy.14
  173.0 1.3 slice.16
  174.4 0.7 copy.20
  (1 shorter events, 0.0 us)
Async XLA Ops:
  1.6 0.8 copy-start
  2.4 0.8 copy-start.1
  3.2 0.7 copy-start.2
  8.2 15.9 %copy-start.3 = (bf16[128,128,128]{2,1,0:T(8,128)(2,1)S(1)}, bf16[128,128,128]{2,1,0:T(8,128)(2,1)}, u32[]{:S(2)}) copy-start(bf16[128,128,128]{2,1,0:T(8,128)(2,1)} %param.13) | copy-start | bytes 12582916
  8.3 15.9 %copy-start.4 = (bf16[2,128,128]{2,1,0:T(8,128)(2,1)S(1)}, bf16[2,128,128]{2,1,0:T(8,128)(2,1)}, u32[]{:S(2)}) copy-start(bf16[2,128,128]{2,1,0:T(8,128)(2,1)} %param.18) | copy-start | bytes 196612
  8.3 15.9 %copy-start.5 = (f32[128]{0:T(128)S(1)}, f32[128]{0:T(128)}, u32[]{:S(2)}) copy-start(f32[128]{0:T(128)} %param.19) | copy-start | bytes 1540
